TPU v7x, 32 devices: a whole 2x2x4 slice. The times are simulated.
32 devices in a mesh: samp: 8 (over z, y), feat: 4 (over x, core).
Axes of the slice: x: 2, y: 2, z: 4, core: 2. Of those that a mesh axis runs over, the one named last changes fastest.
Arguments:
- layer_input: bfloat16 [512, 64, 512], P('samp', 'feat'), may hold values from -6 to 6
- segment_ids: int32 [512], replicated, may hold values from 0 to 3, as said below
- context_flags: int32 [512], replicated, may hold values from 0 to 1, as said below
- first_gain: float32 [512], replicated, may hold values from 0.1 to 1.9
- first_shift: float32 [512], replicated, may hold values from -3 to 3
- sample_weight: bfloat16 [512, 1536], replicated, may hold values from -0.25 to 0.25
- sample_bias: float32 [1024], replicated, may hold values from -3 to 3
- sample_mixer: bfloat16 [512, 512], replicated, may hold values from -1 to 1
- sample_offset: float32 [512], replicated, may hold values from -3 to 3
- second_gain: float32 [512], replicated, may hold values from 0.1 to 1.9
- second_shift: float32 [512], replicated, may hold values from -3 to 3
- feature_weight: bfloat16 [512, 1536], replicated, may hold values from -0.25 to 0.25
- feature_bias: float32 [1024], replicated, may hold values from -3 to 3
- feature_mixer: bfloat16 [512, 512], replicated, may hold values from -1.5 to 1.5
- feature_offset: float32 [512], replicated, may hold values from -3 to 3
- third_gain: float32 [512], replicated, may hold values from 0.1 to 1.9
- third_shift: float32 [512], replicated, may hold values from -3 to 3
- expand_weight: bfloat16 [512, 2048], replicated, may hold values from -0.25 to 0.25
- expand_bias: float32 [2048], replicated, may hold values from -3 to 3
- reduce_weight: bfloat16 [2048, 512], replicated, may hold values from -0.125 to 0.125
- reduce_bias: float32 [512], replicated, may hold values from -3 to 3
- cotangent: bfloat16 [512, 64, 512], P('samp', 'feat'), may hold values from -6 to 6
Outputs:
- layer_output: bfloat16 [512, 64, 512], P('samp', 'feat')
- input_grad: bfloat16 [512, 64, 512], P('samp', 'feat')
- first_gain_grad: float32 [512], P('samp')
- first_shift_grad: float32 [512], P('samp')
- sample_weight_grad: float32 [512, 1536], P('samp')
- sample_bias_grad: float32 [1024], P('samp')
- sample_mixer_grad: float32 [512, 512], P('samp')
- sample_offset_grad: float32 [512], P('samp')
- second_gain_grad: float32 [512], P('samp')
- second_shift_grad: float32 [512], P('samp')
- feature_weight_grad: float32 [512, 1536], P('samp')
- feature_bias_grad: float32 [1024], P('samp')
- feature_mixer_grad: float32 [512, 512], P('samp')
- feature_offset_grad: float32 [512], P('samp')
- third_gain_grad: float32 [512], P('samp')
- third_shift_grad: float32 [512], P('samp')
- expand_weight_grad: float32 [512, 2048], P('samp')
- expand_bias_grad: float32 [2048], P('samp')
- reduce_weight_grad: float32 [2048, 512], P('samp')
- reduce_bias_grad: float32 [512], P('samp')
Inputs may be any that keep to these rules, and one draw needn't show every extreme that they name: `context_flags`: the samples of one index of samp (an aligned block of 64 samples) are all context samples or all query samples; exactly 1 block are context blocks, which ones is drawn. `segment_ids`: every task holds exactly 16 context samples.
All inputs are finite; a program needn't handle non-finite values.
Results may differ from a plain program's by a relative error of at most 0.017.
Values may be sent and summed in bfloat16 or wider, within the bound.
No kernel may reach another device: no remote copies, remote signals or barrier semaphores. Data moves between devices by JAX's collectives and lax.ppermute only.
A program may use at most 256 MiB of HBM per device.

v0:
```python
from functools import partial

import jax
import jax.numpy as jnp
from jax import lax
from jax.experimental import pallas as pl
from jax.experimental.pallas import tpu as pltpu
from jax.sharding import PartitionSpec as P

HEADS = 8
HEAD_DIM = 64
EPS = 1e-05
MASKED = -1000000000.0
SCALE = HEAD_DIM ** (-0.5)
QUAD = 4 * HEAD_DIM
BF = jnp.bfloat16
F32 = jnp.float32


def mm(a, b, ca=1, cb=0):
    return lax.dot_general(a, b, (((ca,), (cb,)), ((), ())), preferred_element_type=F32)


def norm_parts(values):
    center = jnp.mean(values, axis=-1, keepdims=True)
    spread = values - center
    variance = jnp.mean(spread * spread, axis=-1, keepdims=True)
    inverse = lax.rsqrt(variance + EPS)
    return spread * inverse, inverse


def norm_back(grad, unit, inverse, gain):
    scaled = grad * gain
    first = jnp.mean(scaled, axis=-1, keepdims=True)
    second = jnp.mean(scaled * unit, axis=-1, keepdims=True)
    return (scaled - first - unit * second) * inverse


def lane_ids(rows):
    return lax.broadcasted_iota(jnp.int32, (rows, 128), 1)


def group_reduce(values, op, fill):
    rows = values.shape[0]
    low = lane_ids(rows) < HEAD_DIM
    outs = []
    for t in range(values.shape[1] // 128):
        tile = values[:, t * 128 : (t + 1) * 128]
        left = op(jnp.where(low, tile, fill), axis=1, keepdims=True)
        right = op(jnp.where(low, fill, tile), axis=1, keepdims=True)
        outs.append(jnp.where(low, left, right))
    return jnp.concatenate(outs, axis=1)


def head_masks(dtype):
    lanes = lax.broadcasted_iota(jnp.int32, (1, QUAD), 1) // HEAD_DIM
    return [jnp.where(lanes == h, 1.0, 0.0).astype(dtype) for h in range(4)]


def stack_heads(part, masks):
    return jnp.concatenate([part * m for m in masks], axis=0)


def pick_heads(stacked, masks):
    rows = stacked.shape[0] // 4
    total = stacked[:rows] * masks[0]
    for h in range(1, 4):
        total = total + stacked[h * rows : (h + 1) * rows] * masks[h]
    return total


def attend(q, k, v, masks, allow):
    outs, probs = [], []
    for quad in range(2):
        cols = slice(quad * QUAD, (quad + 1) * QUAD)
        scores = mm(q[:, cols], stack_heads(k[:, cols], masks), 1, 1)
        if allow is not None:
            scores = jnp.where(allow, scores, MASKED)
        raised = jnp.exp(scores - group_reduce(scores, jnp.max, -jnp.inf))
        prob = raised / group_reduce(raised, jnp.sum, 0.0)
        outs.append(mm(prob.astype(BF), stack_heads(v[:, cols], masks)))
        probs.append(prob)
    return jnp.concatenate(outs, axis=1), jnp.concatenate(probs, axis=1)


def attend_back(q, k, v, prob, grad, masks, masks32):
    dqs, dks, dvs = [], [], []
    for quad in range(2):
        cols = slice(quad * QUAD, (quad + 1) * QUAD)
        p, g = prob[:, cols], grad[:, cols]
        back = mm(g, stack_heads(v[:, cols], masks), 1, 1)
        inner = group_reduce(p * back, jnp.sum, 0.0)
        gs = (p * (back - inner)).astype(BF)
        dqs.append(mm(gs, stack_heads(k[:, cols], masks)) * SCALE)
        dks.append(pick_heads(mm(gs, q[:, cols], 0, 0), masks32))
        dvs.append(pick_heads(mm(p.astype(BF), g, 0, 0), masks32))
    join = lambda parts: jnp.concatenate(parts, axis=1).astype(BF)
    return join(dqs), join(dks), join(dvs)


def swap_matrix(rows=16):
    n = rows * 16
    r = lax.broadcasted_iota(jnp.int32, (n, n), 0)
    c = lax.broadcasted_iota(jnp.int32, (n, n), 1)
    return jnp.where((r // rows == c % 16) & (r % rows == c // 16), 1.0, 0.0).astype(BF)


def swap(matrix, values, back=False):
    return mm(matrix, values, 0 if back else 1, 0).astype(BF)


def gelu_parts(u):
    cdf = 0.5 * (1.0 + lax.erf(u * (2.0**-0.5)))
    density = jnp.exp(u * u * -0.5) * 0.3989422804014327
    return cdf, density


def col_sum(values):
    return jnp.sum(values.astype(F32), axis=0, keepdims=True)


def turn_in(x_ref, out_ref):
    matrix = swap_matrix()
    for d in range(4):
        rows = x_ref[d * 256 : (d + 1) * 256]
        out_ref[:, d] = swap(matrix, rows).reshape(16, 16, 512)


def turn_out(got_ref, out_ref):
    matrix = swap_matrix()
    for d in range(4):
        out_ref[d * 256 : (d + 1) * 256] = swap(matrix, got_ref[:, d].reshape(256, 512))


def each_feature(body):
    lax.fori_loop(0, 4, lambda e, carry: (body(e), carry)[1], 0)


def project_queries(x_ref, gain_ref, shift_ref, w_ref, b_ref, act_ref, q_ref):
    def body(e):
        unit, _ = norm_parts(x_ref[:, e].reshape(256, 512).astype(F32))
        act = (unit * gain_ref[...] + shift_ref[...]).astype(BF)
        act_ref[e] = act
        q = (mm(act, w_ref[:, :512]) + b_ref[:, :512]).astype(BF)
        q_ref[e] = q * jnp.asarray(SCALE, BF)

    each_feature(body)


def forward_one(
    me_ref, q_ref, own_ref, got_ref, tasks_ref, context_ref, gain_ref, shift_ref, w_ref, b_ref,
    oa_ref, ob_ref, c_ref, cact_ref, k_ref, v_ref, p_ref,
):
    here = me_ref[1] == me_ref[2]
    masks = head_masks(BF)
    allow = tasks_ref[...] == context_ref[...]

    @pl.when(here)
    def _():
        c_ref[...] = own_ref[...]

    @pl.when(jnp.logical_not(here))
    def _():
        c_ref[...] = got_ref[...]

    unit, _ = norm_parts(c_ref[...].reshape(256, 512).astype(F32))
    act = (unit * gain_ref[...] + shift_ref[...]).astype(BF)
    cact_ref[...] = act.reshape(4, 64, 512)
    kv = mm(act, w_ref[:, 512:])
    k_ref[...] = kv[:, :512].astype(BF).reshape(4, 64, 512)
    v_ref[...] = (kv[:, 512:] + b_ref[:, 512:]).astype(BF).reshape(4, 64, 512)

    def body(e):
        out, prob = attend(q_ref[e], k_ref[e], v_ref[e], masks, allow)
        out = out.reshape(4, 4, 2, 8, 512)
        oa_ref[:, :, e] = out[:, :, 0].astype(BF)
        ob_ref[:, :, e] = out[:, :, 1].astype(BF)
        p_ref[e] = prob

    each_feature(body)


HALF = 512


def middle(me_ref, *refs):
    (
        o1_ref, x0, x1, x2, x3, c0, c1, c2, c3,
        off1_ref, g2_ref, s2_ref, bf_ref, off2_ref, g3_ref, s3_ref, be_ref, br_ref,
    ) = refs[:18]
    weights_hbm = refs[18:23]
    refs = refs[-42:]
    gb1_ref, vec_ref, bias_ref = refs[:3]
    outs_hbm, kept_hbm = refs[3:6], refs[6:14]
    wm1_ref, wf_ref, wm2_ref, we_ref, wr_ref = refs[14:19]
    kept = refs[19:27]
    a2_ref, dqkv_ref, o2_ref, gb2_ref, a3_ref, gu_ref, hid_ref, gb3_ref = kept
    (
        o_scr, q_scr, k_scr, v_scr, p_scr, e_scr, gs_scr, go_scr, out_scr, back_scr,
        out0, out2, out13, in_sems, out_sems,
    ) = refs[27:]
    loads = [
        pltpu.make_async_copy(source, target, in_sems.at[i])
        for i, (source, target) in enumerate(zip(weights_hbm, refs[14:19]))
    ]
    for load in loads:
        load.start()
    stores = []

    def store(source, target, i):
        stores.append(pltpu.make_async_copy(source, target, out_sems.at[i]))
        stores[-1].start()

    def keep(ref):
        i = next(j for j in range(8) if kept[j] is ref)
        store(ref, kept_hbm[i], i)

    me = me_ref[0]
    matrix = swap_matrix(8)
    masks, masks32 = head_masks(BF), head_masks(F32)
    for f in range(4):
        o_scr[f] = swap(matrix, o1_ref[:, f].reshape(128, 512), True)

    def gather(*refs):
        return jnp.concatenate(
            [ref[s * 16 : (s + 1) * 16] for s in range(8) for ref in refs], axis=0
        )

    def scatter(values, *refs):
        for s in range(8):
            for d, ref in enumerate(refs):
                at = (s * 4 + d) * 16
                ref[s * 16 : (s + 1) * 16] = values[at : at + 16]

    def each_sample(body):
        def step(i, carry):
            for j in range(SAMPLE_UNROLL):
                rows = pl.ds(pl.multiple_of((i * SAMPLE_UNROLL + j) * 64, 64), 64)
                for quad in range(2):
                    body(rows, slice(quad * QUAD, (quad + 1) * QUAD))
            return carry

        lax.fori_loop(0, 8 // SAMPLE_UNROLL, step, 0)

    attended = gather(*(o_scr.at[d ^ me] for d in range(4)))
    gb3_ref[...] = gather(c0, c1, c2, c3)
    keep(gb3_ref)
    loads[0].wait()
    r1 = gather(x0, x1, x2, x3).astype(F32) + mm(attended, wm1_ref[...]) + off1_ref[...]
    unit2, inv2 = norm_parts(r1)
    a2_ref[...] = (unit2 * g2_ref[...] + s2_ref[...]).astype(BF)
    keep(a2_ref)
    loads[1].wait()
    q = (mm(a2_ref[...], wf_ref[:, :512]) + bf_ref[:, :512]).astype(BF)
    q_scr[...] = q * jnp.asarray(SCALE, BF)
    k_scr[...] = mm(a2_ref[...], wf_ref[:, 512:1024]).astype(BF)
    v_scr[...] = (mm(a2_ref[...], wf_ref[:, 1024:]) + bf_ref[:, 512:]).astype(BF)

    def score(rows, cols):
        p_scr[rows, cols] = mm(q_scr[rows, cols], stack_heads(k_scr[rows, cols], masks), 1, 1)

    each_sample(score)
    for i in range(4):
        rows = slice(i * 128, (i + 1) * 128)
        scores = p_scr[rows]
        raised = jnp.exp(scores - group_reduce(scores, jnp.max, -jnp.inf))
        p_scr[rows] = raised / group_reduce(raised, jnp.sum, 0.0)

    def mix(rows, cols):
        o2_ref[rows, cols] = mm(
            p_scr[rows, cols].astype(BF), stack_heads(v_scr[rows, cols], masks)
        ).astype(BF)

    each_sample(mix)
    keep(o2_ref)
    loads[2].wait()
    r2 = r1 + mm(o2_ref[...], wm2_ref[...]) + off2_ref[...]
    unit3, inv3 = norm_parts(r2)
    a3_ref[...] = (unit3 * g3_ref[...] + s3_ref[...]).astype(BF)
    keep(a3_ref)
    loads[3].wait()
    loads[4].wait()
    out_scr[...] = r2 + br_ref[...]
    back_scr[...] = jnp.zeros((HALF, 512), F32)

    def expand(b, carry):
        cols = pl.ds(pl.multiple_of(b * WIDE, WIDE), WIDE)
        u = mm(a3_ref[...], we_ref[:, cols]) + be_ref[:, cols]
        cdf, density = gelu_parts(u)
        hidden = (u * cdf).astype(BF)
        hid_ref[:, cols] = hidden
        gh = mm(gb3_ref[...], wr_ref[cols, :], 1, 1).astype(BF).astype(F32)
        gu = (gh * (cdf + u * density)).astype(BF)
        gu_ref[:, cols] = gu
        bias_ref[:, cols] = col_sum(gu)
        out_scr[...] += mm(hidden, wr_ref[cols, :])
        back_scr[...] += mm(gu, we_ref[:, cols], 1, 1)
        return carry

    lax.fori_loop(0, 2048 // WIDE, expand, 0, unroll=EXPAND_UNROLL)
    keep(hid_ref)
    keep(gu_ref)
    scatter(out_scr[...].astype(BF), out0, out13.at[0], out2, out13.at[1])
    rows = pl.ds(pl.multiple_of(me_ref[8] * 128, 128), 128)
    store(out0, outs_hbm[0].at[rows], 8)
    store(out2, outs_hbm[1].at[rows], 9)
    store(out13, outs_hbm[2].at[:, rows], 10)
    back, cot = back_scr[...], gb3_ref[...]
    vecs = [col_sum(back * unit3), col_sum(back)]
    gr2 = cot.astype(F32) + norm_back(back, unit3, inv3, g3_ref[...])
    gb2_ref[...] = gr2.astype(BF)
    keep(gb2_ref)
    go_scr[...] = mm(gb2_ref[...], wm2_ref[...], 1, 1).astype(BF)

    def weigh(rows, cols):
        e_scr[rows, cols] = mm(go_scr[rows, cols], stack_heads(v_scr[rows, cols], masks), 1, 1)

    each_sample(weigh)
    for i in range(4):
        rows = slice(i * 128, (i + 1) * 128)
        prob, grad = p_scr[rows], e_scr[rows]
        inner = group_reduce(prob * grad, jnp.sum, 0.0)
        gs_scr[rows] = (prob * (grad - inner)).astype(BF)

    def spread(rows, cols):
        gs, at = gs_scr[rows, cols], cols.start
        dq = mm(gs, stack_heads(k_scr[rows, cols], masks)) * SCALE
        dqkv_ref[rows, at : at + QUAD] = dq.astype(BF)
        dk = pick_heads(mm(gs, q_scr[rows, cols], 0, 0), masks32)
        dqkv_ref[rows, 512 + at : 512 + at + QUAD] = dk.astype(BF)
        dv = pick_heads(mm(p_scr[rows, cols].astype(BF), go_scr[rows, cols], 0, 0), masks32)
        dqkv_ref[rows, 1024 + at : 1024 + at + QUAD] = dv.astype(BF)

    each_sample(spread)
    keep(dqkv_ref)
    dqkv = dqkv_ref[...]
    back = mm(dqkv, wf_ref[...], 1, 1)
    vecs += [col_sum(back * unit2), col_sum(back)]
    gr1 = gr2 + norm_back(back, unit2, inv2, g2_ref[...])
    scatter(gr1.astype(BF), *(o_scr.at[d ^ me] for d in range(4)))
    for f in range(4):
        gb1_ref[:, f] = swap(matrix, o_scr[f]).reshape(4, 4, 8, 512)
    vecs += [
        col_sum(gb2_ref[...]), col_sum(cot), col_sum(dqkv[:, :512]), col_sum(dqkv[:, 1024:])
    ]
    vec_ref[...] = jnp.concatenate(vecs, axis=0)
    for copy in stores:
        copy.wait()


SAMPLE_UNROLL = 8
EXPAND_UNROLL = False
WIDE = 512


def backward_one(
    ga_ref, gb_ref, c_ref, q_ref, k_ref, v_ref, p_ref, w_ref, wm_ref,
    gb1_ref, dq_ref, dkv_ref, term_ref, vec_ref,
    g_scr,
):
    masks, masks32 = head_masks(BF), head_masks(F32)
    vec_ref[...] = jnp.zeros((8, 512), F32)

    def body(e):
        g_scr[:, :, 0] = ga_ref[:, :, e]
        g_scr[:, :, 1] = gb_ref[:, :, e]
        gb1 = g_scr[...].reshape(256, 512)
        gb1_ref[e] = gb1
        go = mm(gb1, wm_ref[...], 1, 1).astype(BF)
        dq, dk, dv = attend_back(q_ref[e], k_ref[e], v_ref[e], p_ref[e], go, masks, masks32)
        dq_ref[e], dkv_ref[e, :, :512], dkv_ref[e, :, 512:] = dq, dk, dv
        vec_ref[2:3] += col_sum(gb1)
        vec_ref[3:4] += col_sum(dq)

    each_feature(body)
    dkv = dkv_ref[...].reshape(256, 1024)
    term = mm(dkv, w_ref[:, 512:], 1, 1)
    term_ref[...] = term.astype(BF).reshape(4, 64, 512)
    unit, _ = norm_parts(c_ref[...].reshape(256, 512).astype(F32))
    vec_ref[0:1], vec_ref[1:2] = col_sum(term * unit), col_sum(term)
    vec_ref[4:5] = col_sum(dkv[:, 512:])


def backward_input(
    me_ref, gb1_ref, x_ref, dq_ref, term_ref, got_ref, vec1_ref, gain_ref, w_ref,
    grad_ref, vec_ref, a_scr,
):
    here, quad = me_ref[1] == me_ref[2], me_ref[3]
    gain = gain_ref[...]
    vec_ref[...] = vec1_ref[...]

    def body(e):
        back = mm(dq_ref[e], w_ref[:, :512], 1, 1)
        unit, inverse = norm_parts(x_ref[:, e].reshape(256, 512).astype(F32))
        vec_ref[0:1] += col_sum(back * unit)
        vec_ref[1:2] += col_sum(back)
        a_scr[...] = back.reshape(4, 64, 512)

        @pl.when(here)
        def _():
            a_scr[quad] += term_ref[e].astype(F32) + got_ref[e].astype(F32)

        back = a_scr[...].reshape(256, 512)
        grad = gb1_ref[e].astype(F32) + norm_back(back, unit, inverse, gain)
        grad_ref[:, e] = grad.astype(BF).reshape(4, 64, 512)

    each_feature(body)


def split(got_ref, out_ref):
    rest = jnp.sum(got_ref[...], axis=0, keepdims=True)
    out_ref[...] = jnp.zeros_like(out_ref)
    for i in range(3):
        term = rest.astype(BF)
        out_ref[i : i + 1] = term
        rest = rest - term.astype(F32)


def place(me_ref, b0, b1, b2, b3, out_ref):
    for d, ref in enumerate((b0, b1, b2, b3)):
        out_ref[d ^ me_ref[0]] = ref[...]


def lay_out(me_ref, read, order, *pairs):
    core, xx, yy, zz = me_ref[4], me_ref[5], me_ref[6], me_ref[7]
    for bits in range(16):
        index = tuple((bits >> i) & 1 for i in (3, 2, 1, 0))
        dx, dy, d1, d2 = (index[order.index(name)] for name in ("x", "y", "z", "w"))
        shard = (zz ^ d1 ^ (2 * d2)) * 2 + (yy ^ dy)
        for keep_ref, send_ref, start, rows in pairs:
            keep_ref[index] = read(2 * core + (dx ^ xx), shard, start, rows)
            send_ref[index] = read(2 * (1 - core) + (dx ^ xx), shard, start, rows)


def read_units(scr):
    def read(unit, shard, start, rows):
        return scr[unit, pl.ds(pl.multiple_of(shard * 64 + start, rows), rows)]

    return read


def over_tokens(*pairs):
    return sum(mm(a[...], b[...], 0, 0) for a, b in pairs).astype(BF)


def grads_reduce(me_ref, hida_ref, hidb_ref, gba_ref, gbb_ref, keep_ref, send_ref, scr):
    step = pl.program_id(0)
    start = pl.multiple_of(step * 512, 512)
    scr[pl.ds(start, 512)] = over_tokens((hida_ref, gba_ref), (hidb_ref, gbb_ref))

    def read(unit, shard, start, rows):
        return scr[pl.ds(pl.multiple_of(shard * 256 + unit * 64, 64), 64)]

    @pl.when(step == 3)
    def _():
        lay_out(me_ref, read, "zxyw", (keep_ref, send_ref, 0, 64))


def grads_expand(me_ref, acta_ref, actb_ref, gua_ref, gub_ref, keep_ref, send_ref, scr):
    step = pl.program_id(0)
    scr[step] = over_tokens((acta_ref, gua_ref), (actb_ref, gub_ref))

    @pl.when(step == 3)
    def _():
        lay_out(me_ref, read_units(scr), "yxzw", (keep_ref, send_ref, 0, 64))


def grads_feature(
    me_ref, acta_ref, actb_ref, dqa_ref, dqb_ref, oa_ref, ob_ref, gba_ref, gbb_ref,
    keep_ref, send_ref, scr,
):
    step = pl.program_id(0)

    @pl.when(step < 3)
    def _():
        scr[step] = over_tokens((acta_ref, dqa_ref), (actb_ref, dqb_ref))

    @pl.when(step == 3)
    def _():
        scr[3] = over_tokens((oa_ref, gba_ref), (ob_ref, gbb_ref))
        lay_out(me_ref, read_units(scr), "xyzw", (keep_ref, send_ref, 0, 64))


def grads_sample(
    me_ref, act_ref, dq_ref, cact_ref, dkv_ref, oa_ref, ga_ref, ob_ref, gb_ref,
    keepa_ref, senda_ref, keepb_ref, sendb_ref, scr,
):
    scr[0] = mm(act_ref[...], dq_ref[...], 0, 0).astype(BF)
    scr[1] = mm(cact_ref[...], dkv_ref[:, :512], 0, 0).astype(BF)
    scr[2] = mm(cact_ref[...], dkv_ref[:, 512:], 0, 0).astype(BF)
    total = mm(oa_ref[...], ga_ref[...], 0, 0) + mm(ob_ref[...], gb_ref[...], 0, 0)
    scr[3] = total.astype(BF)
    lay_out(me_ref, read_units(scr), "xyzw", (keepa_ref, senda_ref, 0, 32))
    lay_out(me_ref, read_units(scr), "xyzw", (keepb_ref, sendb_ref, 32, 32))


def spec(shape, index=None):
    return pl.BlockSpec(shape, index if index is not None else (lambda *a: (0,) * len(shape)))


def sds(shape, dtype=BF):
    return jax.ShapeDtypeStruct(shape, dtype)


def big(shape, dtype=BF):
    return pltpu.HBM(shape, dtype)


def outside(array):
    if array.size * array.dtype.itemsize < 1 << 18:
        return array
    return pltpu.with_memory_space_constraint(array, pltpu.HBM)


def params(limit):
    return pltpu.CompilerParams(vmem_limit_bytes=limit << 20)


def row(vector):
    return vector.reshape(1, -1)


def cost(microseconds):
    return pl.CostEstimate(
        flops=int(microseconds * 1.1e9), transcendentals=0, bytes_accessed=int(microseconds * 2e6)
    )


def whole_block(out):
    shape = out.shape
    return pl.BlockSpec(shape, lambda i: (0,) * len(shape))


def whole(kernel, name, limit, outs, scratch, *inputs, steps=1, time=3):
    arrays, specs = [], []
    for entry in inputs:
        if not isinstance(entry, tuple) and entry.ndim == 1:
            arrays.append(entry)
            specs.append(pl.BlockSpec(memory_space=pltpu.SMEM))
            continue
        array, block, index = entry if isinstance(entry, tuple) else (entry, None, None)
        arrays.append(outside(array))
        block = array.shape if block is None else block
        index = (0,) * array.ndim if index is None else index
        if not callable(index):
            index = lambda i, index=index: index
        specs.append(pl.BlockSpec(block, index))
    return pl.pallas_call(
        kernel,
        grid=(steps,),
        out_shape=outs,
        in_specs=specs,
        out_specs=jax.tree.map(whole_block, outs, is_leaf=lambda o: hasattr(o, "dtype")),
        scratch_shapes=scratch,
        compiler_params=params(limit),
        cost_estimate=cost(time),
        name=name,
    )(*arrays)


def shuffle(value, axis, mask):
    size = lax.axis_size(axis)
    return lax.ppermute(value, axis, [(i, i ^ mask) for i in range(size)])


SAMP = ("half", "quad")
CORE, X, Y, Z, W = ("feat", 1), ("feat", 2), ("quad", 1), ("quad", 2), ("half", 1)


def at(stacked, index, axis=0):
    return lax.dynamic_index_in_dim(stacked, index, axis, keepdims=False)


def fence(tree):
    return lax.optimization_barrier(tree)


def plus(a, b):
    return (a.astype(F32) + b.astype(F32)).astype(BF)


class Chain:
    def __init__(self, keep, sent, dims):
        self.keep, self.sent, self.dims = keep, sent, (CORE,) + dims

    def start(self):
        return shuffle(self.sent, *self.dims[0])

    def take(self, got):
        self.dims = self.dims[1:]
        if self.dims:
            self.keep, self.sent = plus(self.keep[0], got[0]), plus(self.keep[1], got[1])
        else:
            self.keep = plus(self.keep, got)


def together(chains, make=lambda: ()):
    got = [chain.start() for chain in chains]
    got, other = fence((got, make()))
    for chain, value in zip(chains, got):
        chain.take(value)
    return other


def local_small(
    layer_input, segment_ids, context_flags,
    first_gain, first_shift, sample_weight, sample_bias, sample_mixer, sample_offset,
    second_gain, second_shift, feature_weight, feature_bias, feature_mixer, feature_offset,
    third_gain, third_shift, expand_weight, expand_bias, reduce_weight, reduce_bias, cotangent,
):
    half, quad, feat = (lax.axis_index(name) for name in ("half", "quad", "feat"))
    samp = half * 4 + quad
    core, xx = feat % 2, feat // 2
    flags = context_flags.reshape(8, 64)[:, 0]
    root = jnp.sum(jnp.where(flags == 1, jnp.arange(8, dtype=jnp.int32), 0))
    me = [feat, half, root // 4, root % 4, core, xx, samp % 2, samp // 2]
    me = jnp.stack(me).astype(jnp.int32)

    turned = whole(turn_in, "turn_in", 8, big((16, 4, 16, 512)), [], layer_input.reshape(1024, 512))
    turned, layer_input, cotangent = fence((turned, layer_input, cotangent))
    x_t = lax.all_to_all(turned.reshape(4, 4, 64, 512), "quad", 0, 0)
    x4, cot4 = layer_input.reshape(4, 256, 512), cotangent.reshape(4, 256, 512)
    block = lambda value, d: at(value, feat ^ d)
    to_core = jnp.stack([block(x4, 1), block(cot4, 1), block(x4, 3), block(cot4, 3)])
    from_core = shuffle(to_core, *CORE)
    x_far = shuffle(jnp.stack([block(x4, 2), from_core[2]]), *X)
    x_t, from_core, x_far = fence((x_t, from_core, x_far))
    cot_far = shuffle(jnp.stack([block(cot4, 2), from_core[3]]), *X)
    own_context = at(x_t, root % 4)
    got_context = shuffle(own_context, *W)
    act1, queries = whole(
        project_queries, "project_queries", 16, (big((4, 256, 512)), big((4, 256, 512))), [],
        x_t, row(first_gain), row(first_shift), sample_weight, row(sample_bias),
    )
    cot_far, got_context, q1 = fence((cot_far, got_context, queries))

    tasks = segment_ids.reshape(8, 64)
    context_tasks = jnp.concatenate([at(tasks, root)] * 4).reshape(1, 256)
    sent = big((4, 4, 4, 8, 512))
    four = sds((4, 64, 512))
    oa, ob, context, cact, k1, v1, p1 = whole(
        forward_one, "forward_one", 24,
        (sent, sent, four, four, four, four, big((4, 256, 512), F32)), [],
        me, q1, own_context, got_context, at(segment_ids.reshape(2, 256, 1), half), context_tasks,
        row(first_gain), row(first_shift), sample_weight, row(sample_bias), time=7,
    )

    def exchange(value):
        shape = value.shape
        value = value.reshape((16,) + shape[2:])
        return lax.all_to_all(value, ("quad", "feat"), 0, 0).reshape(shape)

    rows_in = [
        row(v)
        for v in (
            sample_offset, second_gain, second_shift, feature_bias, feature_offset, third_gain,
            third_shift, expand_bias, reduce_bias,
        )
    ]
    weights = [sample_mixer, feature_weight, feature_mixer, expand_weight, reduce_weight]

    def run_middle(half, attended, earlier):
        own = spec((None, 128, 512), lambda i, m: (m[0], m[8], 0))
        part = lambda n: spec((None, 128, 512), lambda i, m: (n, m[8], 0))
        outs = (sent, sds((8, 512), F32), sds((1, 2048), F32))
        blocks = ((256, 512), (256, 512), (2, 256, 512))
        kept = tuple((HALF, n) for n in (512, 1536, 512, 512, 512, 2048, 2048, 512))
        still = lambda shape: spec(shape, lambda i, m: (0,) * len(shape))
        far = pl.BlockSpec(memory_space=pl.ANY)
        vmem = lambda shape, dtype=BF: pltpu.VMEM(shape, dtype)
        rows, rows32 = vmem((HALF, 512)), vmem((HALF, 512), F32)
        return pl.pallas_call(
            middle,
            grid_spec=pltpu.PrefetchScalarGridSpec(
                num_scalar_prefetch=1,
                grid=(1,),
                in_specs=[still((4, 4, 4, 8, 512))]
                + [own, part(0), part(0), part(1), own, part(1), part(0), part(1)]
                + [still(r.shape) for r in rows_in]
                + [far] * (5 + len(earlier)),
                out_specs=[still(o.shape) for o in outs] + [far] * 11,
                scratch_shapes=[vmem(w.shape) for w in weights]
                + [vmem(shape) for shape in kept]
                + [
                    vmem((4, 128, 512)), rows, rows, rows, rows32, rows32, rows, rows, rows32,
                    rows32, vmem((128, 512)), vmem((128, 512)), vmem((2, 128, 512)),
                    pltpu.SemaphoreType.DMA((5,)), pltpu.SemaphoreType.DMA((11,)),
                ],
            ),
            out_shape=outs + tuple(big(shape) for shape in blocks + kept),
            input_output_aliases={24 + i: 3 + i for i in range(len(earlier))},
            compiler_params=params(44),
            cost_estimate=cost(30),
            name="middle",
        )(
            jnp.concatenate([me, jnp.full((1,), half, jnp.int32)]),
            *(
                outside(array)
                for array in (
                    attended, x4, from_core, x_far, x_far, cot4, from_core, cot_far, cot_far,
                    *rows_in, *weights, *earlier,
                )
            ),
        )

    oa_f, ob = fence((exchange(oa), ob))
    ob_f = exchange(ob)
    ga, vec_a, bias_a, *first = run_middle(0, oa_f, [])
    ob_f, ga, first = fence((ob_f, ga, first))
    ga_t = exchange(ga)
    gb, vec_b, bias_b, *second = run_middle(1, ob_f, first[:3])
    ga_t, gb, second = fence((ga_t, gb, second))
    out0, out2, out13 = second[:3]
    act2, dqkv, o2, gb2, act3, gu, hidden, gb3 = zip(first[3:], second[3:])
    gb_t = exchange(gb)
    vec2, bias2 = vec_a + vec_b, bias_a + bias_b

    parts = sds((2, 2, 2, 2, 64, 512))
    moving = lambda pair: [(a, (512, 512), lambda i: (0, i)) for a in pair]
    upto = lambda pair: [(a, (512, 512), lambda i: (0, jnp.minimum(i, 2))) for a in pair]
    units = [pltpu.VMEM((4, 512, 512), BF)]
    r_chain = Chain(
        *whole(
            grads_reduce, "grads_reduce", 16, (parts, parts), [pltpu.VMEM((2048, 512), BF)],
            me, *moving(hidden), *gb3, steps=4, time=6,
        ),
        (Z, X, Y, W),
    )
    e_chain = Chain(
        *whole(
            grads_expand, "grads_expand", 16, (parts, parts), units,
            me, *act3, *moving(gu), steps=4, time=6,
        ),
        (Y, X, Z, W),
    )
    f_chain = Chain(
        *whole(
            grads_feature, "grads_feature", 20, (parts, parts), units,
            me, *act2, *upto(dqkv), *o2, *gb2, steps=4, time=6,
        ),
        (X, Y, Z, W),
    )
    chains = [r_chain, e_chain, f_chain]
    near = shuffle(out13, *CORE)
    gb_t, near, kept = fence((gb_t, near, [(chain.keep, chain.sent) for chain in chains]))
    for chain, pair in zip(chains, kept):
        chain.keep, chain.sent = pair

    full = big((4, 256, 512))
    gb1, dq1, dkv, term, vec1 = together(
        chains,
        lambda: whole(
            backward_one, "backward_one", 32,
            (full, full, sds((4, 64, 1024)), four, sds((8, 512), F32)),
            [pltpu.VMEM((4, 4, 2, 8, 512), BF)],
            ga_t, gb_t, context, q1, k1, v1, p1, sample_weight, sample_mixer, time=10,
        ),
    )

    small = sds((2, 2, 2, 2, 32, 512))
    flat2 = lambda a: a.reshape(-1, a.shape[-1])
    grads = whole(
        grads_sample, "grads_sample", 20, (small,) * 4, units,
        me, *(flat2(a) for a in (act1, dq1, cact, dkv, oa, ga_t, ob, gb_t)),
    )
    got_term, (ak, as_, bk, bs) = together(chains, lambda: (shuffle(term, *W), grads))
    late = [Chain(ak, as_, (X, Y)), Chain(bk, bs, (X, Y))]
    grad_t, vec1 = together(
        late + chains,
        lambda: whole(
            backward_input, "backward_input", 24, (big((4, 4, 64, 512)), sds((8, 512), F32)),
            [pltpu.VMEM((4, 64, 512), F32)],
            me, gb1, x_t, dq1, term, got_term, vec1, row(first_gain), sample_weight,
        ),
    )

    owned = lambda v, n: v.reshape(-1, 8, n).transpose(1, 0, 2).reshape(8, -1)
    vectors = jnp.concatenate(
        [
            owned(vec2[:6], 64), vec2[6:].reshape(8, 128), bias2.reshape(8, 256),
            owned(vec1[:3], 64), vec1[3:5].reshape(8, 128),
        ],
        axis=1,
    )
    got, far, vectors = together(
        late + chains,
        lambda: (
            lax.all_to_all(grad_t, "quad", 0, 0),
            shuffle(jnp.stack([out2, near[1]]), *X),
            vectors,
        ),
    )
    vectors = lax.all_to_all(vectors, SAMP, 0, 0)
    input_grad = whole(
        turn_out, "turn_out", 8, sds((1024, 512)), [], got.reshape(16, 4, 16, 512)
    ).reshape(64, 16, 512)
    layer_output = whole(
        place, "place", 16, sds((4, 256, 512)), [], me, out0,
        (near, (None, 256, 512), (0, 0, 0)), (far, (None, 256, 512), (0, 0, 0)),
        (far, (None, 256, 512), (1, 0, 0)),
    ).reshape(64, 16, 512)
    vectors, input_grad, layer_output = together(
        late + chains, lambda: (vectors, input_grad, layer_output)
    )

    rows = jnp.concatenate([chain.keep for chain in late], axis=2)
    around_z = lambda value, mask: lax.ppermute(value, SAMP, [(j, j ^ mask) for j in range(8)])
    from_z = [around_z(rows[i // 2, i % 2], (0, 4, 2, 6)[i]) for i in (1, 2, 3)]
    vectors = whole(split, "split", 8, sds((24, 1088)), [], vectors)
    early = lax.all_gather(jnp.concatenate([chain.keep for chain in chains]), "feat")
    from_z, early, vectors = fence((from_z, early, vectors))
    total = rows[0, 0].astype(F32)
    for value in from_z:
        total = total + value.astype(F32)
    vectors = jnp.pad(vectors[:3].reshape(-1), (0, 8 * 512 - 3 * 1088)).reshape(8, 512)
    last = lax.all_gather(jnp.concatenate([total.astype(BF), vectors]), "feat")
    mine = last[:, 64:].reshape(4, -1).astype(F32)
    mine = sum(mine[:, i * 1088 : (i + 1) * 1088] for i in range(3))
    mine = (mine[0] + mine[1]) + (mine[2] + mine[3])

    units_of = lambda rows: [rows[i].astype(F32) for i in (0, 2, 1, 3)]
    reduce_grad = jnp.concatenate(units_of(early[:, :64]))
    expand, feature = units_of(early[:, 64:128]), units_of(early[:, 128:])
    sample = units_of(last[:, :64])

    gain3, shift3, gain2, shift2, off2, bias_r = (mine[i * 64 : (i + 1) * 64] for i in range(6))
    feature_b, expand_b = mine[384:512], mine[512:768]
    gain1, shift1, off1 = (mine[768 + i * 64 : 832 + i * 64] for i in range(3))
    sample_b = mine[960:1088]
    columns = lambda blocks: jnp.concatenate(blocks, axis=1)

    return (
        layer_output, input_grad,
        gain1, shift1, columns(sample[:3]), sample_b, sample[3], off1,
        gain2, shift2, columns(feature[:3]), feature_b, feature[3], off2,
        gain3, shift3, columns(expand), expand_b,
        reduce_grad, bias_r,
    )


def spread_2(block, axis, owner):
    block = jnp.where(lax.axis_index(axis) == owner, block, jnp.zeros_like(block))
    return lax.psum(block, axis)


def layer_norm(values, gain_row, shift_row):
    center = jnp.mean(values, axis=-1, keepdims=True)
    spread = values - center
    variance = jnp.mean(spread * spread, axis=-1, keepdims=True)
    return spread * lax.rsqrt(variance + EPS) * gain_row + shift_row


def apply_weight(active, weight):
    return jnp.einsum("sfd,de->sfe", active, weight, preferred_element_type=jnp.float32)


def input_back(grad_out, weight):
    return jnp.einsum("sfe,de->sfd", grad_out, weight, preferred_element_type=jnp.float32)


def weight_grad(active, grad_out):
    return jnp.einsum("sfd,sfe->de", active, grad_out, preferred_element_type=jnp.float32)


def column_sum(values):
    return jnp.sum(values.astype(jnp.float32), axis=(0, 1))


def project(active, weight, bias_row):
    model_width = active.shape[-1]
    joined = apply_weight(active, weight)
    queries = (joined[..., :model_width] + bias_row[:model_width]).astype(jnp.bfloat16)
    key_part = joined[..., model_width : 2 * model_width].astype(jnp.bfloat16)
    value_part = (joined[..., 2 * model_width :] + bias_row[model_width:]).astype(jnp.bfloat16)
    return (queries, key_part, value_part)


def split_heads(values):
    return values.reshape(values.shape[0], values.shape[1], HEADS, HEAD_DIM)


def join_heads(values):
    return values.reshape(values.shape[0], values.shape[1], HEADS * HEAD_DIM)


def soft_weights(scores):
    top_score = jnp.max(scores, axis=-1, keepdims=True)
    raised = jnp.exp(scores - top_score)
    return raised / jnp.sum(raised, axis=-1, keepdims=True)


def feature_attend(queries, key_part, value_part):
    score_scale = HEAD_DIM ** (-0.5)
    scores = (
        jnp.einsum(
            "sfhd,sghd->shfg",
            split_heads(queries),
            split_heads(key_part),
            preferred_element_type=jnp.float32,
        )
        * score_scale
    )
    probability = soft_weights(scores)
    mixed = jnp.einsum(
        "shfg,sghd->sfhd",
        probability.astype(jnp.bfloat16),
        split_heads(value_part),
        preferred_element_type=jnp.float32,
    )
    return (join_heads(mixed).astype(jnp.bfloat16), probability)


def feature_grads(queries, key_part, value_part, probability, grad_mixed):
    score_scale = HEAD_DIM ** (-0.5)
    grad_heads = split_heads(grad_mixed)
    grad_weights = jnp.einsum(
        "sfhd,sghd->shfg", grad_heads, split_heads(value_part), preferred_element_type=jnp.float32
    )
    inner_sum = jnp.sum(probability * grad_weights, axis=-1, keepdims=True)
    grad_scores = (probability * (grad_weights - inner_sum)).astype(jnp.bfloat16)
    grad_queries = (
        jnp.einsum(
            "shfg,sghd->sfhd",
            grad_scores,
            split_heads(key_part),
            preferred_element_type=jnp.float32,
        )
        * score_scale
    )
    grad_keys = (
        jnp.einsum(
            "shfg,sfhd->sghd", grad_scores, split_heads(queries), preferred_element_type=jnp.float32
        )
        * score_scale
    )
    grad_values = jnp.einsum(
        "shfg,sfhd->sghd",
        probability.astype(jnp.bfloat16),
        grad_heads,
        preferred_element_type=jnp.float32,
    )
    return (join_heads(grad_queries), join_heads(grad_keys), join_heads(grad_values))


def local_large(
    layer_input,
    segment_ids,
    context_flags,
    first_gain,
    first_shift,
    sample_weight,
    sample_bias,
    sample_mixer,
    sample_offset,
    second_gain,
    second_shift,
    feature_weight,
    feature_bias,
    feature_mixer,
    feature_offset,
    third_gain,
    third_shift,
    expand_weight,
    expand_bias,
    reduce_weight,
    reduce_bias,
    cotangent,
):
    sample_rows = layer_input.shape[0]
    feature_rows = layer_input.shape[1]
    model_width = layer_input.shape[2]
    score_scale = HEAD_DIM ** (-0.5)
    shard_count = lax.axis_size("samp")
    context_shards = shard_count // 8
    total_context = context_shards * sample_rows
    residual_zero = layer_input.astype(jnp.float32)
    normed_one, norm_one_back = jax.vjp(layer_norm, residual_zero, first_gain, first_shift)
    active_one = normed_one.astype(jnp.bfloat16)
    queries_one, keys_one, values_one = project(active_one, sample_weight, sample_bias)
    my_index = lax.axis_index("samp")
    shard_flags = context_flags.reshape(shard_count, sample_rows)[:, 0]
    shard_rank = jnp.cumsum(shard_flags) - 1
    shard_ids = jnp.arange(shard_count, dtype=jnp.int32)
    slot_ids = jnp.arange(context_shards, dtype=jnp.int32)
    root_hits = (shard_rank[None, :] == slot_ids[:, None]) & (shard_flags[None, :] == 1)
    roots = jnp.sum(jnp.where(root_hits, shard_ids[None, :], 0), axis=1)
    context_tasks = jnp.take(segment_ids.reshape(shard_count, sample_rows), roots, axis=0).reshape(
        total_context
    )
    local_tasks = lax.dynamic_slice_in_dim(segment_ids, my_index * sample_rows, sample_rows)
    allowed = local_tasks[:, None] == context_tasks[None, :]
    is_context = shard_flags[my_index] == 1
    own_rank = jnp.maximum(shard_rank[my_index], 0)
    own_block = jnp.concatenate([keys_one, values_one], axis=-1)

    def fetch_rows(step, buffer):
        piece = spread_2(own_block, "samp", roots[step])
        return lax.dynamic_update_slice_in_dim(buffer, piece, step * sample_rows, 0)

    empty_rows = jnp.zeros((total_context, feature_rows, 2 * model_width), jnp.bfloat16)
    fetched = lax.fori_loop(0, context_shards, fetch_rows, empty_rows)
    context_keys = fetched[..., :model_width]
    context_values = fetched[..., model_width:]
    query_heads = split_heads(queries_one)
    key_heads = split_heads(context_keys)
    value_heads = split_heads(context_values)
    scores = (
        jnp.einsum("sfhd,cfhd->fhsc", query_heads, key_heads, preferred_element_type=jnp.float32)
        * score_scale
    )
    sample_prob = soft_weights(jnp.where(allowed[None, None], scores, MASKED))
    sample_weights = sample_prob.astype(jnp.bfloat16)
    mixed_one = join_heads(
        jnp.einsum(
            "fhsc,cfhd->sfhd", sample_weights, value_heads, preferred_element_type=jnp.float32
        )
    ).astype(jnp.bfloat16)
    residual_one = residual_zero + apply_weight(mixed_one, sample_mixer) + sample_offset
    normed_two, norm_two_back = jax.vjp(layer_norm, residual_one, second_gain, second_shift)
    active_two = normed_two.astype(jnp.bfloat16)
    queries_two, keys_two, values_two = project(active_two, feature_weight, feature_bias)
    all_keys, all_values = (
        lax.all_gather(keys_two, "feat", axis=1, tiled=True),
        lax.all_gather(values_two, "feat", axis=1, tiled=True),
    )
    mixed_two, feature_prob = feature_attend(queries_two, all_keys, all_values)
    residual_two = residual_one + apply_weight(mixed_two, feature_mixer) + feature_offset
    normed_three, norm_three_back = jax.vjp(layer_norm, residual_two, third_gain, third_shift)
    active_three = normed_three.astype(jnp.bfloat16)
    expanded = apply_weight(active_three, expand_weight) + expand_bias
    activated, gelu_back = jax.vjp(partial(jax.nn.gelu, approximate=False), expanded)
    hidden = activated.astype(jnp.bfloat16)
    layer_output = (residual_two + apply_weight(hidden, reduce_weight) + reduce_bias).astype(
        jnp.bfloat16
    )
    grad_out = cotangent.astype(jnp.float32)
    grad_branch = cotangent
    reduce_bias_grad = column_sum(grad_branch)
    reduce_weight_grad = weight_grad(hidden, grad_branch)
    grad_hidden = input_back(grad_branch, reduce_weight).astype(jnp.bfloat16)
    grad_expanded = gelu_back(grad_hidden.astype(jnp.float32))[0].astype(jnp.bfloat16)
    expand_bias_grad = column_sum(grad_expanded)
    expand_weight_grad = weight_grad(active_three, grad_expanded)
    grad_norm, third_gain_grad, third_shift_grad = norm_three_back(
        input_back(grad_expanded, expand_weight)
    )
    grad_two = grad_out + grad_norm
    grad_branch = grad_two.astype(jnp.bfloat16)
    feature_offset_grad = column_sum(grad_branch)
    feature_mixer_grad = weight_grad(mixed_two, grad_branch)
    grad_mixed = input_back(grad_branch, feature_mixer).astype(jnp.bfloat16)
    grad_queries, grad_keys, grad_values = feature_grads(
        queries_two, all_keys, all_values, feature_prob, grad_mixed
    )
    own_key_grads, own_value_grads = (
        lax.psum_scatter(grad_keys, "feat", scatter_dimension=1, tiled=True),
        lax.psum_scatter(grad_values, "feat", scatter_dimension=1, tiled=True),
    )
    grad_project = jnp.concatenate(
        [
            grad_queries.astype(jnp.bfloat16),
            own_key_grads.astype(jnp.bfloat16),
            own_value_grads.astype(jnp.bfloat16),
        ],
        axis=-1,
    )
    feature_weight_grad = weight_grad(active_two, grad_project)
    feature_bias_grad = jnp.concatenate(
        [
            column_sum(grad_project[..., :model_width]),
            column_sum(grad_project[..., 2 * model_width :]),
        ]
    )
    grad_norm, second_gain_grad, second_shift_grad = norm_two_back(
        input_back(grad_project, feature_weight)
    )
    grad_one = grad_two + grad_norm
    grad_branch = grad_one.astype(jnp.bfloat16)
    sample_offset_grad = column_sum(grad_branch)
    sample_mixer_grad = weight_grad(mixed_one, grad_branch)
    grad_heads = split_heads(input_back(grad_branch, sample_mixer).astype(jnp.bfloat16))
    grad_weights = jnp.einsum(
        "sfhd,cfhd->fhsc", grad_heads, value_heads, preferred_element_type=jnp.float32
    )
    inner_sum = jnp.sum(sample_prob * grad_weights, axis=-1, keepdims=True)
    grad_scores = (sample_prob * (grad_weights - inner_sum)).astype(jnp.bfloat16)
    grad_queries = (
        join_heads(
            jnp.einsum(
                "fhsc,cfhd->sfhd", grad_scores, key_heads, preferred_element_type=jnp.float32
            )
        )
        * score_scale
    ).astype(jnp.bfloat16)
    key_terms = (
        join_heads(
            jnp.einsum(
                "fhsc,sfhd->cfhd", grad_scores, query_heads, preferred_element_type=jnp.float32
            )
        )
        * score_scale
    )
    value_terms = join_heads(
        jnp.einsum(
            "fhsc,sfhd->cfhd", sample_weights, grad_heads, preferred_element_type=jnp.float32
        )
    )
    term_block = jnp.concatenate([key_terms, value_terms], axis=-1)
    summed_terms = lax.psum_scatter(term_block, "samp", scatter_dimension=0, tiled=True)
    summed_rows = lax.all_gather(summed_terms.astype(jnp.bfloat16), "samp", axis=0, tiled=True)
    own_grads = lax.dynamic_slice_in_dim(summed_rows, own_rank * sample_rows, sample_rows, 0)
    own_grads = jnp.where(is_context, own_grads, jnp.zeros_like(own_grads))
    grad_project = jnp.concatenate([grad_queries, own_grads], axis=-1)
    sample_weight_grad = weight_grad(active_one, grad_project)
    sample_bias_grad = jnp.concatenate(
        [column_sum(grad_queries), column_sum(own_grads[..., model_width:])]
    )
    grad_norm, first_gain_grad, first_shift_grad = norm_one_back(
        input_back(grad_project, sample_weight)
    )
    input_grad = (grad_one + grad_norm).astype(jnp.bfloat16)
    summed = lax.psum(
        (
            first_gain_grad,
            first_shift_grad,
            sample_weight_grad,
            sample_bias_grad,
            sample_mixer_grad,
            sample_offset_grad,
            second_gain_grad,
            second_shift_grad,
            feature_weight_grad,
            feature_bias_grad,
            feature_mixer_grad,
            feature_offset_grad,
            third_gain_grad,
            third_shift_grad,
            expand_weight_grad,
            expand_bias_grad,
            reduce_weight_grad,
            reduce_bias_grad,
        ),
        "feat",
    )
    shares = (
        lax.psum_scatter(summed[0], "samp", scatter_dimension=0, tiled=True),
        lax.psum_scatter(summed[1], "samp", scatter_dimension=0, tiled=True),
        lax.psum_scatter(summed[2], "samp", scatter_dimension=0, tiled=True),
        lax.psum_scatter(summed[3], "samp", scatter_dimension=0, tiled=True),
        lax.psum_scatter(summed[4], "samp", scatter_dimension=0, tiled=True),
        lax.psum_scatter(summed[5], "samp", scatter_dimension=0, tiled=True),
        lax.psum_scatter(summed[6], "samp", scatter_dimension=0, tiled=True),
        lax.psum_scatter(summed[7], "samp", scatter_dimension=0, tiled=True),
        lax.psum_scatter(summed[8], "samp", scatter_dimension=0, tiled=True),
        lax.psum_scatter(summed[9], "samp", scatter_dimension=0, tiled=True),
        lax.psum_scatter(summed[10], "samp", scatter_dimension=0, tiled=True),
        lax.psum_scatter(summed[11], "samp", scatter_dimension=0, tiled=True),
        lax.psum_scatter(summed[12], "samp", scatter_dimension=0, tiled=True),
        lax.psum_scatter(summed[13], "samp", scatter_dimension=0, tiled=True),
        lax.psum_scatter(summed[14], "samp", scatter_dimension=0, tiled=True),
        lax.psum_scatter(summed[15], "samp", scatter_dimension=0, tiled=True),
        lax.psum_scatter(summed[16], "samp", scatter_dimension=0, tiled=True),
        lax.psum_scatter(summed[17], "samp", scatter_dimension=0, tiled=True),
    )
    return (
        layer_output,
        input_grad,
        shares[0],
        shares[1],
        shares[2],
        shares[3],
        shares[4],
        shares[5],
        shares[6],
        shares[7],
        shares[8],
        shares[9],
        shares[10],
        shares[11],
        shares[12],
        shares[13],
        shares[14],
        shares[15],
        shares[16],
        shares[17],
    )


def solution(mesh):
    if mesh.shape["samp"] == 8 and mesh.shape["feat"] == 4:
        return solution_small(mesh)
    return jax.shard_map(
        local_large,
        mesh=mesh,
        in_specs=(
            P("samp", "feat", None),
            P(),
            P(),
            P(),
            P(),
            P(),
            P(),
            P(),
            P(),
            P(),
            P(),
            P(),
            P(),
            P(),
            P(),
            P(),
            P(),
            P(),
            P(),
            P(),
            P(),
            P("samp", "feat", None),
        ),
        out_specs=(
            P("samp", "feat", None),
            P("samp", "feat", None),
            P("samp"),
            P("samp"),
            P("samp", None),
            P("samp"),
            P("samp", None),
            P("samp"),
            P("samp"),
            P("samp"),
            P("samp", None),
            P("samp"),
            P("samp", None),
            P("samp"),
            P("samp"),
            P("samp"),
            P("samp", None),
            P("samp"),
            P("samp", None),
            P("samp"),
        ),
        check_vma=False,
    )


def solution_small(mesh):
    mesh = jax.sharding.Mesh(mesh.devices.reshape(2, 4, 4), ("half", "quad", "feat"))
    tokens, copied = P(SAMP, "feat", None), P()
    vector, matrix = P(SAMP), P(SAMP, None)
    return jax.shard_map(
        local_small,
        mesh=mesh,
        in_specs=(tokens,) + (copied,) * 20 + (tokens,),
        out_specs=(
            tokens, tokens, vector, vector, matrix, vector, matrix, vector,
            vector, vector, matrix, vector, matrix, vector,
            vector, vector, matrix, vector, matrix, vector,
        ),
        check_vma=False,
    )
```

profile of v0, /device:TPU:0, one launch (start us, length us, event | category | flops | bytes accessed | tf_op | source)
XLA Modules:
  0.0 270.1 jit_solution(3991782711669213055)
XLA Ops:
  0.7 2.8 %turn_in.1 = bf16[16,4,16,512]{3,2,1,0:T(8,128)(2,1)} custom-call(bf16[1024,512]{1,0:T(8,128)(2,1)} %bitcast.337), custom_call_target="tpu_custom_call" | custom-call | flops 3300000000 | bytes 6000000 | tf_op jit(solution)/shard_map/turn_in/pallas_call | solution.py:548
  4.3 4.8 %all-to-all-start = ((bf16[4,4,64,512]{3,2,1,0:T(8,128)(2,1)}), bf16[4,4,64,512]{3,2,1,0:T(8,128)(2,1)S(1)}, u32[]{:S(2)}, u32[]{:S(2)}) async-start(bf16[4,4,64,512]{3,2,1,0:T(8,128)(2,1)} %bitcast.10), calls=%async_computation | async-start | bytes 2097152 | tf_op jit(solution)/shard_map/all_to_all | solution.py:621
  10.2 1.6 collective-permute-start.1
  16.9 7.4 %collective-permute-done.1.refs_3_.refs_4_ = bf16[2,256,512]{2,1,0:T(8,128)(2,1)S(1)} collective-permute-done((bf16[2,256,512]{2,1,0:T(8,128)(2,1)S(1)}, bf16[2,256,512]{2,1,0:T(8,128)(2,1)S(1)}, u32[]{:S(2)}, u32[]{:S(2)}) %collective-permute-start.1) | collective-permute-done | bytes 524320 | tf_op jit(solution)/shard_map/ppermute | solution.py:563
  25.5 1.6 collective-permute-start.2
  27.1 2.7 collective-permute-start.3
  29.8 4.9 %project_queries.1 = (bf16[4,256,512]{2,1,0:T(8,128)(2,1)}, bf16[4,256,512]{2,1,0:T(8,128)(2,1)}) custom-call(bf16[4,4,64,512]{3,2,1,0:T(8,128)(2,1)} %copy-done.21, f32[1,512]{1,0:T(1,128)S(1)} %bitcast.327, f32[1,512]{1,0:T(1,128)S(1)} %bitcast.311, bf16[512,1536]{1,0:T(8,128)(2,1)} %w_ref.7, f32[1,1024]{1,0:T(1,128)S(1)} %bitcast.307), custom_call_target="tpu_custom_call" | custom-call | flops 3300000000 | bytes 6000000 | tf_op jit(solution)/shard_map/project_queries/pallas_call | solution.py:548
  34.8 6.3 %collective-permute-done.3.got_ref = bf16[4,64,512]{2,1,0:T(8,128)(2,1)S(1)} collective-permute-done((bf16[4,64,512]{2,1,0:T(8,128)(2,1)S(1)}, bf16[4,64,512]{2,1,0:T(8,128)(2,1)S(1)}, u32[]{:S(2)}, u32[]{:S(2)}) %collective-permute-start.3) | collective-permute-done | bytes 262176 | tf_op jit(solution)/shard_map/ppermute | solution.py:563
  41.8 8.9 %forward_one.1 = (bf16[4,4,4,8,512]{4,3,2,1,0:T(8,128)(2,1)}, bf16[4,4,4,8,512]{4,3,2,1,0:T(8,128)(2,1)}, bf16[4,64,512]{2,1,0:T(8,128)(2,1)S(1)}, bf16[4,64,512...) custom-call(s32[8]{0:T(128)S(1)} %stack.56.me_ref, ...), custom_call_target="tpu_custom_call" | custom-call | flops 7699999744 | bytes 14000000 | tf_op jit(solution)/shard_map/forward_one/pallas_call | solution.py:548
  52.9 3.7 %all-to-all-start.1 = ((bf16[16,4,8,512]{3,2,1,0:T(8,128)(2,1)}), bf16[16,4,8,512]{3,2,1,0:T(8,128)(2,1)S(1)}, u32[]{:S(2)}, u32[]{:S(2)}) async-start(bf16[16,4,8,512]{3,2,1,0:T(8,128)(2,1)} %bitcast.344), calls=%async_computation.1 | async-start | bytes 1048576 | tf_op jit(solution)/shard_map/all_to_all | solution.py:651
  56.8 10.3 %all-to-all-done.1 = bf16[16,4,8,512]{3,2,1,0:T(8,128)(2,1)S(1)} async-done(((bf16[16,4,8,512]{3,2,1,0:T(8,128)(2,1)}), bf16[16,4,8,512]{3,2,1,0:T(8,128)(2,1)S(1)}, u32[]{:S(2)}, u32[]{:S(2)}) %all-to-all-start.1) | async-done | bytes 524320 | tf_op jit(solution)/shard_map/all_to_all | solution.py:651
  67.1 3.8 %all-to-all-start.2 = ((bf16[16,4,8,512]{3,2,1,0:T(8,128)(2,1)}), bf16[16,4,8,512]{3,2,1,0:T(8,128)(2,1)S(1)}, u32[]{:S(2)}, u32[]{:S(2)}) async-start(bf16[16,4,8,512]{3,2,1,0:T(8,128)(2,1)} %bitcast.346), calls=%async_computation.2 | async-start | bytes 1048576 | tf_op jit(solution)/shard_map/all_to_all | solution.py:651
  71.0 20.7 %middle.2 = (bf16[4,4,4,8,512]{4,3,2,1,0:T(8,128)(2,1)}, f32[8,512]{1,0:T(8,128)S(1)}, f32[1,2048]{1,0:T(1,128)S(1)}, bf16[256,512]{1,0:T(8,128)(2,1)}, bf16[256...) custom-call(s32[9]{0:T(128)S(1)} %concatenate.48.me_ref, ...), custom_call_target="tpu_custom_call" | custom-call | flops 32999999488 | bytes 60000000 | tf_op jit(solution)/shard_map/middle/pallas_call | solution.py:672
  91.7 4.9 %all-to-all-start.3 = ((bf16[16,4,8,512]{3,2,1,0:T(8,128)(2,1)}), bf16[16,4,8,512]{3,2,1,0:T(8,128)(2,1)S(1)}, u32[]{:S(2)}, u32[]{:S(2)}) async-start(bf16[16,4,8,512]{3,2,1,0:T(8,128)(2,1)} %bitcast.352), calls=%async_computation.3 | async-start | bytes 1048576 | tf_op jit(solution)/shard_map/all_to_all | solution.py:651
  96.7 20.6 %middle.3 = (bf16[4,4,4,8,512]{4,3,2,1,0:T(8,128)(2,1)}, f32[8,512]{1,0:T(8,128)S(1)}, f32[1,2048]{1,0:T(1,128)S(1)}, bf16[256,512]{1,0:T(8,128)(2,1)}, bf16[256...) custom-call(s32[9]{0:T(128)S(1)} %concatenate.49.me_ref, ...), custom_call_target="tpu_custom_call", output_to_operand_aliasing={{3}: (24, {}), {4}: (25, {}), {5}: (26, {})} | custom-call | flops 32999999488 | bytes 60000000 | tf_op jit(solution)/shard_map/middle/pallas_call | solution.py:672
  117.3 5.2 %all-to-all-start.4 = ((bf16[16,4,8,512]{3,2,1,0:T(8,128)(2,1)}), bf16[16,4,8,512]{3,2,1,0:T(8,128)(2,1)}, u32[]{:S(2)}, u32[]{:S(2)}) async-start(bf16[16,4,8,512]{3,2,1,0:T(8,128)(2,1)} %bitcast.350), calls=%async_computation.4 | async-start | bytes 1048576 | tf_op jit(solution)/shard_map/all_to_all | solution.py:651
  122.9 5.2 %grads_expand.1 = (bf16[2,2,2,2,64,512]{5,4,3,2,1,0:T(8,128)(2,1)S(1)}, bf16[2,2,2,2,64,512]{5,4,3,2,1,0:T(8,128)(2,1)S(1)}) custom-call(s32[8]{0:T(128)S(1)} %stack.56.me_ref, bf16[512,512]{1,0:T(8,128)(2,1)} %get-tuple-element.214.acta_ref, bf16[512,512]{1,0:T(8,128)(2,1)} %get-tuple-element.215.actb_ref, bf16[512,2048]{1,0:T(8,128)(2,1)} %get-tuple-element.216.gua_ref, ...), custom_call_target="tpu_custom_call" | custom-call | flops 6600000000 | bytes 12000000 | tf_op jit(solution)/shard_map/grads_expand/pallas_call | solution.py:548
  129.1 5.2 %grads_reduce.1 = (bf16[2,2,2,2,64,512]{5,4,3,2,1,0:T(8,128)(2,1)S(1)}, bf16[2,2,2,2,64,512]{5,4,3,2,1,0:T(8,128)(2,1)S(1)}) custom-call(s32[8]{0:T(128)S(1)} %stack.56.me_ref, bf16[512,2048]{1,0:T(8,128)(2,1)} %get-tuple-element.208.hida_ref, bf16[512,2048]{1,0:T(8,128)(2,1)} %get-tuple-element.209.hidb_ref, bf16[512,512]{1,0:T(8,128)(2,1)} %get-tuple-element.210.gba_ref, ...), custom_call_target="tpu_custom_call" | custom-call | flops 6600000000 | bytes 12000000 | tf_op jit(solution)/shard_map/grads_reduce/pallas_call | solution.py:548
  135.4 5.8 %grads_feature.1 = (bf16[2,2,2,2,64,512]{5,4,3,2,1,0:T(8,128)(2,1)S(1)}, bf16[2,2,2,2,64,512]{5,4,3,2,1,0:T(8,128)(2,1)S(1)}) custom-call(s32[8]{0:T(128)S(1)} %stack.56.me_ref, bf16[512,512]{1,0:T(8,128)(2,1)} %get-tuple-element.220.acta_ref, bf16[512,512]{1,0:T(8,128)(2,1)} %get-tuple-element.221.actb_ref, bf16[512,1536]{1,0:T(8,128)(2,1)} %get-tuple-element.222.dqa_ref, ...), custom_call_target="tpu_custom_call" | custom-call | flops 6600000000 | bytes 12000000 | tf_op jit(solution)/shard_map/grads_feature/pallas_call | solution.py:548
  142.9 9.5 %backward_one.1 = (bf16[4,256,512]{2,1,0:T(8,128)(2,1)}, bf16[4,256,512]{2,1,0:T(8,128)(2,1)}, bf16[4,64,1024]{2,1,0:T(8,128)(2,1)S(1)}, bf16[4,64,512]{2,1,0:T(8,128)(2,1)S(1)}, f32[8,512]{1,0:T(8,128)S(1)}) custom-call(bf16[4,4,4,8,512]{4,3,2,1,0:T(8,128)(2,1)} %bitcast.348, bf16[4,4,4,8,512]{4,3,2,1,0:T(8,128)(2,1)} %bitcast.35.gb_ref, ...), custom_call_target="tpu_custom_call" | custom-call | flops 11000000512 | bytes 20000000 | tf_op jit(solution)/shard_map/backward_one/pallas_call | solution.py:548
  152.8 1.9 collective-permute-start.10
  155.0 1.5 collective-permute-start.9
  156.9 1.5 collective-permute-start.8
  158.4 2.7 %collective-permute-start.11 = (bf16[4,64,512]{2,1,0:T(8,128)(2,1)S(1)}, bf16[4,64,512]{2,1,0:T(8,128)(2,1)S(1)}, u32[]{:S(2)}, u32[]{:S(2)}) collective-permute-start(bf16[4,64,512]{2,1,0:T(8,128)(2,1)S(1)} %get-tuple-element.250.term_ref), channel_id=1, source_target_pairs={{0,16},{16,0},{1,17},{17,1},{2,18},{18,2},{3,19},{19,3},{4,20},{20... | collective-permute-start | bytes 786440 | tf_op jit(solution)/shard_map/ppermute | solution.py:563
  161.1 4.1 %grads_sample.1 = (bf16[2,2,2,2,32,512]{5,4,3,2,1,0:T(8,128)(2,1)S(1)}, bf16[2,2,2,2,32,512]{5,4,3,2,1,0:T(8,128)(2,1)S(1)}, bf16[2,2,2,2,32,512]{5,4,3,2,1,0:T(...) custom-call(s32[8]{0:T(128)S(1)} %stack.56.me_ref, bf16[1024,512]{1,0:T(8,128)(2,1)} %bitcast.362, ...), custom_call_target="tpu_custom_call" | custom-call | flops 3300000000 | bytes 6000000 | tf_op jit(solution)/shard_map/grads_sample/pallas_call | solution.py:548
  165.2 9.8 %collective-permute-done.11.got_ref = bf16[4,64,512]{2,1,0:T(8,128)(2,1)S(1)} collective-permute-done((bf16[4,64,512]{2,1,0:T(8,128)(2,1)S(1)}, bf16[4,64,512]{2,1,0:T(8,128)(2,1)S(1)}, u32[]{:S(2)}, u32[]{:S(2)}) %collective-permute-start.11) | collective-permute-done | bytes 262176 | tf_op jit(solution)/shard_map/ppermute | solution.py:563
  178.0 1.7 collective-permute-start.14
  179.7 5.9 %backward_input.1 = (bf16[4,4,64,512]{3,2,1,0:T(8,128)(2,1)}, f32[8,512]{1,0:T(8,128)S(1)}) custom-call(s32[8]{0:T(128)S(1)} %stack.56.me_ref, bf16[4,256,512]{2,1,0:T(8,128)(2,1)} %get-tuple-element.265.gb1_ref, bf16[4,4,64,512]{3,2,1,0:T(8,128)(2,1)} %copy-done.21, bf16[4,256,512]{2,1,0:T(8,128)(2,1)} %get-tuple-element.252.dq_ref, ...), custom_call_target="tpu_custom_call" | custom-call | flops 3300000000 | bytes 6000000 | tf_op jit(solution)/shard_map/backward_input/pallas_call | solution.py:548
  186.2 3.0 %collective-permute-done.14 = bf16[2,2,64,512]{3,2,1,0:T(8,128)(2,1)S(1)} collective-permute-done((bf16[2,2,64,512]{3,2,1,0:T(8,128)(2,1)S(1)}, bf16[2,2,64,512]{3,2,1,0:T(8,128)(2,1)S(1)}, u32[]{:S(2)}, u32[]{:S(2)}) %collective-permute-start.14) | collective-permute-done | bytes 262176 | tf_op jit(solution)/shard_map/ppermute | solution.py:563
  190.1 5.0 %all-to-all-start.5 = ((bf16[4,4,64,512]{3,2,1,0:T(8,128)(2,1)}), bf16[4,4,64,512]{3,2,1,0:T(8,128)(2,1)S(1)}, u32[]{:S(2)}, u32[]{:S(2)}) async-start(bf16[4,4,64,512]{3,2,1,0:T(8,128)(2,1)} %get-tuple-element.276), calls=%async_computation.5 | async-start | bytes 2097152 | tf_op jit(solution)/shard_map/all_to_all | solution.py:788
  197.7 1.8 fusion.18
  199.5 2.0 collective-permute-start.21
  205.4 6.6 %collective-permute-done.22.b2.b3 = bf16[2,256,512]{2,1,0:T(8,128)(2,1)S(1)} collective-permute-done((bf16[2,256,512]{2,1,0:T(8,128)(2,1)S(1)}, bf16[2,256,512]{2,1,0:T(8,128)(2,1)S(1)}, u32[]{:S(2)}, u32[]{:S(2)}) %collective-permute-start.22) | collective-permute-done | bytes 524320 | tf_op jit(solution)/shard_map/ppermute | solution.py:563
  212.0 2.0 collective-permute-start.19
  214.6 2.4 collective-permute-done.19
  217.0 2.4 collective-permute-done.17
  220.4 2.7 turn_out.1
  223.1 5.0 %all-to-all-start.6 = ((f32[8,1,1088]{2,1,0:T(1,128)}), f32[8,1,1088]{2,1,0:T(1,128)S(1)}, u32[]{:S(2)}, u32[]{:S(2)}) async-start(f32[8,1,1088]{2,1,0:T(1,128)} %copy.55), calls=%async_computation.6 | async-start | bytes 73728 | tf_op jit(solution)/shard_map/all_to_all | solution.py:793
  228.9 3.0 %collective-permute-start.27 = (bf16[64,512]{1,0:T(8,128)(2,1)S(1)}, bf16[64,512]{1,0:T(8,128)(2,1)S(1)}, u32[]{:S(2)}, u32[]{:S(2)}) collective-permute-start(bf16[64,512]{1,0:T(8,128)(2,1)S(1)} %fusion.47), channel_id=1, source_target_pairs={{0,16},{16,0},{1,17},{17,1},{2,18},{18,2},{3,19},{19,3},{4,20},{20... | collective-permute-start | bytes 196616 | tf_op jit(solution)/shard_map/ppermute | solution.py:563
  232.9 3.0 %collective-permute-start.25 = (bf16[64,512]{1,0:T(8,128)(2,1)S(1)}, bf16[64,512]{1,0:T(8,128)(2,1)S(1)}, u32[]{:S(2)}, u32[]{:S(2)}) collective-permute-start(bf16[64,512]{1,0:T(8,128)(2,1)S(1)} %fusion.45), channel_id=1, source_target_pairs={{0,16},{16,0},{1,17},{17,1},{2,18},{18,2},{3,19},{19,3},{4,20},{20... | collective-permute-start | bytes 196616 | tf_op jit(solution)/shard_map/ppermute | solution.py:563
  235.9 1.5 collective-permute-start.24
  238.1 2.2 place.1
  240.9 1.6 collective-permute-done.23
  244.5 1.5 collective-permute-start.30
  246.0 1.5 collective-permute-start.28
  247.5 1.5 collective-permute-start.29
  248.9 8.3 %all-gather = bf16[768,512]{1,0:T(8,128)(2,1)S(1)} all-gather(bf16[192,512]{1,0:T(8,128)(2,1)S(1)} %pad_maximum_fusion.4), channel_id=2, replica_groups=mesh['half'=2,'quad'=4,'feat'=4] {'feat'}, dimensions={0}, use_global_device_ids=true | all-gather | bytes 983040 | tf_op jit(solution)/shard_map/all_gather | solution.py:810
  257.5 6.0 %all-gather.1 = bf16[288,512]{1,0:T(8,128)(2,1)S(1)} all-gather(bf16[72,512]{1,0:T(8,128)(2,1)S(1)} %pad_maximum_fusion.5), channel_id=3, replica_groups=mesh['half'=2,'quad'=4,'feat'=4] {'feat'}, dimensions={0}, use_global_device_ids=true | all-gather | bytes 368640 | tf_op jit(solution)/shard_map/all_gather | solution.py:816
  (218 shorter events, 36.7 us)
Async XLA Ops:
  3.8 5.4 %collective-permute-start = (bf16[4,256,512]{2,1,0:T(8,128)(2,1)S(1)}, bf16[4,256,512]{2,1,0:T(8,128)(2,1)}, u32[]{:S(2)}, u32[]{:S(2)}) collective-permute-start(bf16[4,256,512]{2,1,0:T(8,128)(2,1)S(1)} %pad_maximum_fusion), channel_id=1, source_target_pairs={{0,1},{1,0},{2,3},{3,2},{4,5},{5,4},{6,7},{7,6},{8,9},{9,8},{10,11... | collective-permute-start | bytes 3145736 | tf_op jit(solution)/shard_map/ppermute | solution.py:563
  4.3 20.0 %all-to-all-start = ((bf16[4,4,64,512]{3,2,1,0:T(8,128)(2,1)}), bf16[4,4,64,512]{3,2,1,0:T(8,128)(2,1)S(1)}, u32[]{:S(2)}, u32[]{:S(2)}) async-start(bf16[4,4,64,512]{3,2,1,0:T(8,128)(2,1)} %bitcast.10), calls=%async_computation | async-start | bytes 2097152 | tf_op jit(solution)/shard_map/all_to_all | solution.py:621
  9.1 20.7 %copy-start.5 = (f32[1024]{0:T(1024)S(1)}, f32[1024]{0:T(1024)}, u32[]{:S(2)}) copy-start(f32[1024]{0:T(1024)} %param.28) | copy-start | bytes 12292
  9.1 20.7 %copy-start.7 = (f32[512]{0:T(512)S(1)}, f32[512]{0:T(512)}, u32[]{:S(2)}) copy-start(f32[512]{0:T(512)} %param.26) | copy-start | bytes 6148
  9.1 20.7 %copy-start.15 = (f32[512]{0:T(512)S(1)}, f32[512]{0:T(512)}, u32[]{:S(2)}) copy-start(f32[512]{0:T(512)} %param.25) | copy-start | bytes 6148
  10.2 14.1 %collective-permute-start.1 = (bf16[2,256,512]{2,1,0:T(8,128)(2,1)S(1)}, bf16[2,256,512]{2,1,0:T(8,128)(2,1)S(1)}, u32[]{:S(2)}, u32[]{:S(2)}) collective-permute-start(bf16[2,256,512]{2,1,0:T(8,128)(2,1)S(1)} %pad_maximum_fusion.1), channel_id=1, source_target_pairs={{0,2},{1,3},{2,0},{3,1},{4,6},{5,7},{6,4},{7,5},{8,10},{9,11},{10,... | collective-permute-start | bytes 1572872 | tf_op jit(solution)/shard_map/ppermute | solution.py:563
  25.5 15.6 %collective-permute-start.2 = (bf16[2,256,512]{2,1,0:T(8,128)(2,1)S(1)}, bf16[2,256,512]{2,1,0:T(8,128)(2,1)S(1)}, u32[]{:S(2)}, u32[]{:S(2)}) collective-permute-start(bf16[2,256,512]{2,1,0:T(8,128)(2,1)S(1)} %pad_maximum_fusion.2), channel_id=1, source_target_pairs={{0,2},{1,3},{2,0},{3,1},{4,6},{5,7},{6,4},{7,5},{8,10},{9,11},{10,... | collective-permute-start | bytes 1572872 | tf_op jit(solution)/shard_map/ppermute | solution.py:563
  27.1 13.9 %collective-permute-start.3 = (bf16[4,64,512]{2,1,0:T(8,128)(2,1)S(1)}, bf16[4,64,512]{2,1,0:T(8,128)(2,1)S(1)}, u32[]{:S(2)}, u32[]{:S(2)}) collective-permute-start(bf16[4,64,512]{2,1,0:T(8,128)(2,1)S(1)} %dynamic-slice_bitcast_fusion.own_ref), channel_id=1, source_target_pairs={{0,16},{16,0},{1,17},{17,1},{2,18},{18,2},{3,19},{19,3},{4,20},{20... | collective-permute-start | bytes 786440 | tf_op jit(solution)/shard_map/ppermute | solution.py:563
  52.8 38.9 %copy-start.20 = (bf16[4,64,512]{2,1,0:T(8,128)(2,1)}, bf16[4,64,512]{2,1,0:T(8,128)(2,1)S(1)}, u32[]{:S(2)}) copy-start(bf16[4,64,512]{2,1,0:T(8,128)(2,1)S(1)} %get-tuple-element.238.v_ref) | copy-start | bytes 786436
  52.8 18.1 %copy-start.8 = (f32[512]{0:T(512)S(1)}, f32[512]{0:T(512)}, u32[]{:S(2)}) copy-start(f32[512]{0:T(512)} %param.30) | copy-start | bytes 6148
  52.8 18.1 %copy-start.9 = (f32[512]{0:T(512)S(1)}, f32[512]{0:T(512)}, u32[]{:S(2)}) copy-start(f32[512]{0:T(512)} %param.31) | copy-start | bytes 6148
  52.8 18.1 %copy-start.10 = (f32[512]{0:T(512)S(1)}, f32[512]{0:T(512)}, u32[]{:S(2)}) copy-start(f32[512]{0:T(512)} %param.32) | copy-start | bytes 6148
  52.8 18.1 %copy-start.11 = (f32[512]{0:T(512)S(1)}, f32[512]{0:T(512)}, u32[]{:S(2)}) copy-start(f32[512]{0:T(512)} %param.36) | copy-start | bytes 6148
  52.8 18.1 %copy-start.12 = (f32[512]{0:T(512)S(1)}, f32[512]{0:T(512)}, u32[]{:S(2)}) copy-start(f32[512]{0:T(512)} %param.37) | copy-start | bytes 6148
  52.9 14.2 %all-to-all-start.1 = ((bf16[16,4,8,512]{3,2,1,0:T(8,128)(2,1)}), bf16[16,4,8,512]{3,2,1,0:T(8,128)(2,1)S(1)}, u32[]{:S(2)}, u32[]{:S(2)}) async-start(bf16[16,4,8,512]{3,2,1,0:T(8,128)(2,1)} %bitcast.344), calls=%async_computation.1 | async-start | bytes 1048576 | tf_op jit(solution)/shard_map/all_to_all | solution.py:651
  67.1 24.6 %all-to-all-start.2 = ((bf16[16,4,8,512]{3,2,1,0:T(8,128)(2,1)}), bf16[16,4,8,512]{3,2,1,0:T(8,128)(2,1)S(1)}, u32[]{:S(2)}, u32[]{:S(2)}) async-start(bf16[16,4,8,512]{3,2,1,0:T(8,128)(2,1)} %bitcast.346), calls=%async_computation.2 | async-start | bytes 1048576 | tf_op jit(solution)/shard_map/all_to_all | solution.py:651
  91.7 25.6 %all-to-all-start.3 = ((bf16[16,4,8,512]{3,2,1,0:T(8,128)(2,1)}), bf16[16,4,8,512]{3,2,1,0:T(8,128)(2,1)S(1)}, u32[]{:S(2)}, u32[]{:S(2)}) async-start(bf16[16,4,8,512]{3,2,1,0:T(8,128)(2,1)} %bitcast.352), calls=%async_computation.3 | async-start | bytes 1048576 | tf_op jit(solution)/shard_map/all_to_all | solution.py:651
  117.3 24.9 %all-to-all-start.4 = ((bf16[16,4,8,512]{3,2,1,0:T(8,128)(2,1)}), bf16[16,4,8,512]{3,2,1,0:T(8,128)(2,1)}, u32[]{:S(2)}, u32[]{:S(2)}) async-start(bf16[16,4,8,512]{3,2,1,0:T(8,128)(2,1)} %bitcast.350), calls=%async_computation.4 | async-start | bytes 1048576 | tf_op jit(solution)/shard_map/all_to_all | solution.py:651
  122.5 19.7 %collective-permute-start.4 = (bf16[2,256,512]{2,1,0:T(8,128)(2,1)}, bf16[2,256,512]{2,1,0:T(8,128)(2,1)}, u32[]{:S(2)}, u32[]{:S(2)}) collective-permute-start(bf16[2,256,512]{2,1,0:T(8,128)(2,1)} %get-tuple-element.207), channel_id=1, source_target_pairs={{0,1},{1,0},{2,3},{3,2},{4,5},{5,4},{6,7},{7,6},{8,9},{9,8},{10,11... | collective-permute-start | bytes 1572872 | tf_op jit(solution)/shard_map/ppermute | solution.py:563
  142.2 10.2 %collective-permute-start.5 = (bf16[2,2,2,2,64,512]{5,4,3,2,1,0:T(8,128)(2,1)}, bf16[2,2,2,2,64,512]{5,4,3,2,1,0:T(8,128)(2,1)S(1)}, u32[]{:S(2)}, u32[]{:S(2)}) collective-permute-start(bf16[2,2,2,2,64,512]{5,4,3,2,1,0:T(8,128)(2,1)} %copy-done.2), channel_id=1, source_target_pairs={{0,1},{1,0},{2,3},{3,2},{4,5},{5,4},{6,7},{7,6},{8,9},{9,8},{10,11... | collective-permute-start | bytes 3145736 | tf_op jit(solution)/shard_map/ppermute | solution.py:563
  142.4 10.0 %collective-permute-start.6 = (bf16[2,2,2,2,64,512]{5,4,3,2,1,0:T(8,128)(2,1)}, bf16[2,2,2,2,64,512]{5,4,3,2,1,0:T(8,128)(2,1)S(1)}, u32[]{:S(2)}, u32[]{:S(2)}) collective-permute-start(bf16[2,2,2,2,64,512]{5,4,3,2,1,0:T(8,128)(2,1)} %copy-done), channel_id=1, source_target_pairs={{0,1},{1,0},{2,3},{3,2},{4,5},{5,4},{6,7},{7,6},{8,9},{9,8},{10,11... | collective-permute-start | bytes 3145736 | tf_op jit(solution)/shard_map/ppermute | solution.py:563
  142.8 9.7 %collective-permute-start.7 = (bf16[2,2,2,2,64,512]{5,4,3,2,1,0:T(8,128)(2,1)}, bf16[2,2,2,2,64,512]{5,4,3,2,1,0:T(8,128)(2,1)S(1)}, u32[]{:S(2)}, u32[]{:S(2)}) collective-permute-start(bf16[2,2,2,2,64,512]{5,4,3,2,1,0:T(8,128)(2,1)} %copy-done.1), channel_id=1, source_target_pairs={{0,1},{1,0},{2,3},{3,2},{4,5},{5,4},{6,7},{7,6},{8,9},{9,8},{10,11... | collective-permute-start | bytes 3145736 | tf_op jit(solution)/shard_map/ppermute | solution.py:563
  152.8 22.2 %collective-permute-start.10 = (bf16[2,2,2,64,512]{4,3,2,1,0:T(8,128)(2,1)S(1)}, bf16[2,2,2,64,512]{4,3,2,1,0:T(8,128)(2,1)S(1)}, u32[]{:S(2)}, u32[]{:S(2)}) collective-permute-start(bf16[2,2,2,64,512]{4,3,2,1,0:T(8,128)(2,1)S(1)} %get-tuple-element.307), channel_id=1, source_target_pairs={{0,2},{1,3},{2,0},{3,1},{4,6},{5,7},{6,4},{7,5},{8,10},{9,11},{10,... | collective-permute-start | bytes 1572872 | tf_op jit(solution)/shard_map/ppermute | solution.py:563
  155.0 20.0 %collective-permute-start.9 = (bf16[2,2,2,64,512]{4,3,2,1,0:T(8,128)(2,1)S(1)}, bf16[2,2,2,64,512]{4,3,2,1,0:T(8,128)(2,1)S(1)}, u32[]{:S(2)}, u32[]{:S(2)}) collective-permute-start(bf16[2,2,2,64,512]{4,3,2,1,0:T(8,128)(2,1)S(1)} %get-tuple-element.309), channel_id=1, source_target_pairs={{0,4},{4,0},{8,12},{12,8},{1,5},{5,1},{9,13},{13,9},{2,6},{6,2},{1... | collective-permute-start | bytes 1572872 | tf_op jit(solution)/shard_map/ppermute | solution.py:563
  156.9 19.1 %collective-permute-start.8 = (bf16[2,2,2,64,512]{4,3,2,1,0:T(8,128)(2,1)S(1)}, bf16[2,2,2,64,512]{4,3,2,1,0:T(8,128)(2,1)S(1)}, u32[]{:S(2)}, u32[]{:S(2)}) collective-permute-start(bf16[2,2,2,64,512]{4,3,2,1,0:T(8,128)(2,1)S(1)} %get-tuple-element.311), channel_id=1, source_target_pairs={{0,8},{4,12},{8,0},{12,4},{1,9},{5,13},{9,1},{13,5},{2,10},{6,14},... | collective-permute-start | bytes 1572872 | tf_op jit(solution)/shard_map/ppermute | solution.py:563
  158.4 16.6 %collective-permute-start.11 = (bf16[4,64,512]{2,1,0:T(8,128)(2,1)S(1)}, bf16[4,64,512]{2,1,0:T(8,128)(2,1)S(1)}, u32[]{:S(2)}, u32[]{:S(2)}) collective-permute-start(bf16[4,64,512]{2,1,0:T(8,128)(2,1)S(1)} %get-tuple-element.250.term_ref), channel_id=1, source_target_pairs={{0,16},{16,0},{1,17},{17,1},{2,18},{18,2},{3,19},{19,3},{4,20},{20... | collective-permute-start | bytes 786440 | tf_op jit(solution)/shard_map/ppermute | solution.py:563
  176.1 9.5 %collective-permute-start.16 = (bf16[2,2,64,512]{3,2,1,0:T(8,128)(2,1)S(1)}, bf16[2,2,64,512]{3,2,1,0:T(8,128)(2,1)S(1)}, u32[]{:S(2)}, u32[]{:S(2)}) collective-permute-start(bf16[2,2,64,512]{3,2,1,0:T(8,128)(2,1)S(1)} %get-tuple-element.315), channel_id=1, source_target_pairs={{0,4},{4,0},{8,12},{12,8},{1,5},{5,1},{9,13},{13,9},{2,6},{6,2},{1... | collective-permute-start | bytes 786440 | tf_op jit(solution)/shard_map/ppermute | solution.py:563
  176.9 9.3 %collective-permute-start.15 = (bf16[2,2,64,512]{3,2,1,0:T(8,128)(2,1)S(1)}, bf16[2,2,64,512]{3,2,1,0:T(8,128)(2,1)S(1)}, u32[]{:S(2)}, u32[]{:S(2)}) collective-permute-start(bf16[2,2,64,512]{3,2,1,0:T(8,128)(2,1)S(1)} %get-tuple-element.317), channel_id=1, source_target_pairs={{0,2},{1,3},{2,0},{3,1},{4,6},{5,7},{6,4},{7,5},{8,10},{9,11},{10,... | collective-permute-start | bytes 786440 | tf_op jit(solution)/shard_map/ppermute | solution.py:563
  177.3 11.9 %collective-permute-start.12 = (bf16[2,2,2,2,32,512]{5,4,3,2,1,0:T(8,128)(2,1)S(1)}, bf16[2,2,2,2,32,512]{5,4,3,2,1,0:T(8,128)(2,1)S(1)}, u32[]{:S(2)}, u32[]{:S(2)}) collective-permute-start(bf16[2,2,2,2,32,512]{5,4,3,2,1,0:T(8,128)(2,1)S(1)} %get-tuple-element.260), channel_id=1, source_target_pairs={{0,1},{1,0},{2,3},{3,2},{4,5},{5,4},{6,7},{7,6},{8,9},{9,8},{10,11... | collective-permute-start | bytes 1572872 | tf_op jit(solution)/shard_map/ppermute | solution.py:563
  177.3 11.9 %collective-permute-start.13 = (bf16[2,2,2,2,32,512]{5,4,3,2,1,0:T(8,128)(2,1)S(1)}, bf16[2,2,2,2,32,512]{5,4,3,2,1,0:T(8,128)(2,1)S(1)}, u32[]{:S(2)}, u32[]{:S(2)}) collective-permute-start(bf16[2,2,2,2,32,512]{5,4,3,2,1,0:T(8,128)(2,1)S(1)} %get-tuple-element.261), channel_id=1, source_target_pairs={{0,1},{1,0},{2,3},{3,2},{4,5},{5,4},{6,7},{7,6},{8,9},{9,8},{10,11... | collective-permute-start | bytes 1572872 | tf_op jit(solution)/shard_map/ppermute | solution.py:563
  178.0 11.2 %collective-permute-start.14 = (bf16[2,2,64,512]{3,2,1,0:T(8,128)(2,1)S(1)}, bf16[2,2,64,512]{3,2,1,0:T(8,128)(2,1)S(1)}, u32[]{:S(2)}, u32[]{:S(2)}) collective-permute-start(bf16[2,2,64,512]{3,2,1,0:T(8,128)(2,1)S(1)} %get-tuple-element.319), channel_id=1, source_target_pairs={{0,2},{1,3},{2,0},{3,1},{4,6},{5,7},{6,4},{7,5},{8,10},{9,11},{10,... | collective-permute-start | bytes 786440 | tf_op jit(solution)/shard_map/ppermute | solution.py:563
  190.1 29.3 %all-to-all-start.5 = ((bf16[4,4,64,512]{3,2,1,0:T(8,128)(2,1)}), bf16[4,4,64,512]{3,2,1,0:T(8,128)(2,1)S(1)}, u32[]{:S(2)}, u32[]{:S(2)}) async-start(bf16[4,4,64,512]{3,2,1,0:T(8,128)(2,1)} %get-tuple-element.276), calls=%async_computation.5 | async-start | bytes 2097152 | tf_op jit(solution)/shard_map/all_to_all | solution.py:788
  197.1 14.9 %collective-permute-start.22 = (bf16[2,256,512]{2,1,0:T(8,128)(2,1)S(1)}, bf16[2,256,512]{2,1,0:T(8,128)(2,1)S(1)}, u32[]{:S(2)}, u32[]{:S(2)}) collective-permute-start(bf16[2,256,512]{2,1,0:T(8,128)(2,1)S(1)} %pad_maximum_fusion.3), channel_id=1, source_target_pairs={{0,2},{1,3},{2,0},{3,1},{4,6},{5,7},{6,4},{7,5},{8,10},{9,11},{10,... | collective-permute-start | bytes 1572872 | tf_op jit(solution)/shard_map/ppermute | solution.py:563
  199.5 15.1 %collective-permute-start.21 = (bf16[2,64,512]{2,1,0:T(8,128)(2,1)}, bf16[2,64,512]{2,1,0:T(8,128)(2,1)}, u32[]{:S(2)}, u32[]{:S(2)}) collective-permute-start(bf16[2,64,512]{2,1,0:T(8,128)(2,1)} %get-tuple-element.341), channel_id=1, source_target_pairs={{0,8},{4,12},{8,0},{12,4},{1,9},{5,13},{9,1},{13,5},{2,10},{6,14},... | collective-permute-start | bytes 393224 | tf_op jit(solution)/shard_map/ppermute | solution.py:563
  202.3 12.3 %collective-permute-start.20 = (bf16[2,64,512]{2,1,0:T(8,128)(2,1)}, bf16[2,64,512]{2,1,0:T(8,128)(2,1)}, u32[]{:S(2)}, u32[]{:S(2)}) collective-permute-start(bf16[2,64,512]{2,1,0:T(8,128)(2,1)} %get-tuple-element.343), channel_id=1, source_target_pairs={{0,8},{4,12},{8,0},{12,4},{1,9},{5,13},{9,1},{13,5},{2,10},{6,14},... | collective-permute-start | bytes 393224 | tf_op jit(solution)/shard_map/ppermute | solution.py:563
  203.1 13.9 %collective-permute-start.18 = (bf16[2,2,2,32,512]{4,3,2,1,0:T(8,128)(2,1)}, bf16[2,2,2,32,512]{4,3,2,1,0:T(8,128)(2,1)S(1)}, u32[]{:S(2)}, u32[]{:S(2)}) collective-permute-start(bf16[2,2,2,32,512]{4,3,2,1,0:T(8,128)(2,1)} %get-tuple-element.313), channel_id=1, source_target_pairs={{0,2},{1,3},{2,0},{3,1},{4,6},{5,7},{6,4},{7,5},{8,10},{9,11},{10,... | collective-permute-start | bytes 786440 | tf_op jit(solution)/shard_map/ppermute | solution.py:563
  204.7 14.7 %collective-permute-start.17 = (bf16[2,2,2,32,512]{4,3,2,1,0:T(8,128)(2,1)S(1)}, bf16[2,2,2,32,512]{4,3,2,1,0:T(8,128)(2,1)S(1)}, u32[]{:S(2)}, u32[]{:S(2)}) collective-permute-start(bf16[2,2,2,32,512]{4,3,2,1,0:T(8,128)(2,1)S(1)} %get-tuple-element.320), channel_id=1, source_target_pairs={{0,2},{1,3},{2,0},{3,1},{4,6},{5,7},{6,4},{7,5},{8,10},{9,11},{10,... | collective-permute-start | bytes 786440 | tf_op jit(solution)/shard_map/ppermute | solution.py:563
  212.0 5.0 %collective-permute-start.19 = (bf16[2,64,512]{2,1,0:T(8,128)(2,1)S(1)}, bf16[2,64,512]{2,1,0:T(8,128)(2,1)S(1)}, u32[]{:S(2)}, u32[]{:S(2)}) collective-permute-start(bf16[2,64,512]{2,1,0:T(8,128)(2,1)S(1)} %get-tuple-element.345), channel_id=1, source_target_pairs={{0,4},{4,0},{8,12},{12,8},{1,5},{5,1},{9,13},{13,9},{2,6},{6,2},{1... | collective-permute-start | bytes 393224 | tf_op jit(solution)/shard_map/ppermute | solution.py:563
  217.0 18.9 %copy-start.38 = (bf16[2,2,2,32,512]{4,3,2,1,0:T(8,128)(2,1)}, bf16[2,2,2,32,512]{4,3,2,1,0:T(8,128)(2,1)S(1)}, u32[]{:S(2)}) copy-start(bf16[2,2,2,32,512]{4,3,2,1,0:T(8,128)(2,1)S(1)} %collective-permute-done.18) | copy-start | bytes 786436
  223.1 17.2 %all-to-all-start.6 = ((f32[8,1,1088]{2,1,0:T(1,128)}), f32[8,1,1088]{2,1,0:T(1,128)S(1)}, u32[]{:S(2)}, u32[]{:S(2)}) async-start(f32[8,1,1088]{2,1,0:T(1,128)} %copy.55), calls=%async_computation.6 | async-start | bytes 73728 | tf_op jit(solution)/shard_map/all_to_all | solution.py:793
  228.9 11.4 %collective-permute-start.27 = (bf16[64,512]{1,0:T(8,128)(2,1)S(1)}, bf16[64,512]{1,0:T(8,128)(2,1)S(1)}, u32[]{:S(2)}, u32[]{:S(2)}) collective-permute-start(bf16[64,512]{1,0:T(8,128)(2,1)S(1)} %fusion.47), channel_id=1, source_target_pairs={{0,16},{16,0},{1,17},{17,1},{2,18},{18,2},{3,19},{19,3},{4,20},{20... | collective-permute-start | bytes 196616 | tf_op jit(solution)/shard_map/ppermute | solution.py:563
  232.8 7.6 %collective-permute-start.26 = (bf16[64,512]{1,0:T(8,128)(2,1)S(1)}, bf16[64,512]{1,0:T(8,128)(2,1)S(1)}, u32[]{:S(2)}, u32[]{:S(2)}) collective-permute-start(bf16[64,512]{1,0:T(8,128)(2,1)S(1)} %fusion.46), channel_id=1, source_target_pairs={{0,16},{16,0},{1,17},{17,1},{2,18},{18,2},{3,19},{19,3},{4,20},{20... | collective-permute-start | bytes 196616 | tf_op jit(solution)/shard_map/ppermute | solution.py:563
  232.9 7.5 %collective-permute-start.25 = (bf16[64,512]{1,0:T(8,128)(2,1)S(1)}, bf16[64,512]{1,0:T(8,128)(2,1)S(1)}, u32[]{:S(2)}, u32[]{:S(2)}) collective-permute-start(bf16[64,512]{1,0:T(8,128)(2,1)S(1)} %fusion.45), channel_id=1, source_target_pairs={{0,16},{16,0},{1,17},{17,1},{2,18},{18,2},{3,19},{19,3},{4,20},{20... | collective-permute-start | bytes 196616 | tf_op jit(solution)/shard_map/ppermute | solution.py:563
  235.9 5.0 %collective-permute-start.24 = (bf16[2,2,32,512]{3,2,1,0:T(8,128)(2,1)S(1)}, bf16[2,2,32,512]{3,2,1,0:T(8,128)(2,1)S(1)}, u32[]{:S(2)}, u32[]{:S(2)}) collective-permute-start(bf16[2,2,32,512]{3,2,1,0:T(8,128)(2,1)S(1)} %fusion.30), channel_id=1, source_target_pairs={{0,4},{4,0},{8,12},{12,8},{1,5},{5,1},{9,13},{13,9},{2,6},{6,2},{1... | collective-permute-start | bytes 393224 | tf_op jit(solution)/shard_map/ppermute | solution.py:563
  237.5 5.0 %collective-permute-start.23 = (bf16[2,2,32,512]{3,2,1,0:T(8,128)(2,1)S(1)}, bf16[2,2,32,512]{3,2,1,0:T(8,128)(2,1)S(1)}, u32[]{:S(2)}, u32[]{:S(2)}) collective-permute-start(bf16[2,2,32,512]{3,2,1,0:T(8,128)(2,1)S(1)} %fusion.26), channel_id=1, source_target_pairs={{0,4},{4,0},{8,12},{12,8},{1,5},{5,1},{9,13},{13,9},{2,6},{6,2},{1... | collective-permute-start | bytes 393224 | tf_op jit(solution)/shard_map/ppermute | solution.py:563
  244.5 12.8 %collective-permute-start.30 = (bf16[64,512]{1,0:T(8,128)(2,1)S(1)}, bf16[64,512]{1,0:T(8,128)(2,1)S(1)}, u32[]{:S(2)}, u32[]{:S(2)}) collective-permute-start(bf16[64,512]{1,0:T(8,128)(2,1)S(1)} %get-tuple-element.350), channel_id=1, source_target_pairs={{0,24},{4,28},{8,16},{12,20},{16,8},{20,12},{24,0},{28,4},{1,25},{... | collective-permute-start | bytes 196616 | tf_op jit(solution)/shard_map/ppermute | solution.py:807
  246.0 11.3 %collective-permute-start.28 = (bf16[64,512]{1,0:T(8,128)(2,1)S(1)}, bf16[64,512]{1,0:T(8,128)(2,1)S(1)}, u32[]{:S(2)}, u32[]{:S(2)}) collective-permute-start(bf16[64,512]{1,0:T(8,128)(2,1)S(1)} %get-tuple-element.351), channel_id=1, source_target_pairs={{0,16},{4,20},{8,24},{12,28},{16,0},{20,4},{24,8},{28,12},{1,17},{... | collective-permute-start | bytes 196616 | tf_op jit(solution)/shard_map/ppermute | solution.py:807
  247.5 9.8 %collective-permute-start.29 = (bf16[64,512]{1,0:T(8,128)(2,1)S(1)}, bf16[64,512]{1,0:T(8,128)(2,1)S(1)}, u32[]{:S(2)}, u32[]{:S(2)}) collective-permute-start(bf16[64,512]{1,0:T(8,128)(2,1)S(1)} %get-tuple-element.352), channel_id=1, source_target_pairs={{0,8},{4,12},{8,0},{12,4},{16,24},{20,28},{24,16},{28,20},{1,9},{5... | collective-permute-start | bytes 196616 | tf_op jit(solution)/shard_map/ppermute | solution.py:807
  (37 other events, 218.8 us)
where the time goes:
time: 272 us; the launch traced here: 270 us
  Pallas kernels  98.6 us (36%)
  starting transfers between devices  70.1 us (26%)
  waiting for transfers between devices  52 us (19%)
  other arithmetic  15.6 us (6%)
  blocking collectives  14.4 us (5%)
  local copies, waits for them, and re-layouts  14 us (5%)
  between operations  5.41 us (2%)
    pallas_call x12, Pallas kernels, whole(): pl.pallas_call(kernel, grid=(steps,), out_shape=outs, in_specs=specs, out...  57.3 us
    ppermute x28, waiting for transfers between devices, shuffle(): return lax.ppermute(value, axis, [(i, i ^ mask) for i in range(size)])  41.6 us
    pallas_call x2, Pallas kernels, run_middle(): pl.pallas_call(middle, grid_spec=pltpu.PrefetchScalarGridSpec(num_scalar_...  41.3 us
    ppermute x28, starting transfers between devices, shuffle(): return lax.ppermute(value, axis, [(i, i ^ mask) for i in range(size)])  33.3 us
    all_to_all x4, starting transfers between devices, exchange(): return lax.all_to_all(value, ('quad', 'feat'), 0, 0).reshape(shape)  17.6 us
    all_to_all x4, waiting for transfers between devices, exchange(): return lax.all_to_all(value, ('quad', 'feat'), 0, 0).reshape(shape)  10.3 us
    convert_element_type x21, other arithmetic, plus(): return (a.astype(F32) + b.astype(F32)).astype(BF)  8.65 us
    all_gather x1, blocking collectives, local_small(): lax.all_gather(jnp.concatenate([chain.keep for chain in chains]), 'feat')  8.33 us
  transfers between devices with their start and end apart: 38, of which 12 were waited for; matrix products, arithmetic and copies ran while one was open for 4% of the time, Pallas kernels for 31%

commit v1 on v0

--- a/solution.py
+++ b/solution.py
@@ -189,19 +189,19 @@
         off1_ref, g2_ref, s2_ref, bf_ref, off2_ref, g3_ref, s3_ref, be_ref, br_ref,
     ) = refs[:18]
     weights_hbm = refs[18:23]
-    refs = refs[-42:]
+    refs = refs[-44:]
     gb1_ref, vec_ref, bias_ref = refs[:3]
-    outs_hbm, kept_hbm = refs[3:6], refs[6:14]
-    wm1_ref, wf_ref, wm2_ref, we_ref, wr_ref = refs[14:19]
-    kept = refs[19:27]
+    outs_hbm, kept_hbm = refs[3:7], refs[7:15]
+    wm1_ref, wf_ref, wm2_ref, we_ref, wr_ref = refs[15:20]
+    kept = refs[20:28]
     a2_ref, dqkv_ref, o2_ref, gb2_ref, a3_ref, gu_ref, hid_ref, gb3_ref = kept
     (
         o_scr, q_scr, k_scr, v_scr, p_scr, e_scr, gs_scr, go_scr, out_scr, back_scr,
-        out0, out2, out13, in_sems, out_sems,
-    ) = refs[27:]
+        out0, out1, out2, out3, in_sems, out_sems,
+    ) = refs[28:]
     loads = [
         pltpu.make_async_copy(source, target, in_sems.at[i])
-        for i, (source, target) in enumerate(zip(weights_hbm, refs[14:19]))
+        for i, (source, target) in enumerate(zip(weights_hbm, refs[15:20]))
     ]
     for load in loads:
         load.start()
@@ -300,11 +300,10 @@
     lax.fori_loop(0, 2048 // WIDE, expand, 0, unroll=EXPAND_UNROLL)
     keep(hid_ref)
     keep(gu_ref)
-    scatter(out_scr[...].astype(BF), out0, out13.at[0], out2, out13.at[1])
+    scatter(out_scr[...].astype(BF), out0, out1, out2, out3)
     rows = pl.ds(pl.multiple_of(me_ref[8] * 128, 128), 128)
-    store(out0, outs_hbm[0].at[rows], 8)
-    store(out2, outs_hbm[1].at[rows], 9)
-    store(out13, outs_hbm[2].at[:, rows], 10)
+    for i, ref in enumerate((out0, out1, out2, out3)):
+        store(ref, outs_hbm[i].at[rows], 8 + i)
     back, cot = back_scr[...], gb3_ref[...]
     vecs = [col_sum(back * unit3), col_sum(back)]
     gr2 = cot.astype(F32) + norm_back(back, unit3, inv3, g3_ref[...])
@@ -354,8 +353,8 @@
 
 
 def backward_one(
-    ga_ref, gb_ref, c_ref, q_ref, k_ref, v_ref, p_ref, w_ref, wm_ref,
-    gb1_ref, dq_ref, dkv_ref, term_ref, vec_ref,
+    ga_ref, gb_ref, x_ref, c_ref, q_ref, k_ref, v_ref, p_ref, w_ref, wm_ref,
+    gb1_ref, a_ref, dq_ref, dkv_ref, term_ref, vec_ref,
     g_scr,
 ):
     masks, masks32 = head_masks(BF), head_masks(F32)
@@ -369,6 +368,11 @@
         go = mm(gb1, wm_ref[...], 1, 1).astype(BF)
         dq, dk, dv = attend_back(q_ref[e], k_ref[e], v_ref[e], p_ref[e], go, masks, masks32)
         dq_ref[e], dkv_ref[e, :, :512], dkv_ref[e, :, 512:] = dq, dk, dv
+        back = mm(dq, w_ref[:, :512], 1, 1)
+        a_ref[e] = back
+        unit, _ = norm_parts(x_ref[:, e].reshape(256, 512).astype(F32))
+        vec_ref[0:1] += col_sum(back * unit)
+        vec_ref[1:2] += col_sum(back)
         vec_ref[2:3] += col_sum(gb1)
         vec_ref[3:4] += col_sum(dq)
 
@@ -377,31 +381,24 @@
     term = mm(dkv, w_ref[:, 512:], 1, 1)
     term_ref[...] = term.astype(BF).reshape(4, 64, 512)
     unit, _ = norm_parts(c_ref[...].reshape(256, 512).astype(F32))
-    vec_ref[0:1], vec_ref[1:2] = col_sum(term * unit), col_sum(term)
+    vec_ref[0:1] += col_sum(term * unit)
+    vec_ref[1:2] += col_sum(term)
     vec_ref[4:5] = col_sum(dkv[:, 512:])
 
 
-def backward_input(
-    me_ref, gb1_ref, x_ref, dq_ref, term_ref, got_ref, vec1_ref, gain_ref, w_ref,
-    grad_ref, vec_ref, a_scr,
-):
+def backward_input(me_ref, gb1_ref, x_ref, a_ref, term_ref, got_ref, gain_ref, grad_ref, a_scr):
     here, quad = me_ref[1] == me_ref[2], me_ref[3]
-    gain = gain_ref[...]
-    vec_ref[...] = vec1_ref[...]
 
     def body(e):
-        back = mm(dq_ref[e], w_ref[:, :512], 1, 1)
         unit, inverse = norm_parts(x_ref[:, e].reshape(256, 512).astype(F32))
-        vec_ref[0:1] += col_sum(back * unit)
-        vec_ref[1:2] += col_sum(back)
-        a_scr[...] = back.reshape(4, 64, 512)
+        a_scr[...] = a_ref[e].reshape(4, 64, 512)
 
         @pl.when(here)
         def _():
             a_scr[quad] += term_ref[e].astype(F32) + got_ref[e].astype(F32)
 
         back = a_scr[...].reshape(256, 512)
-        grad = gb1_ref[e].astype(F32) + norm_back(back, unit, inverse, gain)
+        grad = gb1_ref[e].astype(F32) + norm_back(back, unit, inverse, gain_ref[...])
         grad_ref[:, e] = grad.astype(BF).reshape(4, 64, 512)
 
     each_feature(body)
@@ -439,59 +436,75 @@
     return read
 
 
-def over_tokens(*pairs):
-    return sum(mm(a[...], b[...], 0, 0) for a, b in pairs).astype(BF)
-
-
-def grads_reduce(me_ref, hida_ref, hidb_ref, gba_ref, gbb_ref, keep_ref, send_ref, scr):
-    step = pl.program_id(0)
-    start = pl.multiple_of(step * 512, 512)
-    scr[pl.ds(start, 512)] = over_tokens((hida_ref, gba_ref), (hidb_ref, gbb_ref))
-
-    def read(unit, shard, start, rows):
-        return scr[pl.ds(pl.multiple_of(shard * 256 + unit * 64, 64), 64)]
-
-    @pl.when(step == 3)
-    def _():
-        lay_out(me_ref, read, "zxyw", (keep_ref, send_ref, 0, 64))
-
-
-def grads_expand(me_ref, acta_ref, actb_ref, gua_ref, gub_ref, keep_ref, send_ref, scr):
-    step = pl.program_id(0)
-    scr[step] = over_tokens((acta_ref, gua_ref), (actb_ref, gub_ref))
-
-    @pl.when(step == 3)
-    def _():
-        lay_out(me_ref, read_units(scr), "yxzw", (keep_ref, send_ref, 0, 64))
-
-
-def grads_feature(
-    me_ref, acta_ref, actb_ref, dqa_ref, dqb_ref, oa_ref, ob_ref, gba_ref, gbb_ref,
-    keep_ref, send_ref, scr,
-):
-    step = pl.program_id(0)
-
-    @pl.when(step < 3)
-    def _():
-        scr[step] = over_tokens((acta_ref, dqa_ref), (actb_ref, dqb_ref))
-
-    @pl.when(step == 3)
-    def _():
-        scr[3] = over_tokens((oa_ref, gba_ref), (ob_ref, gbb_ref))
-        lay_out(me_ref, read_units(scr), "xyzw", (keep_ref, send_ref, 0, 64))
+def grads_middle(me_ref, *refs):
+    sources, targets, held, staged = refs[:16], refs[16:22], refs[22:30], refs[30:36]
+    scr, in_sems, out_sems = refs[36:]
+    loads = []
+    for i in range(16):
+        rows = pl.ds((i % 2) * 512, 512)
+        loads.append(
+            pltpu.make_async_copy(sources[i], held[i // 2].at[rows], in_sems.at[i])
+        )
+        loads[-1].start()
+    stores = []
+
+    def wait(*places):
+        for place in places:
+            loads[2 * place].wait()
+            loads[2 * place + 1].wait()
+
+    def put(part, order):
+        lay_out(me_ref, read_units(scr), order, (staged[2 * part], staged[2 * part + 1], 0, 64))
+        for i in (2 * part, 2 * part + 1):
+            stores.append(pltpu.make_async_copy(staged[i], targets[i], out_sems.at[i]))
+            stores[-1].start()
+
+    gb3, hid, act3, gu, act2, dqkv, o2, gb2 = held
+    wait(0, 1)
+
+    def loop(count, body):
+        lax.fori_loop(0, count, lambda n, carry: (body(n), carry)[1], 0)
+
+    block = lambda n: pl.ds(pl.multiple_of(n * 512, 512), 512)
+
+    def from_hidden(n):
+        piece = mm(hid[:, block(n)], gb3[...], 0, 0).astype(BF).reshape(2, 4, 64, 512)
+        for i in range(2):
+            rows = pl.ds(pl.multiple_of((2 * n + i) * 64, 64), 64)
+            for unit in range(4):
+                scr[unit, rows] = piece[i, unit]
+
+    loop(4, from_hidden)
+    put(0, "zxyw")
+    wait(2, 3)
+
+    def from_expand(n):
+        scr[n] = mm(act3[...], gu[:, block(n)], 0, 0).astype(BF)
+
+    loop(4, from_expand)
+    put(1, "yxzw")
+    wait(4, 5, 6, 7)
+
+    def from_feature(n):
+        scr[n] = mm(act2[...], dqkv[:, block(n)], 0, 0).astype(BF)
+
+    loop(3, from_feature)
+    scr[3] = mm(o2[...], gb2[...], 0, 0).astype(BF)
+    put(2, "xyzw")
+    for store in stores:
+        store.wait()
 
 
 def grads_sample(
     me_ref, act_ref, dq_ref, cact_ref, dkv_ref, oa_ref, ga_ref, ob_ref, gb_ref,
-    keepa_ref, senda_ref, keepb_ref, sendb_ref, scr,
+    keep_ref, send_ref, scr,
 ):
     scr[0] = mm(act_ref[...], dq_ref[...], 0, 0).astype(BF)
     scr[1] = mm(cact_ref[...], dkv_ref[:, :512], 0, 0).astype(BF)
     scr[2] = mm(cact_ref[...], dkv_ref[:, 512:], 0, 0).astype(BF)
     total = mm(oa_ref[...], ga_ref[...], 0, 0) + mm(ob_ref[...], gb_ref[...], 0, 0)
     scr[3] = total.astype(BF)
-    lay_out(me_ref, read_units(scr), "xyzw", (keepa_ref, senda_ref, 0, 32))
-    lay_out(me_ref, read_units(scr), "xyzw", (keepb_ref, sendb_ref, 32, 32))
+    lay_out(me_ref, read_units(scr), "xyzw", (keep_ref, send_ref, 0, 64))
 
 
 def spec(shape, index=None):
@@ -637,7 +650,7 @@
     tasks = segment_ids.reshape(8, 64)
     context_tasks = jnp.concatenate([at(tasks, root)] * 4).reshape(1, 256)
     sent = big((4, 4, 4, 8, 512))
-    four = sds((4, 64, 512))
+    four = big((4, 64, 512))
     oa, ob, context, cact, k1, v1, p1 = whole(
         forward_one, "forward_one", 24,
         (sent, sent, four, four, four, four, big((4, 256, 512), F32)), [],
@@ -663,7 +676,7 @@
         own = spec((None, 128, 512), lambda i, m: (m[0], m[8], 0))
         part = lambda n: spec((None, 128, 512), lambda i, m: (n, m[8], 0))
         outs = (sent, sds((8, 512), F32), sds((1, 2048), F32))
-        blocks = ((256, 512), (256, 512), (2, 256, 512))
+        blocks = ((256, 512),) * 4
         kept = tuple((HALF, n) for n in (512, 1536, 512, 512, 512, 2048, 2048, 512))
         still = lambda shape: spec(shape, lambda i, m: (0,) * len(shape))
         far = pl.BlockSpec(memory_space=pl.ANY)
@@ -678,13 +691,13 @@
                 + [own, part(0), part(0), part(1), own, part(1), part(0), part(1)]
                 + [still(r.shape) for r in rows_in]
                 + [far] * (5 + len(earlier)),
-                out_specs=[still(o.shape) for o in outs] + [far] * 11,
+                out_specs=[still(o.shape) for o in outs] + [far] * 12,
                 scratch_shapes=[vmem(w.shape) for w in weights]
                 + [vmem(shape) for shape in kept]
                 + [
                     vmem((4, 128, 512)), rows, rows, rows, rows32, rows32, rows, rows, rows32,
-                    rows32, vmem((128, 512)), vmem((128, 512)), vmem((2, 128, 512)),
-                    pltpu.SemaphoreType.DMA((5,)), pltpu.SemaphoreType.DMA((11,)),
+                    rows32, *(vmem((128, 512)) for _ in range(4)),
+                    pltpu.SemaphoreType.DMA((5,)), pltpu.SemaphoreType.DMA((12,)),
                 ],
             ),
             out_shape=outs + tuple(big(shape) for shape in blocks + kept),
@@ -708,69 +721,49 @@
     ga, vec_a, bias_a, *first = run_middle(0, oa_f, [])
     ob_f, ga, first = fence((ob_f, ga, first))
     ga_t = exchange(ga)
-    gb, vec_b, bias_b, *second = run_middle(1, ob_f, first[:3])
+    gb, vec_b, bias_b, *second = run_middle(1, ob_f, first[:4])
     ga_t, gb, second = fence((ga_t, gb, second))
-    out0, out2, out13 = second[:3]
-    act2, dqkv, o2, gb2, act3, gu, hidden, gb3 = zip(first[3:], second[3:])
+    out0, out1, out2, out3 = second[:4]
+    act2, dqkv, o2, gb2, act3, gu, hidden, gb3 = zip(first[4:], second[4:])
     gb_t = exchange(gb)
     vec2, bias2 = vec_a + vec_b, bias_a + bias_b
 
     parts = sds((2, 2, 2, 2, 64, 512))
-    moving = lambda pair: [(a, (512, 512), lambda i: (0, i)) for a in pair]
-    upto = lambda pair: [(a, (512, 512), lambda i: (0, jnp.minimum(i, 2))) for a in pair]
     units = [pltpu.VMEM((4, 512, 512), BF)]
-    r_chain = Chain(
-        *whole(
-            grads_reduce, "grads_reduce", 16, (parts, parts), [pltpu.VMEM((2048, 512), BF)],
-            me, *moving(hidden), *gb3, steps=4, time=6,
-        ),
-        (Z, X, Y, W),
-    )
-    e_chain = Chain(
-        *whole(
-            grads_expand, "grads_expand", 16, (parts, parts), units,
-            me, *act3, *moving(gu), steps=4, time=6,
-        ),
-        (Y, X, Z, W),
-    )
-    f_chain = Chain(
-        *whole(
-            grads_feature, "grads_feature", 20, (parts, parts), units,
-            me, *act2, *upto(dqkv), *o2, *gb2, steps=4, time=6,
-        ),
-        (X, Y, Z, W),
-    )
+    far = pl.BlockSpec(memory_space=pl.ANY)
+    sources = [*gb3, *hidden, *act3, *gu, *act2, *dqkv, *o2, *gb2]
+    widths = (512, 2048, 512, 2048, 512, 1536, 512, 512)
+    rk, rs, ek, es, fk, fs = pl.pallas_call(
+        grads_middle,
+        grid=(1,),
+        out_shape=(parts,) * 6,
+        in_specs=[pl.BlockSpec(memory_space=pltpu.SMEM)] + [far] * 16,
+        out_specs=[far] * 6,
+        scratch_shapes=[pltpu.VMEM((1024, n), BF) for n in widths]
+        + [pltpu.VMEM(parts.shape, BF)] * 6
+        + units
+        + [pltpu.SemaphoreType.DMA((16,)), pltpu.SemaphoreType.DMA((6,))],
+        compiler_params=params(32),
+        cost_estimate=cost(9),
+        name="grads_middle",
+    )(me, *(outside(a) for a in sources))
+    r_chain = Chain(rk, rs, (Z, X, Y, W))
+    e_chain = Chain(ek, es, (Y, X))
+    f_chain = Chain(fk, fs, (X, Y))
     chains = [r_chain, e_chain, f_chain]
-    near = shuffle(out13, *CORE)
-    gb_t, near, kept = fence((gb_t, near, [(chain.keep, chain.sent) for chain in chains]))
-    for chain, pair in zip(chains, kept):
-        chain.keep, chain.sent = pair
+    for chain in chains:
+        chain.take(chain.start())
 
     full = big((4, 256, 512))
-    gb1, dq1, dkv, term, vec1 = together(
+    gb1, back, dq1, dkv, term, vec1 = together(
         chains,
         lambda: whole(
-            backward_one, "backward_one", 32,
-            (full, full, sds((4, 64, 1024)), four, sds((8, 512), F32)),
+            backward_one, "backward_one", 28,
+            (
+                full, big((4, 256, 512), F32), full, sds((4, 64, 1024)), four, sds((8, 512), F32),
+            ),
             [pltpu.VMEM((4, 4, 2, 8, 512), BF)],
-            ga_t, gb_t, context, q1, k1, v1, p1, sample_weight, sample_mixer, time=10,
-        ),
-    )
-
-    small = sds((2, 2, 2, 2, 32, 512))
-    flat2 = lambda a: a.reshape(-1, a.shape[-1])
-    grads = whole(
-        grads_sample, "grads_sample", 20, (small,) * 4, units,
-        me, *(flat2(a) for a in (act1, dq1, cact, dkv, oa, ga_t, ob, gb_t)),
-    )
-    got_term, (ak, as_, bk, bs) = together(chains, lambda: (shuffle(term, *W), grads))
-    late = [Chain(ak, as_, (X, Y)), Chain(bk, bs, (X, Y))]
-    grad_t, vec1 = together(
-        late + chains,
-        lambda: whole(
-            backward_input, "backward_input", 24, (big((4, 4, 64, 512)), sds((8, 512), F32)),
-            [pltpu.VMEM((4, 64, 512), F32)],
-            me, gb1, x_t, dq1, term, got_term, vec1, row(first_gain), sample_weight,
+            ga_t, gb_t, x_t, context, q1, k1, v1, p1, sample_weight, sample_mixer, time=10,
         ),
     )
 
@@ -782,33 +775,45 @@
         ],
         axis=1,
     )
-    got, far, vectors = together(
-        late + chains,
-        lambda: (
-            lax.all_to_all(grad_t, "quad", 0, 0),
-            shuffle(jnp.stack([out2, near[1]]), *X),
-            vectors,
+    flat2 = lambda a: a.reshape(-1, a.shape[-1])
+    grads = whole(
+        grads_sample, "grads_sample", 20, (parts, parts), units,
+        me, *(flat2(a) for a in (act1, dq1, cact, dkv, oa, ga_t, ob, gb_t)),
+    )
+    got_term, grads = together(chains, lambda: (shuffle(term, *W), grads))
+    both = [jnp.concatenate([e_chain.keep[i], f_chain.keep[i]], axis=-2) for i in range(2)]
+    both_chain = Chain(both[0], both[1], (W,))
+    both_chain.dims = (Z, W)
+    s_chain = Chain(*grads, (X, Y))
+    grad_t = together(
+        [s_chain, r_chain, both_chain],
+        lambda: whole(
+            backward_input, "backward_input", 24, big((4, 4, 64, 512)),
+            [pltpu.VMEM((4, 64, 512), F32)],
+            me, gb1, x_t, back, term, got_term, row(first_gain),
         ),
     )
-    vectors = lax.all_to_all(vectors, SAMP, 0, 0)
+    got, vectors = together(
+        [s_chain, r_chain, both_chain],
+        lambda: (lax.all_to_all(grad_t, "quad", 0, 0), vectors),
+    )
     input_grad = whole(
         turn_out, "turn_out", 8, sds((1024, 512)), [], got.reshape(16, 4, 16, 512)
     ).reshape(64, 16, 512)
-    layer_output = whole(
-        place, "place", 16, sds((4, 256, 512)), [], me, out0,
-        (near, (None, 256, 512), (0, 0, 0)), (far, (None, 256, 512), (0, 0, 0)),
-        (far, (None, 256, 512), (1, 0, 0)),
-    ).reshape(64, 16, 512)
-    vectors, input_grad, layer_output = together(
-        late + chains, lambda: (vectors, input_grad, layer_output)
-    )
-
-    rows = jnp.concatenate([chain.keep for chain in late], axis=2)
+    early = lax.all_gather(jnp.concatenate([both_chain.keep, r_chain.keep]), "feat")
+    input_grad, vectors, early = together(
+        [s_chain], lambda: (input_grad, lax.all_to_all(vectors, SAMP, 0, 0), early)
+    )
+    vectors = whole(split, "split", 8, sds((24, 1088)), [], vectors)
+
+    rows = s_chain.keep
     around_z = lambda value, mask: lax.ppermute(value, SAMP, [(j, j ^ mask) for j in range(8)])
     from_z = [around_z(rows[i // 2, i % 2], (0, 4, 2, 6)[i]) for i in (1, 2, 3)]
-    vectors = whole(split, "split", 8, sds((24, 1088)), [], vectors)
-    early = lax.all_gather(jnp.concatenate([chain.keep for chain in chains]), "feat")
-    from_z, early, vectors = fence((from_z, early, vectors))
+    outs = [shuffle(out, "feat", d + 1) for d, out in enumerate((out1, out2, out3))]
+    from_z, vectors, outs = fence((from_z, vectors, outs))
+    layer_output = whole(
+        place, "place", 16, sds((4, 256, 512)), [], me, out0, *outs
+    ).reshape(64, 16, 512)
     total = rows[0, 0].astype(F32)
     for value in from_z:
         total = total + value.astype(F32)
@@ -819,8 +824,8 @@
     mine = (mine[0] + mine[1]) + (mine[2] + mine[3])
 
     units_of = lambda rows: [rows[i].astype(F32) for i in (0, 2, 1, 3)]
-    reduce_grad = jnp.concatenate(units_of(early[:, :64]))
-    expand, feature = units_of(early[:, 64:128]), units_of(early[:, 128:])
+    expand, feature = units_of(early[:, :64]), units_of(early[:, 64:128])
+    reduce_grad = jnp.concatenate(units_of(early[:, 128:]))
     sample = units_of(last[:, :64])
 
     gain3, shift3, gain2, shift2, off2, bias_r = (mine[i * 64 : (i + 1) * 64] for i in range(6))

time: 272 us -> 257 us (0.945)
  starting transfers between devices: 70.1 us -> 61.3 us
  other arithmetic: 15.6 us -> 21.4 us
  local copies, waits for them, and re-layouts: 14 us -> 8.36 us
  waiting for transfers between devices: 52 us -> 48 us
    pallas_call x12 -> x9, Pallas kernels: 57.3 us -> 41.9 us  [whole(): pl.pallas_call(kernel, grid=(steps,), out_shape=outs, in_specs=specs, out...]
    pallas_call x0 -> x1, Pallas kernels: none -> 13.8 us  [local_small(): pl.pallas_call(grads_middle, grid=(1,), out_shape=(parts,) * 6, in_specs=...]
    ppermute x28 -> x24, waiting for transfers between devices: 41.6 us -> 33.2 us  [shuffle(): return lax.ppermute(value, axis, [(i, i ^ mask) for i in range(size)])]
    convert_element_type x21 -> x16, other arithmetic: 8.65 us -> 15.5 us  [plus(): return (a.astype(F32) + b.astype(F32)).astype(BF)]
    ppermute x28 -> x24, starting transfers between devices: 33.3 us -> 26.7 us  [shuffle(): return lax.ppermute(value, axis, [(i, i ^ mask) for i in range(size)])]
    unnamed x96 -> x72, local copies, waits for them, and re-layouts: 7.16 us -> 2.51 us
    ppermute x3, waiting for transfers between devices: 0.01 us -> 3.88 us  [local_small(): lax.ppermute(value, SAMP, [(j, j ^ mask) for j in range(8)])]
  transfers between devices with their start and end apart: 38 -> 34, of which waited for: 12 -> 12; matrix products, arithmetic and copies ran while one was open for 4% -> 8% of each run, Pallas kernels for 31% -> 27%
where the time goes in v1:
time: 257 us; the launch traced here: 256 us
  Pallas kernels  97.2 us (38%)
  starting transfers between devices  61.3 us (24%)
  waiting for transfers between devices  48 us (19%)
  other arithmetic  21.4 us (8%)
  blocking collectives  14.4 us (6%)
  local copies, waits for them, and re-layouts  8.36 us (3%)
  between operations  5.32 us (2%)
    pallas_call x9, Pallas kernels, whole(): pl.pallas_call(kernel, grid=(steps,), out_shape=outs, in_specs=specs, out...  41.9 us
    pallas_call x2, Pallas kernels, run_middle(): pl.pallas_call(middle, grid_spec=pltpu.PrefetchScalarGridSpec(num_scalar_...  41.5 us
    ppermute x24, waiting for transfers between devices, shuffle(): return lax.ppermute(value, axis, [(i, i ^ mask) for i in range(size)])  33.2 us
    ppermute x24, starting transfers between devices, shuffle(): return lax.ppermute(value, axis, [(i, i ^ mask) for i in range(size)])  26.7 us
    all_to_all x4, starting transfers between devices, exchange(): return lax.all_to_all(value, ('quad', 'feat'), 0, 0).reshape(shape)  17.3 us
    convert_element_type x16, other arithmetic, plus(): return (a.astype(F32) + b.astype(F32)).astype(BF)  15.5 us
    pallas_call x1, Pallas kernels, local_small(): pl.pallas_call(grads_middle, grid=(1,), out_shape=(parts,) * 6, in_specs=...  13.8 us
    all_to_all x4, waiting for transfers between devices, exchange(): return lax.all_to_all(value, ('quad', 'feat'), 0, 0).reshape(shape)  10.3 us
  transfers between devices with their start and end apart: 34, of which 12 were waited for; matrix products, arithmetic and copies ran while one was open for 8% of the time, Pallas kernels for 27%

profile of v1, /device:TPU:0, one launch (start us, length us, event | category | flops | bytes accessed | tf_op | source)
XLA Modules:
  0.0 256.0 jit_solution(7451933424018582775)
XLA Ops:
  0.7 2.8 %turn_in.1 = bf16[16,4,16,512]{3,2,1,0:T(8,128)(2,1)} custom-call(bf16[1024,512]{1,0:T(8,128)(2,1)} %bitcast.283), custom_call_target="tpu_custom_call" | custom-call | flops 3300000000 | bytes 6000000 | tf_op jit(solution)/shard_map/turn_in/pallas_call | solution.py:561
  4.3 4.8 %all-to-all-start = ((bf16[4,4,64,512]{3,2,1,0:T(8,128)(2,1)}), bf16[4,4,64,512]{3,2,1,0:T(8,128)(2,1)S(1)}, u32[]{:S(2)}, u32[]{:S(2)}) async-start(bf16[4,4,64,512]{3,2,1,0:T(8,128)(2,1)} %bitcast.10), calls=%async_computation | async-start | bytes 2097152 | tf_op jit(solution)/shard_map/all_to_all | solution.py:634
  10.2 1.6 collective-permute-start.1
  16.9 7.4 %collective-permute-done.1.refs_3_.refs_4_ = bf16[2,256,512]{2,1,0:T(8,128)(2,1)S(1)} collective-permute-done((bf16[2,256,512]{2,1,0:T(8,128)(2,1)S(1)}, bf16[2,256,512]{2,1,0:T(8,128)(2,1)S(1)}, u32[]{:S(2)}, u32[]{:S(2)}) %collective-permute-start.1) | collective-permute-done | bytes 524320 | tf_op jit(solution)/shard_map/ppermute | solution.py:576
  26.3 1.6 collective-permute-start.2
  28.0 2.7 %collective-permute-start.3 = (bf16[4,64,512]{2,1,0:T(8,128)(2,1)S(1)}, bf16[4,64,512]{2,1,0:T(8,128)(2,1)S(1)}, u32[]{:S(2)}, u32[]{:S(2)}) collective-permute-start(bf16[4,64,512]{2,1,0:T(8,128)(2,1)S(1)} %dynamic-slice_bitcast_fusion.own_ref), channel_id=1, source_target_pairs={{0,16},{16,0},{1,17},{17,1},{2,18},{18,2},{3,19},{19,3},{4,20},{20... | collective-permute-start | bytes 786440 | tf_op jit(solution)/shard_map/ppermute | solution.py:576
  30.6 4.9 %project_queries.1 = (bf16[4,256,512]{2,1,0:T(8,128)(2,1)}, bf16[4,256,512]{2,1,0:T(8,128)(2,1)}) custom-call(bf16[4,4,64,512]{3,2,1,0:T(8,128)(2,1)} %copy-done.15, f32[1,512]{1,0:T(1,128)S(1)} %bitcast.274, f32[1,512]{1,0:T(1,128)S(1)} %bitcast.258, bf16[512,1536]{1,0:T(8,128)(2,1)} %w_ref.5, f32[1,1024]{1,0:T(1,128)S(1)} %bitcast.254), custom_call_target="tpu_custom_call" | custom-call | flops 3300000000 | bytes 6000000 | tf_op jit(solution)/shard_map/project_queries/pallas_call | solution.py:561
  35.6 6.3 %collective-permute-done.3.got_ref = bf16[4,64,512]{2,1,0:T(8,128)(2,1)S(1)} collective-permute-done((bf16[4,64,512]{2,1,0:T(8,128)(2,1)S(1)}, bf16[4,64,512]{2,1,0:T(8,128)(2,1)S(1)}, u32[]{:S(2)}, u32[]{:S(2)}) %collective-permute-start.3) | collective-permute-done | bytes 262176 | tf_op jit(solution)/shard_map/ppermute | solution.py:576
  42.6 8.9 %forward_one.1 = (bf16[4,4,4,8,512]{4,3,2,1,0:T(8,128)(2,1)}, bf16[4,4,4,8,512]{4,3,2,1,0:T(8,128)(2,1)}, bf16[4,64,512]{2,1,0:T(8,128)(2,1)}, bf16[4,64,512]{2,...) custom-call(s32[8]{0:T(128)S(1)} %stack.50.me_ref, ...), custom_call_target="tpu_custom_call" | custom-call | flops 7699999744 | bytes 14000000 | tf_op jit(solution)/shard_map/forward_one/pallas_call | solution.py:561
  51.6 3.7 %all-to-all-start.1 = ((bf16[16,4,8,512]{3,2,1,0:T(8,128)(2,1)}), bf16[16,4,8,512]{3,2,1,0:T(8,128)(2,1)S(1)}, u32[]{:S(2)}, u32[]{:S(2)}) async-start(bf16[16,4,8,512]{3,2,1,0:T(8,128)(2,1)} %bitcast.290), calls=%async_computation.1 | async-start | bytes 1048576 | tf_op jit(solution)/shard_map/all_to_all | solution.py:664
  55.5 10.3 %all-to-all-done.1 = bf16[16,4,8,512]{3,2,1,0:T(8,128)(2,1)S(1)} async-done(((bf16[16,4,8,512]{3,2,1,0:T(8,128)(2,1)}), bf16[16,4,8,512]{3,2,1,0:T(8,128)(2,1)S(1)}, u32[]{:S(2)}, u32[]{:S(2)}) %all-to-all-start.1) | async-done | bytes 524320 | tf_op jit(solution)/shard_map/all_to_all | solution.py:664
  65.8 3.8 %all-to-all-start.2 = ((bf16[16,4,8,512]{3,2,1,0:T(8,128)(2,1)}), bf16[16,4,8,512]{3,2,1,0:T(8,128)(2,1)S(1)}, u32[]{:S(2)}, u32[]{:S(2)}) async-start(bf16[16,4,8,512]{3,2,1,0:T(8,128)(2,1)} %bitcast.292), calls=%async_computation.2 | async-start | bytes 1048576 | tf_op jit(solution)/shard_map/all_to_all | solution.py:664
  69.7 20.8 %middle.2 = (bf16[4,4,4,8,512]{4,3,2,1,0:T(8,128)(2,1)}, f32[8,512]{1,0:T(8,128)S(1)}, f32[1,2048]{1,0:T(1,128)S(1)}, bf16[256,512]{1,0:T(8,128)(2,1)}, bf16[256...) custom-call(s32[9]{0:T(128)S(1)} %concatenate.51.me_ref, ...), custom_call_target="tpu_custom_call" | custom-call | flops 32999999488 | bytes 60000000 | tf_op jit(solution)/shard_map/middle/pallas_call | solution.py:685
  90.5 4.9 %all-to-all-start.3 = ((bf16[16,4,8,512]{3,2,1,0:T(8,128)(2,1)}), bf16[16,4,8,512]{3,2,1,0:T(8,128)(2,1)S(1)}, u32[]{:S(2)}, u32[]{:S(2)}) async-start(bf16[16,4,8,512]{3,2,1,0:T(8,128)(2,1)} %bitcast.298), calls=%async_computation.3 | async-start | bytes 1048576 | tf_op jit(solution)/shard_map/all_to_all | solution.py:664
  95.5 20.7 %middle.3 = (bf16[4,4,4,8,512]{4,3,2,1,0:T(8,128)(2,1)}, f32[8,512]{1,0:T(8,128)S(1)}, f32[1,2048]{1,0:T(1,128)S(1)}, bf16[256,512]{1,0:T(8,128)(2,1)}, bf16[256...) custom-call(s32[9]{0:T(128)S(1)} %concatenate.52.me_ref, ...), custom_call_target="tpu_custom_call", output_to_operand_aliasing={{3}: (24, {}), {4}: (25, {}), {5}: (26, {}), {6}: (27, {})} | custom-call | flops 32999999488 | bytes 60000000 | tf_op jit(solution)/shard_map/middle/pallas_call | solution.py:685
  117.0 13.8 %grads_middle.1 = (bf16[2,2,2,2,64,512]{5,4,3,2,1,0:T(8,128)(2,1)S(1)}, bf16[2,2,2,2,64,512]{5,4,3,2,1,0:T(8,128)(2,1)}, bf16[2,2,2,2,64,512]{5,4,3,2,1,0:T(8,12...) custom-call(s32[8]{0:T(128)S(1)} %stack.50.me_ref, ...), custom_call_target="tpu_custom_call" | custom-call | flops 9900000256 | bytes 18000000 | tf_op jit(solution)/shard_map/grads_middle/pallas_call | solution.py:736
  131.8 4.9 %all-to-all-start.4 = ((bf16[16,4,8,512]{3,2,1,0:T(8,128)(2,1)}), bf16[16,4,8,512]{3,2,1,0:T(8,128)(2,1)}, u32[]{:S(2)}, u32[]{:S(2)}) async-start(bf16[16,4,8,512]{3,2,1,0:T(8,128)(2,1)} %bitcast.296), calls=%async_computation.4 | async-start | bytes 1048576 | tf_op jit(solution)/shard_map/all_to_all | solution.py:664
  136.7 2.6 %fusion = (bf16[2,2,2,64,512]{4,3,2,1,0:T(8,128)(2,1)}, bf16[1,2,2,2,64,512]{5,4,3,2,1,0:T(8,128)(2,1)}) fusion(bf16[2,2,2,2,64,512]{5,4,3,2,1,0:T(8,128)(2,1)} %collective-permute-done.4, bf16[2,2,2,2,64,512]{5,4,3,2,1,0:T(8,128)(2,1)S(1)} %get-tuple-element.210), kind=kLoop, calls=%fused_computation.9 | loop fusion | flops 2097152 | bytes 3145728 | tf_op jit(solution)/shard_map/convert_element_type | solution.py:592
  139.3 1.9 collective-permute-start.5
  141.2 2.5 add_convert_fusion.3
  143.7 1.5 collective-permute-start.7
  145.2 2.3 add_convert_fusion.2
  147.5 1.5 collective-permute-start.9
  148.9 10.9 %backward_one.1 = (bf16[4,256,512]{2,1,0:T(8,128)(2,1)}, f32[4,256,512]{2,1,0:T(8,128)}, bf16[4,256,512]{2,1,0:T(8,128)(2,1)}, bf16[4,64,1024]{2,1,0:T(8,128)(2,...) custom-call(bf16[4,4,4,8,512]{4,3,2,1,0:T(8,128)(2,1)} %bitcast.294, ...), custom_call_target="tpu_custom_call" | custom-call | flops 11000000512 | bytes 20000000 | tf_op jit(solution)/shard_map/backward_one/pallas_call | solution.py:561
  159.9 1.2 collective-permute-done.9
  162.8 1.5 collective-permute-start.11
  166.2 2.8 %collective-permute-start.13 = (bf16[4,64,512]{2,1,0:T(8,128)(2,1)S(1)}, bf16[4,64,512]{2,1,0:T(8,128)(2,1)S(1)}, u32[]{:S(2)}, u32[]{:S(2)}) collective-permute-start(bf16[4,64,512]{2,1,0:T(8,128)(2,1)S(1)} %copy-done.32), channel_id=1, source_target_pairs={{0,16},{16,0},{1,17},{17,1},{2,18},{18,2},{3,19},{19,3},{4,20},{20... | collective-permute-start | bytes 786440 | tf_op jit(solution)/shard_map/ppermute | solution.py:576
  168.9 4.1 %grads_sample.1 = (bf16[2,2,2,2,64,512]{5,4,3,2,1,0:T(8,128)(2,1)S(1)}, bf16[2,2,2,2,64,512]{5,4,3,2,1,0:T(8,128)(2,1)S(1)}) custom-call(s32[8]{0:T(128)S(1)} %stack.50.me_ref, bf16[1024,512]{1,0:T(8,128)(2,1)} %bitcast.306, bf16[1024,512]{1,0:T(8,128)(2,1)} %bitcast.308, bf16[256,512]{1,0:T(8,128)(2,1)} %bitcast.310, bf16[256,1024]{1,0:T(8,128)(2,1)} %bitcast.277, ...), custom_call_target="tpu_custom_call" | custom-call | flops 3300000000 | bytes 6000000 | tf_op jit(solution)/shard_map/grads_sample/pallas_call | solution.py:561
  173.1 2.1 collective-permute-done.10
  175.1 3.7 %collective-permute-done.13.got_ref = bf16[4,64,512]{2,1,0:T(8,128)(2,1)S(1)} collective-permute-done((bf16[4,64,512]{2,1,0:T(8,128)(2,1)S(1)}, bf16[4,64,512]{2,1,0:T(8,128)(2,1)S(1)}, u32[]{:S(2)}, u32[]{:S(2)}) %collective-permute-start.13) | collective-permute-done | bytes 262176 | tf_op jit(solution)/shard_map/ppermute | solution.py:576
  180.1 1.5 collective-permute-start.15
  181.9 5.3 %backward_input.1 = bf16[4,4,64,512]{3,2,1,0:T(8,128)(2,1)} custom-call(s32[8]{0:T(128)S(1)} %stack.50.me_ref, bf16[4,256,512]{2,1,0:T(8,128)(2,1)} %get-tuple-element.243.gb1_ref, bf16[4,4,64,512]{3,2,1,0:T(8,128)(2,1)} %copy-done.15, f32[4,256,512]{2,1,0:T(8,128)} %get-tuple-element.244.a_ref, bf16[4,64,512]{2,1,0:T(8,128)(2,1)} %get-tuple-element.231.term_ref, ...), custom_call_target="tpu_custom_call" | custom-call | flops 3300000000 | bytes 6000000 | tf_op jit(solution)/shard_map/backward_input/pallas_call | solution.py:561
  187.3 3.4 %collective-permute-done.16 = bf16[2,128,512]{2,1,0:T(8,128)(2,1)S(1)} collective-permute-done((bf16[2,128,512]{2,1,0:T(8,128)(2,1)S(1)}, bf16[2,128,512]{2,1,0:T(8,128)(2,1)S(1)}, u32[]{:S(2)}, u32[]{:S(2)}) %collective-permute-start.16) | collective-permute-done | bytes 262176 | tf_op jit(solution)/shard_map/ppermute | solution.py:576
  190.6 3.5 %all-to-all-start.5 = ((bf16[4,4,64,512]{3,2,1,0:T(8,128)(2,1)}), bf16[4,4,64,512]{3,2,1,0:T(8,128)(2,1)S(1)}, u32[]{:S(2)}, u32[]{:S(2)}) async-start(bf16[4,4,64,512]{3,2,1,0:T(8,128)(2,1)} %backward_input.1), calls=%async_computation.5 | async-start | bytes 2097152 | tf_op jit(solution)/shard_map/all_to_all | solution.py:798
  194.2 2.3 fusion.3
  196.5 1.5 collective-permute-start.17
  198.0 1.5 collective-permute-start.19
  199.6 1.5 collective-permute-start.18
  202.3 7.7 %collective-permute-done.18 = bf16[64,512]{1,0:T(8,128)(2,1)S(1)} collective-permute-done((bf16[64,512]{1,0:T(8,128)(2,1)S(1)}, bf16[64,512]{1,0:T(8,128)(2,1)S(1)}, u32[]{:S(2)}, u32[]{:S(2)}) %collective-permute-start.18) | collective-permute-done | bytes 65568 | tf_op jit(solution)/shard_map/ppermute | solution.py:576
  210.2 1.4 collective-permute-done.17
  213.1 2.6 %turn_out.1 = bf16[1024,512]{1,0:T(8,128)(2,1)} custom-call(bf16[16,4,16,512]{3,2,1,0:T(8,128)(2,1)} %bitcast.282), custom_call_target="tpu_custom_call" | custom-call | flops 3300000000 | bytes 6000000 | tf_op jit(solution)/shard_map/turn_out/pallas_call | solution.py:561
  216.4 4.5 %all-to-all-start.6 = ((f32[8,1,1088]{2,1,0:T(1,128)}), f32[8,1,1088]{2,1,0:T(1,128)S(1)}, u32[]{:S(2)}, u32[]{:S(2)}) async-start(f32[8,1,1088]{2,1,0:T(1,128)} %copy.56), calls=%async_computation.6 | async-start | bytes 73728 | tf_op jit(solution)/shard_map/all_to_all | solution.py:805
  221.0 2.1 collective-permute-start.20
  223.1 8.6 %all-gather = bf16[768,512]{1,0:T(8,128)(2,1)S(1)} all-gather(bf16[192,512]{1,0:T(8,128)(2,1)S(1)} %pad_maximum_fusion.4), channel_id=2, replica_groups=mesh['half'=2,'quad'=4,'feat'=4] {'feat'}, dimensions={0}, use_global_device_ids=true | all-gather | bytes 983040 | tf_op jit(solution)/shard_map/all_gather | solution.py:803
  232.8 3.3 %collective-permute-start.23 = (bf16[64,512]{1,0:T(8,128)(2,1)S(1)}, bf16[64,512]{1,0:T(8,128)(2,1)S(1)}, u32[]{:S(2)}, u32[]{:S(2)}) collective-permute-start(bf16[64,512]{1,0:T(8,128)(2,1)S(1)} %get-tuple-element.308), channel_id=1, source_target_pairs={{0,24},{4,28},{8,16},{12,20},{16,8},{20,12},{24,0},{28,4},{1,25},{... | collective-permute-start | bytes 196616 | tf_op jit(solution)/shard_map/ppermute | solution.py:810
  240.6 3.8 %collective-permute-done.21 = bf16[64,512]{1,0:T(8,128)(2,1)S(1)} collective-permute-done((bf16[64,512]{1,0:T(8,128)(2,1)S(1)}, bf16[64,512]{1,0:T(8,128)(2,1)S(1)}, u32[]{:S(2)}, u32[]{:S(2)}) %collective-permute-start.21) | collective-permute-done | bytes 65568 | tf_op jit(solution)/shard_map/ppermute | solution.py:810
  244.5 5.9 %all-gather.1 = bf16[288,512]{1,0:T(8,128)(2,1)S(1)} all-gather(bf16[72,512]{1,0:T(8,128)(2,1)S(1)} %pad_maximum_fusion.6), channel_id=3, replica_groups=mesh['half'=2,'quad'=4,'feat'=4] {'feat'}, dimensions={0}, use_global_device_ids=true | all-gather | bytes 368640 | tf_op jit(solution)/shard_map/all_gather | solution.py:821
  253.8 2.2 place.1
  (180 shorter events, 25.6 us)
Async XLA Ops:
  3.8 5.4 %collective-permute-start = (bf16[4,256,512]{2,1,0:T(8,128)(2,1)S(1)}, bf16[4,256,512]{2,1,0:T(8,128)(2,1)}, u32[]{:S(2)}, u32[]{:S(2)}) collective-permute-start(bf16[4,256,512]{2,1,0:T(8,128)(2,1)S(1)} %pad_maximum_fusion), channel_id=1, source_target_pairs={{0,1},{1,0},{2,3},{3,2},{4,5},{5,4},{6,7},{7,6},{8,9},{9,8},{10,11... | collective-permute-start | bytes 3145736 | tf_op jit(solution)/shard_map/ppermute | solution.py:576
  4.3 20.8 %all-to-all-start = ((bf16[4,4,64,512]{3,2,1,0:T(8,128)(2,1)}), bf16[4,4,64,512]{3,2,1,0:T(8,128)(2,1)S(1)}, u32[]{:S(2)}, u32[]{:S(2)}) async-start(bf16[4,4,64,512]{3,2,1,0:T(8,128)(2,1)} %bitcast.10), calls=%async_computation | async-start | bytes 2097152 | tf_op jit(solution)/shard_map/all_to_all | solution.py:634
  9.1 21.5 %copy-start.1 = (f32[1024]{0:T(1024)S(1)}, f32[1024]{0:T(1024)}, u32[]{:S(2)}) copy-start(f32[1024]{0:T(1024)} %param.28) | copy-start | bytes 12292
  9.1 21.5 %copy-start.3 = (f32[512]{0:T(512)S(1)}, f32[512]{0:T(512)}, u32[]{:S(2)}) copy-start(f32[512]{0:T(512)} %param.26) | copy-start | bytes 6148
  9.1 21.5 %copy-start.11 = (f32[512]{0:T(512)S(1)}, f32[512]{0:T(512)}, u32[]{:S(2)}) copy-start(f32[512]{0:T(512)} %param.25) | copy-start | bytes 6148
  10.2 14.1 %collective-permute-start.1 = (bf16[2,256,512]{2,1,0:T(8,128)(2,1)S(1)}, bf16[2,256,512]{2,1,0:T(8,128)(2,1)S(1)}, u32[]{:S(2)}, u32[]{:S(2)}) collective-permute-start(bf16[2,256,512]{2,1,0:T(8,128)(2,1)S(1)} %pad_maximum_fusion.1), channel_id=1, source_target_pairs={{0,2},{1,3},{2,0},{3,1},{4,6},{5,7},{6,4},{7,5},{8,10},{9,11},{10,... | collective-permute-start | bytes 1572872 | tf_op jit(solution)/shard_map/ppermute | solution.py:576
  26.3 15.6 %collective-permute-start.2 = (bf16[2,256,512]{2,1,0:T(8,128)(2,1)S(1)}, bf16[2,256,512]{2,1,0:T(8,128)(2,1)S(1)}, u32[]{:S(2)}, u32[]{:S(2)}) collective-permute-start(bf16[2,256,512]{2,1,0:T(8,128)(2,1)S(1)} %pad_maximum_fusion.2), channel_id=1, source_target_pairs={{0,2},{1,3},{2,0},{3,1},{4,6},{5,7},{6,4},{7,5},{8,10},{9,11},{10,... | collective-permute-start | bytes 1572872 | tf_op jit(solution)/shard_map/ppermute | solution.py:576
  28.0 13.9 %collective-permute-start.3 = (bf16[4,64,512]{2,1,0:T(8,128)(2,1)S(1)}, bf16[4,64,512]{2,1,0:T(8,128)(2,1)S(1)}, u32[]{:S(2)}, u32[]{:S(2)}) collective-permute-start(bf16[4,64,512]{2,1,0:T(8,128)(2,1)S(1)} %dynamic-slice_bitcast_fusion.own_ref), channel_id=1, source_target_pairs={{0,16},{16,0},{1,17},{17,1},{2,18},{18,2},{3,19},{19,3},{4,20},{20... | collective-permute-start | bytes 786440 | tf_op jit(solution)/shard_map/ppermute | solution.py:576
  51.5 18.1 %copy-start = (f32[2048]{0:T(1024)S(1)}, f32[2048]{0:T(1024)}, u32[]{:S(2)}) copy-start(f32[2048]{0:T(1024)} %param.40) | copy-start | bytes 24580
  51.5 18.1 %copy-start.2 = (f32[1024]{0:T(1024)S(1)}, f32[1024]{0:T(1024)}, u32[]{:S(2)}) copy-start(f32[1024]{0:T(1024)} %param.34) | copy-start | bytes 12292
  51.5 18.1 %copy-start.4 = (f32[512]{0:T(512)S(1)}, f32[512]{0:T(512)}, u32[]{:S(2)}) copy-start(f32[512]{0:T(512)} %param.30) | copy-start | bytes 6148
  51.5 18.1 %copy-start.5 = (f32[512]{0:T(512)S(1)}, f32[512]{0:T(512)}, u32[]{:S(2)}) copy-start(f32[512]{0:T(512)} %param.31) | copy-start | bytes 6148
  51.5 18.1 %copy-start.6 = (f32[512]{0:T(512)S(1)}, f32[512]{0:T(512)}, u32[]{:S(2)}) copy-start(f32[512]{0:T(512)} %param.32) | copy-start | bytes 6148
  51.5 18.1 %copy-start.7 = (f32[512]{0:T(512)S(1)}, f32[512]{0:T(512)}, u32[]{:S(2)}) copy-start(f32[512]{0:T(512)} %param.36) | copy-start | bytes 6148
  51.6 18.1 %copy-start.8 = (f32[512]{0:T(512)S(1)}, f32[512]{0:T(512)}, u32[]{:S(2)}) copy-start(f32[512]{0:T(512)} %param.37) | copy-start | bytes 6148
  51.6 18.1 %copy-start.9 = (f32[512]{0:T(512)S(1)}, f32[512]{0:T(512)}, u32[]{:S(2)}) copy-start(f32[512]{0:T(512)} %param.38) | copy-start | bytes 6148
  51.6 18.1 %copy-start.10 = (f32[512]{0:T(512)S(1)}, f32[512]{0:T(512)}, u32[]{:S(2)}) copy-start(f32[512]{0:T(512)} %param.42) | copy-start | bytes 6148
  51.6 14.2 %all-to-all-start.1 = ((bf16[16,4,8,512]{3,2,1,0:T(8,128)(2,1)}), bf16[16,4,8,512]{3,2,1,0:T(8,128)(2,1)S(1)}, u32[]{:S(2)}, u32[]{:S(2)}) async-start(bf16[16,4,8,512]{3,2,1,0:T(8,128)(2,1)} %bitcast.290), calls=%async_computation.1 | async-start | bytes 1048576 | tf_op jit(solution)/shard_map/all_to_all | solution.py:664
  65.8 24.7 %all-to-all-start.2 = ((bf16[16,4,8,512]{3,2,1,0:T(8,128)(2,1)}), bf16[16,4,8,512]{3,2,1,0:T(8,128)(2,1)S(1)}, u32[]{:S(2)}, u32[]{:S(2)}) async-start(bf16[16,4,8,512]{3,2,1,0:T(8,128)(2,1)} %bitcast.292), calls=%async_computation.2 | async-start | bytes 1048576 | tf_op jit(solution)/shard_map/all_to_all | solution.py:664
  90.5 25.7 %all-to-all-start.3 = ((bf16[16,4,8,512]{3,2,1,0:T(8,128)(2,1)}), bf16[16,4,8,512]{3,2,1,0:T(8,128)(2,1)S(1)}, u32[]{:S(2)}, u32[]{:S(2)}) async-start(bf16[16,4,8,512]{3,2,1,0:T(8,128)(2,1)} %bitcast.298), calls=%async_computation.3 | async-start | bytes 1048576 | tf_op jit(solution)/shard_map/all_to_all | solution.py:664
  130.8 5.9 %collective-permute-start.4 = (bf16[2,2,2,2,64,512]{5,4,3,2,1,0:T(8,128)(2,1)}, bf16[2,2,2,2,64,512]{5,4,3,2,1,0:T(8,128)(2,1)}, u32[]{:S(2)}, u32[]{:S(2)}) collective-permute-start(bf16[2,2,2,2,64,512]{5,4,3,2,1,0:T(8,128)(2,1)} %get-tuple-element.211), channel_id=1, source_target_pairs={{0,1},{1,0},{2,3},{3,2},{4,5},{5,4},{6,7},{7,6},{8,9},{9,8},{10,11... | collective-permute-start | bytes 3145736 | tf_op jit(solution)/shard_map/ppermute | solution.py:576
  131.3 9.9 %collective-permute-start.6 = (bf16[2,2,2,2,64,512]{5,4,3,2,1,0:T(8,128)(2,1)}, bf16[2,2,2,2,64,512]{5,4,3,2,1,0:T(8,128)(2,1)}, u32[]{:S(2)}, u32[]{:S(2)}) collective-permute-start(bf16[2,2,2,2,64,512]{5,4,3,2,1,0:T(8,128)(2,1)} %get-tuple-element.213), channel_id=1, source_target_pairs={{0,1},{1,0},{2,3},{3,2},{4,5},{5,4},{6,7},{7,6},{8,9},{9,8},{10,11... | collective-permute-start | bytes 3145736 | tf_op jit(solution)/shard_map/ppermute | solution.py:576
  131.4 13.8 %collective-permute-start.8 = (bf16[2,2,2,2,64,512]{5,4,3,2,1,0:T(8,128)(2,1)}, bf16[2,2,2,2,64,512]{5,4,3,2,1,0:T(8,128)(2,1)}, u32[]{:S(2)}, u32[]{:S(2)}) collective-permute-start(bf16[2,2,2,2,64,512]{5,4,3,2,1,0:T(8,128)(2,1)} %get-tuple-element.215), channel_id=1, source_target_pairs={{0,1},{1,0},{2,3},{3,2},{4,5},{5,4},{6,7},{7,6},{8,9},{9,8},{10,11... | collective-permute-start | bytes 3145736 | tf_op jit(solution)/shard_map/ppermute | solution.py:576
  131.8 17.1 %all-to-all-start.4 = ((bf16[16,4,8,512]{3,2,1,0:T(8,128)(2,1)}), bf16[16,4,8,512]{3,2,1,0:T(8,128)(2,1)}, u32[]{:S(2)}, u32[]{:S(2)}) async-start(bf16[16,4,8,512]{3,2,1,0:T(8,128)(2,1)} %bitcast.296), calls=%async_computation.4 | async-start | bytes 1048576 | tf_op jit(solution)/shard_map/all_to_all | solution.py:664
  139.3 20.6 %collective-permute-start.5 = (bf16[2,2,2,64,512]{4,3,2,1,0:T(8,128)(2,1)}, bf16[2,2,2,64,512]{4,3,2,1,0:T(8,128)(2,1)}, u32[]{:S(2)}, u32[]{:S(2)}) collective-permute-start(bf16[2,2,2,64,512]{4,3,2,1,0:T(8,128)(2,1)} %get-tuple-element.280), channel_id=1, source_target_pairs={{0,8},{4,12},{8,0},{12,4},{1,9},{5,13},{9,1},{13,5},{2,10},{6,14},... | collective-permute-start | bytes 1572872 | tf_op jit(solution)/shard_map/ppermute | solution.py:576
  143.7 16.2 %collective-permute-start.7 = (bf16[2,2,2,64,512]{4,3,2,1,0:T(8,128)(2,1)}, bf16[2,2,2,64,512]{4,3,2,1,0:T(8,128)(2,1)}, u32[]{:S(2)}, u32[]{:S(2)}) collective-permute-start(bf16[2,2,2,64,512]{4,3,2,1,0:T(8,128)(2,1)} %get-tuple-element.279), channel_id=1, source_target_pairs={{0,4},{4,0},{8,12},{12,8},{1,5},{5,1},{9,13},{13,9},{2,6},{6,2},{1... | collective-permute-start | bytes 1572872 | tf_op jit(solution)/shard_map/ppermute | solution.py:576
  147.5 13.6 %collective-permute-start.9 = (bf16[2,2,2,64,512]{4,3,2,1,0:T(8,128)(2,1)}, bf16[2,2,2,64,512]{4,3,2,1,0:T(8,128)(2,1)S(1)}, u32[]{:S(2)}, u32[]{:S(2)}) collective-permute-start(bf16[2,2,2,64,512]{4,3,2,1,0:T(8,128)(2,1)} %get-tuple-element.277), channel_id=1, source_target_pairs={{0,2},{1,3},{2,0},{3,1},{4,6},{5,7},{6,4},{7,5},{8,10},{9,11},{10,... | collective-permute-start | bytes 1572872 | tf_op jit(solution)/shard_map/ppermute | solution.py:576
  148.9 12.9 %copy-start.14 = (bf16[1,2,2,2,64,512]{5,4,3,2,1,0:T(8,128)(2,1)S(1)}, bf16[1,2,2,2,64,512]{5,4,3,2,1,0:T(8,128)(2,1)}, u32[]{:S(2)}) copy-start(bf16[1,2,2,2,64,512]{5,4,3,2,1,0:T(8,128)(2,1)} %get-tuple-element.278) | copy-start | bytes 1572868
  148.9 15.4 %copy-start.13 = (bf16[1,2,2,2,64,512]{5,4,3,2,1,0:T(8,128)(2,1)S(1)}, bf16[1,2,2,2,64,512]{5,4,3,2,1,0:T(8,128)(2,1)}, u32[]{:S(2)}) copy-start(bf16[1,2,2,2,64,512]{5,4,3,2,1,0:T(8,128)(2,1)} %get-tuple-element.281) | copy-start | bytes 1572868
  161.2 11.9 %collective-permute-start.12 = (bf16[2,2,64,512]{3,2,1,0:T(8,128)(2,1)S(1)}, bf16[2,2,64,512]{3,2,1,0:T(8,128)(2,1)S(1)}, u32[]{:S(2)}, u32[]{:S(2)}) collective-permute-start(bf16[2,2,64,512]{3,2,1,0:T(8,128)(2,1)S(1)} %fusion.17), channel_id=1, source_target_pairs={{0,4},{4,0},{8,12},{12,8},{1,5},{5,1},{9,13},{13,9},{2,6},{6,2},{1... | collective-permute-start | bytes 786440 | tf_op jit(solution)/shard_map/ppermute | solution.py:576
  162.8 10.2 %collective-permute-start.11 = (bf16[2,2,64,512]{3,2,1,0:T(8,128)(2,1)S(1)}, bf16[2,2,64,512]{3,2,1,0:T(8,128)(2,1)S(1)}, u32[]{:S(2)}, u32[]{:S(2)}) collective-permute-start(bf16[2,2,64,512]{3,2,1,0:T(8,128)(2,1)S(1)} %fusion.16), channel_id=1, source_target_pairs={{0,2},{1,3},{2,0},{3,1},{4,6},{5,7},{6,4},{7,5},{8,10},{9,11},{10,... | collective-permute-start | bytes 786440 | tf_op jit(solution)/shard_map/ppermute | solution.py:576
  165.5 9.6 %collective-permute-start.10 = (bf16[2,2,64,512]{3,2,1,0:T(8,128)(2,1)S(1)}, bf16[2,2,64,512]{3,2,1,0:T(8,128)(2,1)S(1)}, u32[]{:S(2)}, u32[]{:S(2)}) collective-permute-start(bf16[2,2,64,512]{3,2,1,0:T(8,128)(2,1)S(1)} %get-tuple-element.283), channel_id=1, source_target_pairs={{0,2},{1,3},{2,0},{3,1},{4,6},{5,7},{6,4},{7,5},{8,10},{9,11},{10,... | collective-permute-start | bytes 786440 | tf_op jit(solution)/shard_map/ppermute | solution.py:576
  166.2 12.7 %collective-permute-start.13 = (bf16[4,64,512]{2,1,0:T(8,128)(2,1)S(1)}, bf16[4,64,512]{2,1,0:T(8,128)(2,1)S(1)}, u32[]{:S(2)}, u32[]{:S(2)}) collective-permute-start(bf16[4,64,512]{2,1,0:T(8,128)(2,1)S(1)} %copy-done.32), channel_id=1, source_target_pairs={{0,16},{16,0},{1,17},{17,1},{2,18},{18,2},{3,19},{19,3},{4,20},{20... | collective-permute-start | bytes 786440 | tf_op jit(solution)/shard_map/ppermute | solution.py:576
  180.1 7.2 %collective-permute-start.15 = (bf16[2,64,512]{2,1,0:T(8,128)(2,1)S(1)}, bf16[2,64,512]{2,1,0:T(8,128)(2,1)S(1)}, u32[]{:S(2)}, u32[]{:S(2)}) collective-permute-start(bf16[2,64,512]{2,1,0:T(8,128)(2,1)S(1)} %get-tuple-element.303), channel_id=1, source_target_pairs={{0,4},{4,0},{8,12},{12,8},{1,5},{5,1},{9,13},{13,9},{2,6},{6,2},{1... | collective-permute-start | bytes 393224 | tf_op jit(solution)/shard_map/ppermute | solution.py:576
  181.6 9.0 %collective-permute-start.14 = (bf16[2,2,2,2,64,512]{5,4,3,2,1,0:T(8,128)(2,1)S(1)}, bf16[2,2,2,2,64,512]{5,4,3,2,1,0:T(8,128)(2,1)}, u32[]{:S(2)}, u32[]{:S(2)}) collective-permute-start(bf16[2,2,2,2,64,512]{5,4,3,2,1,0:T(8,128)(2,1)S(1)} %get-tuple-element.239), channel_id=1, source_target_pairs={{0,1},{1,0},{2,3},{3,2},{4,5},{5,4},{6,7},{7,6},{8,9},{9,8},{10,11... | collective-permute-start | bytes 3145736 | tf_op jit(solution)/shard_map/ppermute | solution.py:576
  181.8 8.8 %collective-permute-start.16 = (bf16[2,128,512]{2,1,0:T(8,128)(2,1)S(1)}, bf16[2,128,512]{2,1,0:T(8,128)(2,1)S(1)}, u32[]{:S(2)}, u32[]{:S(2)}) collective-permute-start(bf16[2,128,512]{2,1,0:T(8,128)(2,1)S(1)} %pad_maximum_fusion.3), channel_id=1, source_target_pairs={{0,8},{4,12},{8,0},{12,4},{1,9},{5,13},{9,1},{13,5},{2,10},{6,14},... | collective-permute-start | bytes 786440 | tf_op jit(solution)/shard_map/ppermute | solution.py:576
  190.6 21.5 %all-to-all-start.5 = ((bf16[4,4,64,512]{3,2,1,0:T(8,128)(2,1)}), bf16[4,4,64,512]{3,2,1,0:T(8,128)(2,1)S(1)}, u32[]{:S(2)}, u32[]{:S(2)}) async-start(bf16[4,4,64,512]{3,2,1,0:T(8,128)(2,1)} %backward_input.1), calls=%async_computation.5 | async-start | bytes 2097152 | tf_op jit(solution)/shard_map/all_to_all | solution.py:798
  196.5 15.0 %collective-permute-start.17 = (bf16[2,2,2,64,512]{4,3,2,1,0:T(8,128)(2,1)}, bf16[2,2,2,64,512]{4,3,2,1,0:T(8,128)(2,1)S(1)}, u32[]{:S(2)}, u32[]{:S(2)}) collective-permute-start(bf16[2,2,2,64,512]{4,3,2,1,0:T(8,128)(2,1)} %get-tuple-element.274), channel_id=1, source_target_pairs={{0,2},{1,3},{2,0},{3,1},{4,6},{5,7},{6,4},{7,5},{8,10},{9,11},{10,... | collective-permute-start | bytes 1572872 | tf_op jit(solution)/shard_map/ppermute | solution.py:576
  198.0 12.2 %collective-permute-start.19 = (bf16[128,512]{1,0:T(8,128)(2,1)S(1)}, bf16[128,512]{1,0:T(8,128)(2,1)S(1)}, u32[]{:S(2)}, u32[]{:S(2)}) collective-permute-start(bf16[128,512]{1,0:T(8,128)(2,1)S(1)} %fusion.25), channel_id=1, source_target_pairs={{0,16},{16,0},{1,17},{17,1},{2,18},{18,2},{3,19},{19,3},{4,20},{20... | collective-permute-start | bytes 393224 | tf_op jit(solution)/shard_map/ppermute | solution.py:576
  199.6 10.4 %collective-permute-start.18 = (bf16[64,512]{1,0:T(8,128)(2,1)S(1)}, bf16[64,512]{1,0:T(8,128)(2,1)S(1)}, u32[]{:S(2)}, u32[]{:S(2)}) collective-permute-start(bf16[64,512]{1,0:T(8,128)(2,1)S(1)} %fusion.35), channel_id=1, source_target_pairs={{0,16},{16,0},{1,17},{17,1},{2,18},{18,2},{3,19},{19,3},{4,20},{20... | collective-permute-start | bytes 196616 | tf_op jit(solution)/shard_map/ppermute | solution.py:576
  201.3 37.1 %collective-permute-start.24 = (bf16[256,512]{1,0:T(8,128)(2,1)}, bf16[256,512]{1,0:T(8,128)(2,1)}, u32[]{:S(2)}, u32[]{:S(2)}) collective-permute-start(bf16[256,512]{1,0:T(8,128)(2,1)} %get-tuple-element.262), channel_id=1, source_target_pairs={{0,1},{1,0},{2,3},{3,2},{4,5},{5,4},{6,7},{7,6},{8,9},{9,8},{10,11... | collective-permute-start | bytes 786440 | tf_op jit(solution)/shard_map/ppermute | solution.py:576
  201.4 39.1 %collective-permute-start.25 = (bf16[256,512]{1,0:T(8,128)(2,1)}, bf16[256,512]{1,0:T(8,128)(2,1)}, u32[]{:S(2)}, u32[]{:S(2)}) collective-permute-start(bf16[256,512]{1,0:T(8,128)(2,1)} %get-tuple-element.263), channel_id=1, source_target_pairs={{0,2},{1,3},{2,0},{3,1},{4,6},{5,7},{6,4},{7,5},{8,10},{9,11},{10,... | collective-permute-start | bytes 786440 | tf_op jit(solution)/shard_map/ppermute | solution.py:576
  210.0 30.5 %collective-permute-start.26 = (bf16[256,512]{1,0:T(8,128)(2,1)}, bf16[256,512]{1,0:T(8,128)(2,1)}, u32[]{:S(2)}, u32[]{:S(2)}) collective-permute-start(bf16[256,512]{1,0:T(8,128)(2,1)} %get-tuple-element.264), channel_id=1, source_target_pairs={{0,3},{1,2},{2,1},{3,0},{4,7},{5,6},{6,5},{7,4},{8,11},{9,10},{10,... | collective-permute-start | bytes 786440 | tf_op jit(solution)/shard_map/ppermute | solution.py:576
  216.4 15.3 %all-to-all-start.6 = ((f32[8,1,1088]{2,1,0:T(1,128)}), f32[8,1,1088]{2,1,0:T(1,128)S(1)}, u32[]{:S(2)}, u32[]{:S(2)}) async-start(f32[8,1,1088]{2,1,0:T(1,128)} %copy.56), calls=%async_computation.6 | async-start | bytes 73728 | tf_op jit(solution)/shard_map/all_to_all | solution.py:805
  221.0 10.7 %collective-permute-start.20 = (bf16[2,2,64,512]{3,2,1,0:T(8,128)(2,1)S(1)}, bf16[2,2,64,512]{3,2,1,0:T(8,128)(2,1)S(1)}, u32[]{:S(2)}, u32[]{:S(2)}) collective-permute-start(bf16[2,2,64,512]{3,2,1,0:T(8,128)(2,1)S(1)} %fusion.21), channel_id=1, source_target_pairs={{0,4},{4,0},{8,12},{12,8},{1,5},{5,1},{9,13},{13,9},{2,6},{6,2},{1... | collective-permute-start | bytes 786440 | tf_op jit(solution)/shard_map/ppermute | solution.py:576
  232.8 7.7 %collective-permute-start.23 = (bf16[64,512]{1,0:T(8,128)(2,1)S(1)}, bf16[64,512]{1,0:T(8,128)(2,1)S(1)}, u32[]{:S(2)}, u32[]{:S(2)}) collective-permute-start(bf16[64,512]{1,0:T(8,128)(2,1)S(1)} %get-tuple-element.308), channel_id=1, source_target_pairs={{0,24},{4,28},{8,16},{12,20},{16,8},{20,12},{24,0},{28,4},{1,25},{... | collective-permute-start | bytes 196616 | tf_op jit(solution)/shard_map/ppermute | solution.py:810
  236.1 4.5 %collective-permute-start.22 = (bf16[64,512]{1,0:T(8,128)(2,1)S(1)}, bf16[64,512]{1,0:T(8,128)(2,1)S(1)}, u32[]{:S(2)}, u32[]{:S(2)}) collective-permute-start(bf16[64,512]{1,0:T(8,128)(2,1)S(1)} %get-tuple-element.309), channel_id=1, source_target_pairs={{0,8},{4,12},{8,0},{12,4},{16,24},{20,28},{24,16},{28,20},{1,9},{5... | collective-permute-start | bytes 196616 | tf_op jit(solution)/shard_map/ppermute | solution.py:810
  238.5 5.9 %collective-permute-start.21 = (bf16[64,512]{1,0:T(8,128)(2,1)S(1)}, bf16[64,512]{1,0:T(8,128)(2,1)S(1)}, u32[]{:S(2)}, u32[]{:S(2)}) collective-permute-start(bf16[64,512]{1,0:T(8,128)(2,1)S(1)} %get-tuple-element.310), channel_id=1, source_target_pairs={{0,16},{4,20},{8,24},{12,28},{16,0},{20,4},{24,8},{28,12},{1,17},{... | collective-permute-start | bytes 196616 | tf_op jit(solution)/shard_map/ppermute | solution.py:810
  (21 other events, 112.7 us)

commit v2 on v1

--- a/solution.py
+++ b/solution.py
@@ -132,24 +132,18 @@
         out_ref[d * 256 : (d + 1) * 256] = swap(matrix, got_ref[:, d].reshape(256, 512))
 
 
-def each_feature(body):
-    lax.fori_loop(0, 4, lambda e, carry: (body(e), carry)[1], 0)
-
-
 def project_queries(x_ref, gain_ref, shift_ref, w_ref, b_ref, act_ref, q_ref):
-    def body(e):
-        unit, _ = norm_parts(x_ref[:, e].reshape(256, 512).astype(F32))
-        act = (unit * gain_ref[...] + shift_ref[...]).astype(BF)
-        act_ref[e] = act
-        q = (mm(act, w_ref[:, :512]) + b_ref[:, :512]).astype(BF)
-        q_ref[e] = q * jnp.asarray(SCALE, BF)
-
-    each_feature(body)
+    unit, _ = norm_parts(x_ref[:, 0].reshape(256, 512).astype(F32))
+    act = (unit * gain_ref[...] + shift_ref[...]).astype(BF)
+    act_ref[0] = act
+    q = (mm(act, w_ref[:, :512]) + b_ref[:, :512]).astype(BF)
+    q_ref[0] = q * jnp.asarray(SCALE, BF)
 
 
 def forward_one(
-    me_ref, q_ref, own_ref, got_ref, tasks_ref, context_ref, gain_ref, shift_ref, w_ref, b_ref,
-    oa_ref, ob_ref, c_ref, cact_ref, k_ref, v_ref, p_ref,
+    me_ref, q_ref, own_ref, got_ref, x_ref, tasks_ref, context_ref, gain_ref, shift_ref, w_ref,
+    b_ref, wm_ref, off_ref,
+    r_ref, o_ref, c_ref, cact_ref, k_ref, v_ref, p_ref,
 ):
     here = me_ref[1] == me_ref[2]
     masks = head_masks(BF)
@@ -163,21 +157,18 @@
     def _():
         c_ref[...] = got_ref[...]
 
-    unit, _ = norm_parts(c_ref[...].reshape(256, 512).astype(F32))
+    unit, _ = norm_parts(c_ref[0].astype(F32))
     act = (unit * gain_ref[...] + shift_ref[...]).astype(BF)
-    cact_ref[...] = act.reshape(4, 64, 512)
+    cact_ref[0] = act
     kv = mm(act, w_ref[:, 512:])
-    k_ref[...] = kv[:, :512].astype(BF).reshape(4, 64, 512)
-    v_ref[...] = (kv[:, 512:] + b_ref[:, 512:]).astype(BF).reshape(4, 64, 512)
-
-    def body(e):
-        out, prob = attend(q_ref[e], k_ref[e], v_ref[e], masks, allow)
-        out = out.reshape(4, 4, 2, 8, 512)
-        oa_ref[:, :, e] = out[:, :, 0].astype(BF)
-        ob_ref[:, :, e] = out[:, :, 1].astype(BF)
-        p_ref[e] = prob
-
-    each_feature(body)
+    k = kv[:, :512].astype(BF)
+    v = (kv[:, 512:] + b_ref[:, 512:]).astype(BF)
+    k_ref[0], v_ref[0] = k, v
+    out, prob = attend(q_ref[0], k, v, masks, allow)
+    o_ref[0] = out.astype(BF)
+    p_ref[0] = prob
+    r1 = x_ref[:, 0].reshape(256, 512).astype(F32) + mm(o_ref[0], wm_ref[...]) + off_ref[...]
+    r_ref[:, :, 0] = r1.astype(BF).reshape(4, 4, 16, 512)
 
 
 HALF = 512
@@ -185,41 +176,41 @@
 
 def middle(me_ref, *refs):
     (
-        o1_ref, x0, x1, x2, x3, c0, c1, c2, c3,
-        off1_ref, g2_ref, s2_ref, bf_ref, off2_ref, g3_ref, s3_ref, be_ref, br_ref,
-    ) = refs[:18]
-    weights_hbm = refs[18:23]
-    refs = refs[-44:]
-    gb1_ref, vec_ref, bias_ref = refs[:3]
-    outs_hbm, kept_hbm = refs[3:7], refs[7:15]
-    wm1_ref, wf_ref, wm2_ref, we_ref, wr_ref = refs[15:20]
-    kept = refs[20:28]
-    a2_ref, dqkv_ref, o2_ref, gb2_ref, a3_ref, gu_ref, hid_ref, gb3_ref = kept
+        r1_ref, c0, c1, c2, c3, g2_ref, s2_ref, bf_ref, off2_ref, g3_ref, s3_ref, be_ref, br_ref,
+    ) = refs[:13]
+    weights_hbm = refs[13:17]
+    gb1_ref, vec_ref, bias_ref, out0, out1, out2, out3 = refs[17:24]
+    targets = refs[24:28]
+    wf_ref, wm2_ref, we_ref, wr_ref = refs[28:32]
+    kept = refs[32:40]
     (
-        o_scr, q_scr, k_scr, v_scr, p_scr, e_scr, gs_scr, go_scr, out_scr, back_scr,
-        out0, out1, out2, out3, in_sems, out_sems,
-    ) = refs[28:]
+        r_scr, g_scr, q_scr, k_scr, v_scr, p_scr, e_scr, gs_scr, go_scr, out_scr, back_scr,
+        part_p, part_q, turn, in_sems, out_sems,
+    ) = refs[40:]
+    me, step = me_ref[0], pl.program_id(0)
+    tokens = pl.ds(pl.multiple_of(step * HALF, HALF), HALF)
+    a2_ref, dqkv_ref, o2_ref, gb2_ref, a3_ref, gu_ref, hid_ref, gb3_ref = (
+        ref.at[tokens] for ref in kept
+    )
     loads = [
         pltpu.make_async_copy(source, target, in_sems.at[i])
-        for i, (source, target) in enumerate(zip(weights_hbm, refs[15:20]))
+        for i, (source, target) in enumerate(zip(weights_hbm, refs[28:32]))
     ]
-    for load in loads:
-        load.start()
-    stores = []
-
-    def store(source, target, i):
-        stores.append(pltpu.make_async_copy(source, target, out_sems.at[i]))
-        stores[-1].start()
-
-    def keep(ref):
-        i = next(j for j in range(8) if kept[j] is ref)
-        store(ref, kept_hbm[i], i)
-
-    me = me_ref[0]
-    matrix = swap_matrix(8)
+
+    def first(make):
+        pl.when(step == 0)(make)
+
+    matrix = swap_matrix()
     masks, masks32 = head_masks(BF), head_masks(F32)
-    for f in range(4):
-        o_scr[f] = swap(matrix, o1_ref[:, f].reshape(128, 512), True)
+
+    @first
+    def _():
+        loads[0].start()
+        loads[1].start()
+        for f in range(4):
+            r_scr[f] = swap(matrix, r1_ref[:, f].reshape(256, 512))
+
+    now = pl.ds(pl.multiple_of(step * 128, 128), 128)
 
     def gather(*refs):
         return jnp.concatenate(
@@ -242,15 +233,17 @@
 
         lax.fori_loop(0, 8 // SAMPLE_UNROLL, step, 0)
 
-    attended = gather(*(o_scr.at[d ^ me] for d in range(4)))
     gb3_ref[...] = gather(c0, c1, c2, c3)
-    keep(gb3_ref)
-    loads[0].wait()
-    r1 = gather(x0, x1, x2, x3).astype(F32) + mm(attended, wm1_ref[...]) + off1_ref[...]
+    r1 = gather(*(r_scr.at[d ^ me, now] for d in range(4))).astype(F32)
     unit2, inv2 = norm_parts(r1)
     a2_ref[...] = (unit2 * g2_ref[...] + s2_ref[...]).astype(BF)
-    keep(a2_ref)
-    loads[1].wait()
+
+    @first
+    def _():
+        loads[0].wait()
+        loads[2].start()
+        loads[3].start()
+
     q = (mm(a2_ref[...], wf_ref[:, :512]) + bf_ref[:, :512]).astype(BF)
     q_scr[...] = q * jnp.asarray(SCALE, BF)
     k_scr[...] = mm(a2_ref[...], wf_ref[:, 512:1024]).astype(BF)
@@ -272,14 +265,18 @@
         ).astype(BF)
 
     each_sample(mix)
-    keep(o2_ref)
-    loads[2].wait()
+    first(loads[1].wait)
     r2 = r1 + mm(o2_ref[...], wm2_ref[...]) + off2_ref[...]
     unit3, inv3 = norm_parts(r2)
     a3_ref[...] = (unit3 * g3_ref[...] + s3_ref[...]).astype(BF)
-    keep(a3_ref)
-    loads[3].wait()
-    loads[4].wait()
+    first(loads[2].wait)
+    first(loads[3].wait)
+
+    @first
+    def _():
+        vec_ref[...] = jnp.zeros((8, 512), F32)
+        bias_ref[...] = jnp.zeros((1, 2048), F32)
+
     out_scr[...] = r2 + br_ref[...]
     back_scr[...] = jnp.zeros((HALF, 512), F32)
 
@@ -292,23 +289,17 @@
         gh = mm(gb3_ref[...], wr_ref[cols, :], 1, 1).astype(BF).astype(F32)
         gu = (gh * (cdf + u * density)).astype(BF)
         gu_ref[:, cols] = gu
-        bias_ref[:, cols] = col_sum(gu)
+        bias_ref[:, cols] += col_sum(gu)
         out_scr[...] += mm(hidden, wr_ref[cols, :])
         back_scr[...] += mm(gu, we_ref[:, cols], 1, 1)
         return carry
 
     lax.fori_loop(0, 2048 // WIDE, expand, 0, unroll=EXPAND_UNROLL)
-    keep(hid_ref)
-    keep(gu_ref)
     scatter(out_scr[...].astype(BF), out0, out1, out2, out3)
-    rows = pl.ds(pl.multiple_of(me_ref[8] * 128, 128), 128)
-    for i, ref in enumerate((out0, out1, out2, out3)):
-        store(ref, outs_hbm[i].at[rows], 8 + i)
     back, cot = back_scr[...], gb3_ref[...]
     vecs = [col_sum(back * unit3), col_sum(back)]
     gr2 = cot.astype(F32) + norm_back(back, unit3, inv3, g3_ref[...])
     gb2_ref[...] = gr2.astype(BF)
-    keep(gb2_ref)
     go_scr[...] = mm(gb2_ref[...], wm2_ref[...], 1, 1).astype(BF)
 
     def weigh(rows, cols):
@@ -331,81 +322,93 @@
         dqkv_ref[rows, 1024 + at : 1024 + at + QUAD] = dv.astype(BF)
 
     each_sample(spread)
-    keep(dqkv_ref)
     dqkv = dqkv_ref[...]
     back = mm(dqkv, wf_ref[...], 1, 1)
     vecs += [col_sum(back * unit2), col_sum(back)]
     gr1 = gr2 + norm_back(back, unit2, inv2, g2_ref[...])
-    scatter(gr1.astype(BF), *(o_scr.at[d ^ me] for d in range(4)))
-    for f in range(4):
-        gb1_ref[:, f] = swap(matrix, o_scr[f]).reshape(4, 4, 8, 512)
+    scatter(gr1.astype(BF), *(g_scr.at[d ^ me, now] for d in range(4)))
     vecs += [
         col_sum(gb2_ref[...]), col_sum(cot), col_sum(dqkv[:, :512]), col_sum(dqkv[:, 1024:])
     ]
-    vec_ref[...] = jnp.concatenate(vecs, axis=0)
-    for copy in stores:
-        copy.wait()
+    vec_ref[...] += jnp.concatenate(vecs, axis=0)
+
+    @pl.when(step == 1)
+    def _():
+        for f in range(4):
+            gb1_ref[:, f] = swap(matrix, g_scr[f]).reshape(4, 4, 16, 512)
+        grads_middle(me_ref, kept, (part_p, part_q), turn, targets, out_sems)
 
 
 SAMPLE_UNROLL = 8
-EXPAND_UNROLL = False
+EXPAND_UNROLL = True
 WIDE = 512
 
 
 def backward_one(
-    ga_ref, gb_ref, x_ref, c_ref, q_ref, k_ref, v_ref, p_ref, w_ref, wm_ref,
-    gb1_ref, a_ref, dq_ref, dkv_ref, term_ref, vec_ref,
-    g_scr,
+    me_ref, g_ref, o_ref, act_ref, cact_ref, x_ref, c_ref, q_ref, k_ref, v_ref,
+    p_ref, w_ref, wm_ref,
+    gb1_ref, a_ref, term_ref, vec_ref, keep_ref, send_ref,
+    dq_scr, dkv_scr, g_scr,
 ):
     masks, masks32 = head_masks(BF), head_masks(F32)
-    vec_ref[...] = jnp.zeros((8, 512), F32)
-
-    def body(e):
-        g_scr[:, :, 0] = ga_ref[:, :, e]
-        g_scr[:, :, 1] = gb_ref[:, :, e]
-        gb1 = g_scr[...].reshape(256, 512)
-        gb1_ref[e] = gb1
-        go = mm(gb1, wm_ref[...], 1, 1).astype(BF)
-        dq, dk, dv = attend_back(q_ref[e], k_ref[e], v_ref[e], p_ref[e], go, masks, masks32)
-        dq_ref[e], dkv_ref[e, :, :512], dkv_ref[e, :, 512:] = dq, dk, dv
-        back = mm(dq, w_ref[:, :512], 1, 1)
-        a_ref[e] = back
-        unit, _ = norm_parts(x_ref[:, e].reshape(256, 512).astype(F32))
-        vec_ref[0:1] += col_sum(back * unit)
-        vec_ref[1:2] += col_sum(back)
-        vec_ref[2:3] += col_sum(gb1)
-        vec_ref[3:4] += col_sum(dq)
-
-    each_feature(body)
-    dkv = dkv_ref[...].reshape(256, 1024)
+
+    @pl.when(pl.program_id(0) == 0)
+    def _():
+        vec_ref[...] = jnp.zeros((8, 512), F32)
+
+    gb1 = g_ref[:, :, 0].reshape(256, 512)
+    gb1_ref[0] = gb1
+    go = mm(gb1, wm_ref[...], 1, 1).astype(BF)
+    dq, dk, dv = attend_back(q_ref[0], k_ref[0], v_ref[0], p_ref[0], go, masks, masks32)
+    dkv = jnp.concatenate([dk, dv], axis=1)
+    step = pl.program_id(0)
+    rows = pl.ds(pl.multiple_of(step * 256, 256), 256)
+    dq_scr[rows], g_scr[rows] = dq, gb1
+    dkv_scr[pl.ds(pl.multiple_of(step * 64, 64), 64)] = dkv
+
+    @pl.when(step == 3)
+    def _():
+        whole_rows = lambda ref: ref[...].reshape(-1, 512)
+        act_c = whole_rows(cact_ref)
+        terms = (
+            (whole_rows(act_ref), dq_scr[...]), (act_c, dkv_scr[:, :512]),
+            (act_c, dkv_scr[:, 512:]), (whole_rows(o_ref), g_scr[...]),
+        )
+        for unit, (left, right) in enumerate(terms):
+            place_sample(me_ref, mm(left, right, 0, 0).astype(BF), unit, keep_ref, send_ref)
+
+    back = mm(dq, w_ref[:, :512], 1, 1)
+    a_ref[0] = back
     term = mm(dkv, w_ref[:, 512:], 1, 1)
-    term_ref[...] = term.astype(BF).reshape(4, 64, 512)
-    unit, _ = norm_parts(c_ref[...].reshape(256, 512).astype(F32))
-    vec_ref[0:1] += col_sum(term * unit)
-    vec_ref[1:2] += col_sum(term)
-    vec_ref[4:5] = col_sum(dkv[:, 512:])
+    term_ref[0] = term.astype(BF)
+    unit, _ = norm_parts(x_ref[:, 0].reshape(256, 512).astype(F32))
+    unit_c, _ = norm_parts(c_ref[0].astype(F32))
+    zero = jnp.zeros((3, 512), F32)
+    vec_ref[...] += jnp.concatenate(
+        [
+            col_sum(back * unit) + col_sum(term * unit_c), col_sum(back) + col_sum(term),
+            col_sum(gb1), col_sum(dq), col_sum(dv), zero,
+        ],
+        axis=0,
+    )
 
 
 def backward_input(me_ref, gb1_ref, x_ref, a_ref, term_ref, got_ref, gain_ref, grad_ref, a_scr):
     here, quad = me_ref[1] == me_ref[2], me_ref[3]
-
-    def body(e):
-        unit, inverse = norm_parts(x_ref[:, e].reshape(256, 512).astype(F32))
-        a_scr[...] = a_ref[e].reshape(4, 64, 512)
-
-        @pl.when(here)
-        def _():
-            a_scr[quad] += term_ref[e].astype(F32) + got_ref[e].astype(F32)
-
-        back = a_scr[...].reshape(256, 512)
-        grad = gb1_ref[e].astype(F32) + norm_back(back, unit, inverse, gain_ref[...])
-        grad_ref[:, e] = grad.astype(BF).reshape(4, 64, 512)
-
-    each_feature(body)
+    unit, inverse = norm_parts(x_ref[:, 0].reshape(256, 512).astype(F32))
+    a_scr[...] = a_ref[0].reshape(4, 64, 512)
+
+    @pl.when(here)
+    def _():
+        a_scr[quad] += term_ref[0].astype(F32) + got_ref[0].astype(F32)
+
+    back = a_scr[...].reshape(256, 512)
+    grad = gb1_ref[0].astype(F32) + norm_back(back, unit, inverse, gain_ref[...])
+    grad_ref[:, 0] = grad.astype(BF).reshape(4, 64, 512)
 
 
 def split(got_ref, out_ref):
-    rest = jnp.sum(got_ref[...], axis=0, keepdims=True)
+    rest = got_ref[...]
     out_ref[...] = jnp.zeros_like(out_ref)
     for i in range(3):
         term = rest.astype(BF)
@@ -418,93 +421,81 @@
         out_ref[d ^ me_ref[0]] = ref[...]
 
 
-def lay_out(me_ref, read, order, *pairs):
+def piece_index(me_ref, unit, shard, order):
     core, xx, yy, zz = me_ref[4], me_ref[5], me_ref[6], me_ref[7]
-    for bits in range(16):
-        index = tuple((bits >> i) & 1 for i in (3, 2, 1, 0))
-        dx, dy, d1, d2 = (index[order.index(name)] for name in ("x", "y", "z", "w"))
-        shard = (zz ^ d1 ^ (2 * d2)) * 2 + (yy ^ dy)
-        for keep_ref, send_ref, start, rows in pairs:
-            keep_ref[index] = read(2 * core + (dx ^ xx), shard, start, rows)
-            send_ref[index] = read(2 * (1 - core) + (dx ^ xx), shard, start, rows)
-
-
-def read_units(scr):
-    def read(unit, shard, start, rows):
-        return scr[unit, pl.ds(pl.multiple_of(shard * 64 + start, rows), rows)]
-
-    return read
-
-
-def grads_middle(me_ref, *refs):
-    sources, targets, held, staged = refs[:16], refs[16:22], refs[22:30], refs[30:36]
-    scr, in_sems, out_sems = refs[36:]
-    loads = []
-    for i in range(16):
-        rows = pl.ds((i % 2) * 512, 512)
-        loads.append(
-            pltpu.make_async_copy(sources[i], held[i // 2].at[rows], in_sems.at[i])
-        )
-        loads[-1].start()
+    other_z = (shard >> 1) ^ zz
+    bit = {
+        "x": (unit & 1) ^ xx, "y": (shard & 1) ^ yy, "z": other_z & 1, "w": other_z >> 1,
+    }
+    index = sum(bit[name] * weight for name, weight in zip(order, (8, 4, 2, 1)))
+    return (unit >> 1) ^ core, index
+
+
+def grads_middle(me_ref, kept, staged, turn, targets, out_sems):
+    act2, dqkv, o2, gb2, act3, gu, hid, gb3 = kept
     stores = []
 
-    def wait(*places):
-        for place in places:
-            loads[2 * place].wait()
-            loads[2 * place + 1].wait()
-
-    def put(part, order):
-        lay_out(me_ref, read_units(scr), order, (staged[2 * part], staged[2 * part + 1], 0, 64))
-        for i in (2 * part, 2 * part + 1):
-            stores.append(pltpu.make_async_copy(staged[i], targets[i], out_sems.at[i]))
+    def put(part):
+        for i in range(2):
+            source = staged[part].at[pl.ds(16 * i, 16)]
+            place = 2 * part + i
+            stores.append(pltpu.make_async_copy(source, targets[place], out_sems.at[place]))
             stores[-1].start()
-
-    gb3, hid, act3, gu, act2, dqkv, o2, gb2 = held
-    wait(0, 1)
 
     def loop(count, body):
         lax.fori_loop(0, count, lambda n, carry: (body(n), carry)[1], 0)
 
     block = lambda n: pl.ds(pl.multiple_of(n * 512, 512), 512)
 
+    def place_piece(part, value, unit, shard, rows):
+        send, index = piece_index(me_ref, unit, shard, ("xyzw", "yxzw")[part])
+        staged[part][send * 16 + index, rows] = value
+
+    def place_unit(part, value, unit):
+        for shard in range(8):
+            place_piece(part, value[shard * 64 : (shard + 1) * 64], unit, shard, slice(0, 64))
+
     def from_hidden(n):
-        piece = mm(hid[:, block(n)], gb3[...], 0, 0).astype(BF).reshape(2, 4, 64, 512)
-        for i in range(2):
-            rows = pl.ds(pl.multiple_of((2 * n + i) * 64, 64), 64)
-            for unit in range(4):
-                scr[unit, rows] = piece[i, unit]
+        piece = mm(hid[:, block(n)], gb3[...], 0, 0).astype(BF)
+        for i in range(8):
+            for part in range(2):
+                at = i * 64 + part * 32
+                rows = piece[at : at + 32]
+                place_piece(part, rows, i % 4, 2 * n + i // 4, slice(64, 96))
 
     loop(4, from_hidden)
-    put(0, "zxyw")
-    wait(2, 3)
+    turn[...] = act3[...].T
 
     def from_expand(n):
-        scr[n] = mm(act3[...], gu[:, block(n)], 0, 0).astype(BF)
+        place_unit(1, mm(turn[...], gu[:, block(n)]).astype(BF), n)
 
     loop(4, from_expand)
-    put(1, "yxzw")
-    wait(4, 5, 6, 7)
+    put(1)
+    turn[...] = act2[...].T
 
     def from_feature(n):
-        scr[n] = mm(act2[...], dqkv[:, block(n)], 0, 0).astype(BF)
+        place_unit(0, mm(turn[...], dqkv[:, block(n)]).astype(BF), n)
 
     loop(3, from_feature)
-    scr[3] = mm(o2[...], gb2[...], 0, 0).astype(BF)
-    put(2, "xyzw")
+    place_unit(0, mm(o2[...], gb2[...], 0, 0).astype(BF), 3)
+    put(0)
     for store in stores:
         store.wait()
 
 
-def grads_sample(
-    me_ref, act_ref, dq_ref, cact_ref, dkv_ref, oa_ref, ga_ref, ob_ref, gb_ref,
-    keep_ref, send_ref, scr,
-):
-    scr[0] = mm(act_ref[...], dq_ref[...], 0, 0).astype(BF)
-    scr[1] = mm(cact_ref[...], dkv_ref[:, :512], 0, 0).astype(BF)
-    scr[2] = mm(cact_ref[...], dkv_ref[:, 512:], 0, 0).astype(BF)
-    total = mm(oa_ref[...], ga_ref[...], 0, 0) + mm(ob_ref[...], gb_ref[...], 0, 0)
-    scr[3] = total.astype(BF)
-    lay_out(me_ref, read_units(scr), "xyzw", (keep_ref, send_ref, 0, 64))
+def place_sample(me_ref, value, unit, keep_ref, send_ref):
+    for which, order in enumerate(("xyzw", "yxzw")):
+        for shard in range(8):
+            at = shard * 64 + which * 32
+            send, index = piece_index(me_ref, unit, shard, order)
+
+            @pl.when(send == 0)
+            def _(at=at, index=index):
+                keep_ref[which, index] = value[at : at + 32]
+
+            @pl.when(send == 1)
+            def _(at=at, index=index):
+                send_ref[which, index] = value[at : at + 32]
 
 
 def spec(shape, index=None):
@@ -542,6 +533,37 @@
 def whole_block(out):
     shape = out.shape
     return pl.BlockSpec(shape, lambda i: (0,) * len(shape))
+
+
+def moving_block(shape, axis):
+    block = tuple(1 if i == axis else n for i, n in enumerate(shape))
+    return pl.BlockSpec(block, lambda i: tuple(i if j == axis else 0 for j in range(len(shape))))
+
+
+def by_feature(kernel, name, limit, outs, scratch, *inputs, time=3):
+    arrays, specs = [], []
+    for entry in inputs:
+        array, axis = entry if isinstance(entry, tuple) else (entry, None)
+        if array.ndim == 1:
+            arrays.append(array)
+            specs.append(pl.BlockSpec(memory_space=pltpu.SMEM))
+            continue
+        arrays.append(outside(array))
+        specs.append(whole_block(array) if axis is None else moving_block(array.shape, axis))
+    return pl.pallas_call(
+        kernel,
+        grid=(4,),
+        out_shape=tuple(out for out, _ in outs),
+        in_specs=specs,
+        out_specs=[
+            whole_block(out) if axis is None else moving_block(out.shape, axis)
+            for out, axis in outs
+        ],
+        scratch_shapes=scratch,
+        compiler_params=params(limit),
+        cost_estimate=cost(time),
+        name=name,
+    )(*arrays)
 
 
 def whole(kernel, name, limit, outs, scratch, *inputs, steps=1, time=3):
@@ -630,32 +652,37 @@
     me = jnp.stack(me).astype(jnp.int32)
 
     turned = whole(turn_in, "turn_in", 8, big((16, 4, 16, 512)), [], layer_input.reshape(1024, 512))
-    turned, layer_input, cotangent = fence((turned, layer_input, cotangent))
+    turned, cotangent = fence((turned, cotangent))
     x_t = lax.all_to_all(turned.reshape(4, 4, 64, 512), "quad", 0, 0)
-    x4, cot4 = layer_input.reshape(4, 256, 512), cotangent.reshape(4, 256, 512)
+    cot4 = cotangent.reshape(4, 256, 512)
     block = lambda value, d: at(value, feat ^ d)
-    to_core = jnp.stack([block(x4, 1), block(cot4, 1), block(x4, 3), block(cot4, 3)])
-    from_core = shuffle(to_core, *CORE)
-    x_far = shuffle(jnp.stack([block(x4, 2), from_core[2]]), *X)
-    x_t, from_core, x_far = fence((x_t, from_core, x_far))
-    cot_far = shuffle(jnp.stack([block(cot4, 2), from_core[3]]), *X)
+    from_core = shuffle(jnp.stack([block(cot4, 1), block(cot4, 3)]), *CORE)
+    cot_far = shuffle(jnp.stack([block(cot4, 2), from_core[1]]), *X)
+    x_t, from_core, cot_far = fence((x_t, from_core, cot_far))
     own_context = at(x_t, root % 4)
     got_context = shuffle(own_context, *W)
-    act1, queries = whole(
-        project_queries, "project_queries", 16, (big((4, 256, 512)), big((4, 256, 512))), [],
-        x_t, row(first_gain), row(first_shift), sample_weight, row(sample_bias),
-    )
-    cot_far, got_context, q1 = fence((cot_far, got_context, queries))
+    full = big((4, 256, 512))
+    act1, queries = by_feature(
+        project_queries, "project_queries", 12, ((full, 0), (full, 0)), [],
+        (x_t, 1), row(first_gain), row(first_shift), sample_weight, row(sample_bias),
+    )
+    got_context, q1 = fence((got_context, queries))
 
     tasks = segment_ids.reshape(8, 64)
     context_tasks = jnp.concatenate([at(tasks, root)] * 4).reshape(1, 256)
-    sent = big((4, 4, 4, 8, 512))
+    sent = big((4, 4, 4, 16, 512))
     four = big((4, 64, 512))
-    oa, ob, context, cact, k1, v1, p1 = whole(
-        forward_one, "forward_one", 24,
-        (sent, sent, four, four, four, four, big((4, 256, 512), F32)), [],
-        me, q1, own_context, got_context, at(segment_ids.reshape(2, 256, 1), half), context_tasks,
-        row(first_gain), row(first_shift), sample_weight, row(sample_bias), time=7,
+    r1, o1, context, cact, k1, v1, p1 = by_feature(
+        forward_one, "forward_one", 20,
+        (
+            (sent, 2), (full, 0), (four, 0), (four, 0), (four, 0), (four, 0),
+            (big((4, 256, 512), F32), 0),
+        ),
+        [],
+        me, (q1, 0), (own_context, 0), (got_context, 0), (x_t, 1),
+        at(segment_ids.reshape(2, 256, 1), half), context_tasks,
+        row(first_gain), row(first_shift), sample_weight, row(sample_bias), sample_mixer,
+        row(sample_offset), time=7,
     )
 
     def exchange(value):
@@ -666,106 +693,76 @@
     rows_in = [
         row(v)
         for v in (
-            sample_offset, second_gain, second_shift, feature_bias, feature_offset, third_gain,
+            second_gain, second_shift, feature_bias, feature_offset, third_gain,
             third_shift, expand_bias, reduce_bias,
         )
     ]
-    weights = [sample_mixer, feature_weight, feature_mixer, expand_weight, reduce_weight]
-
-    def run_middle(half, attended, earlier):
-        own = spec((None, 128, 512), lambda i, m: (m[0], m[8], 0))
-        part = lambda n: spec((None, 128, 512), lambda i, m: (n, m[8], 0))
-        outs = (sent, sds((8, 512), F32), sds((1, 2048), F32))
-        blocks = ((256, 512),) * 4
-        kept = tuple((HALF, n) for n in (512, 1536, 512, 512, 512, 2048, 2048, 512))
-        still = lambda shape: spec(shape, lambda i, m: (0,) * len(shape))
-        far = pl.BlockSpec(memory_space=pl.ANY)
-        vmem = lambda shape, dtype=BF: pltpu.VMEM(shape, dtype)
-        rows, rows32 = vmem((HALF, 512)), vmem((HALF, 512), F32)
-        return pl.pallas_call(
-            middle,
-            grid_spec=pltpu.PrefetchScalarGridSpec(
-                num_scalar_prefetch=1,
-                grid=(1,),
-                in_specs=[still((4, 4, 4, 8, 512))]
-                + [own, part(0), part(0), part(1), own, part(1), part(0), part(1)]
-                + [still(r.shape) for r in rows_in]
-                + [far] * (5 + len(earlier)),
-                out_specs=[still(o.shape) for o in outs] + [far] * 12,
-                scratch_shapes=[vmem(w.shape) for w in weights]
-                + [vmem(shape) for shape in kept]
-                + [
-                    vmem((4, 128, 512)), rows, rows, rows, rows32, rows32, rows, rows, rows32,
-                    rows32, *(vmem((128, 512)) for _ in range(4)),
-                    pltpu.SemaphoreType.DMA((5,)), pltpu.SemaphoreType.DMA((12,)),
-                ],
-            ),
-            out_shape=outs + tuple(big(shape) for shape in blocks + kept),
-            input_output_aliases={24 + i: 3 + i for i in range(len(earlier))},
-            compiler_params=params(44),
-            cost_estimate=cost(30),
-            name="middle",
-        )(
-            jnp.concatenate([me, jnp.full((1,), half, jnp.int32)]),
-            *(
-                outside(array)
-                for array in (
-                    attended, x4, from_core, x_far, x_far, cot4, from_core, cot_far, cot_far,
-                    *rows_in, *weights, *earlier,
-                )
-            ),
-        )
-
-    oa_f, ob = fence((exchange(oa), ob))
-    ob_f = exchange(ob)
-    ga, vec_a, bias_a, *first = run_middle(0, oa_f, [])
-    ob_f, ga, first = fence((ob_f, ga, first))
-    ga_t = exchange(ga)
-    gb, vec_b, bias_b, *second = run_middle(1, ob_f, first[:4])
-    ga_t, gb, second = fence((ga_t, gb, second))
-    out0, out1, out2, out3 = second[:4]
-    act2, dqkv, o2, gb2, act3, gu, hidden, gb3 = zip(first[4:], second[4:])
-    gb_t = exchange(gb)
-    vec2, bias2 = vec_a + vec_b, bias_a + bias_b
-
-    parts = sds((2, 2, 2, 2, 64, 512))
-    units = [pltpu.VMEM((4, 512, 512), BF)]
+    weights = [feature_weight, feature_mixer, expand_weight, reduce_weight]
+
+    own = spec((None, 128, 512), lambda i, m: (m[0], i, 0))
+    part = lambda n: spec((None, 128, 512), lambda i, m: (n, i, 0))
+    still = lambda shape: spec(shape, lambda i, m: (0,) * len(shape))
+    block = spec((128, 512), lambda i, m: (i, 0))
     far = pl.BlockSpec(memory_space=pl.ANY)
-    sources = [*gb3, *hidden, *act3, *gu, *act2, *dqkv, *o2, *gb2]
-    widths = (512, 2048, 512, 2048, 512, 1536, 512, 512)
-    rk, rs, ek, es, fk, fs = pl.pallas_call(
-        grads_middle,
-        grid=(1,),
-        out_shape=(parts,) * 6,
-        in_specs=[pl.BlockSpec(memory_space=pltpu.SMEM)] + [far] * 16,
-        out_specs=[far] * 6,
-        scratch_shapes=[pltpu.VMEM((1024, n), BF) for n in widths]
-        + [pltpu.VMEM(parts.shape, BF)] * 6
-        + units
-        + [pltpu.SemaphoreType.DMA((16,)), pltpu.SemaphoreType.DMA((6,))],
-        compiler_params=params(32),
-        cost_estimate=cost(9),
-        name="grads_middle",
-    )(me, *(outside(a) for a in sources))
-    r_chain = Chain(rk, rs, (Z, X, Y, W))
-    e_chain = Chain(ek, es, (Y, X))
-    f_chain = Chain(fk, fs, (X, Y))
-    chains = [r_chain, e_chain, f_chain]
+    vmem = lambda shape, dtype=BF: pltpu.VMEM(shape, dtype)
+    rows, rows32 = vmem((HALF, 512)), vmem((HALF, 512), F32)
+    outs = (sent, sds((8, 512), F32), sds((1, 2048), F32))
+    gb1_f, vec2, bias2, out0, out1, out2, out3, *grads = pl.pallas_call(
+        middle,
+        grid_spec=pltpu.PrefetchScalarGridSpec(
+            num_scalar_prefetch=1,
+            grid=(2,),
+            in_specs=[
+                pl.BlockSpec(sent.shape, lambda i, m: (0,) * 5, pipeline_mode=pl.Buffered(1)),
+                own, part(0), part(0), part(1),
+            ]
+            + [still(r.shape) for r in rows_in]
+            + [far] * 4,
+            out_specs=[still(o.shape) for o in outs] + [block] * 4 + [far] * 4,
+            scratch_shapes=[vmem(w.shape) for w in weights]
+            + [vmem((1024, n)) for n in (512, 1536, 512, 512, 512, 2048, 2048, 512)]
+            + [
+                vmem((4, 256, 512)), vmem((4, 256, 512)), rows, rows, rows, rows32, rows32, rows,
+                rows, rows32, rows32, vmem((32, 96, 512)), vmem((32, 96, 512)), vmem((512, 1024)),
+                pltpu.SemaphoreType.DMA((4,)), pltpu.SemaphoreType.DMA((4,)),
+            ],
+        ),
+        out_shape=outs + (big((256, 512)),) * 4 + (sds((16, 96, 512)),) * 4,
+        compiler_params=params(58),
+        cost_estimate=cost(45),
+        name="middle",
+    )(
+        me,
+        *(
+            outside(array)
+            for array in (exchange(r1), cot4, from_core, cot_far, cot_far, *rows_in, *weights)
+        ),
+    )
+
+    gb_t = exchange(gb1_f)
+    outs = [shuffle(out, "feat", d + 1) for d, out in enumerate((out1, out2, out3))]
+    pk, ps, qk, qs = (g.reshape(2, 2, 2, 2, 96, 512) for g in grads)
+    p_chain, q_chain = Chain(pk, ps, (X, Y)), Chain(qk, qs, (Y, X))
+    chains = [p_chain, q_chain]
     for chain in chains:
         chain.take(chain.start())
 
-    full = big((4, 256, 512))
-    gb1, back, dq1, dkv, term, vec1 = together(
-        chains,
-        lambda: whole(
-            backward_one, "backward_one", 28,
+    half_rows = sds((2, 16, 32, 512))
+    for chain in chains:
+        chain.take(chain.start())
+    gb1, back, term, vec1, keep_ab, send_ab = (
+        lambda: by_feature(
+            backward_one, "backward_one", 32,
             (
-                full, big((4, 256, 512), F32), full, sds((4, 64, 1024)), four, sds((8, 512), F32),
+                (full, 0), (big((4, 256, 512), F32), 0), (four, 0), (sds((8, 512), F32), None),
+                (half_rows, None), (half_rows, None),
             ),
-            [pltpu.VMEM((4, 4, 2, 8, 512), BF)],
-            ga_t, gb_t, x_t, context, q1, k1, v1, p1, sample_weight, sample_mixer, time=10,
-        ),
-    )
+            [pltpu.VMEM((1024, 512), BF), pltpu.VMEM((256, 1024), BF), pltpu.VMEM((1024, 512), BF)],
+            me, (gb_t, 2), o1, act1, cact, (x_t, 1),
+            (context, 0), (q1, 0), (k1, 0), (v1, 0), (p1, 0), sample_weight, sample_mixer,
+            time=12,
+        )
+    )()
 
     owned = lambda v, n: v.reshape(-1, 8, n).transpose(1, 0, 2).reshape(8, -1)
     vectors = jnp.concatenate(
@@ -775,45 +772,56 @@
         ],
         axis=1,
     )
-    flat2 = lambda a: a.reshape(-1, a.shape[-1])
-    grads = whole(
-        grads_sample, "grads_sample", 20, (parts, parts), units,
-        me, *(flat2(a) for a in (act1, dq1, cact, dkv, oa, ga_t, ob, gb_t)),
-    )
-    got_term, grads = together(chains, lambda: (shuffle(term, *W), grads))
-    both = [jnp.concatenate([e_chain.keep[i], f_chain.keep[i]], axis=-2) for i in range(2)]
-    both_chain = Chain(both[0], both[1], (W,))
+    got_term = shuffle(term, *W)
+    got_term, got_ab = together(chains, lambda: (got_term, shuffle(send_ab, *CORE)))
+    bits = lambda a: a.reshape(2, 2, 2, 2, 2, 32, 512)
+    keep_ab, got_ab = bits(keep_ab), bits(got_ab)
+    late = []
+    for which, dims in enumerate(((X, Y), (Y, X))):
+        pair = [plus(keep_ab[which, i], got_ab[which, i]) for i in range(2)]
+        late.append(Chain(*pair, ()))
+        late[-1].dims = dims
+    both = [jnp.concatenate([chain.keep[i] for chain in chains], axis=-2) for i in range(2)]
+    both_chain = Chain(*both, ())
     both_chain.dims = (Z, W)
-    s_chain = Chain(*grads, (X, Y))
-    grad_t = together(
-        [s_chain, r_chain, both_chain],
-        lambda: whole(
-            backward_input, "backward_input", 24, big((4, 4, 64, 512)),
-            [pltpu.VMEM((4, 64, 512), F32)],
-            me, gb1, x_t, back, term, got_term, row(first_gain),
+    vectors = vectors.reshape(2, 2, 2, 1088)
+    (grad_t,), v = together(
+        late + [both_chain],
+        lambda: (
+            by_feature(
+                backward_input, "backward_input", 16, ((big((4, 4, 64, 512)), 1),),
+                [pltpu.VMEM((4, 64, 512), F32)],
+                me, (gb1, 0), (x_t, 1), (back, 0), (term, 0), (got_term, 0), row(first_gain),
+            ),
+            shuffle(at(vectors, 1 - samp % 2, 2), *Y),
         ),
     )
-    got, vectors = together(
-        [s_chain, r_chain, both_chain],
-        lambda: (lax.all_to_all(grad_t, "quad", 0, 0), vectors),
-    )
+    vectors = at(vectors, samp % 2, 2) + v
+    low = samp // 2 % 2
+    layer_output = whole(
+        place, "place", 16, sds((4, 256, 512)), [], me, out0, *outs
+    ).reshape(64, 16, 512)
+    got, v, layer_output = together(
+        late + [both_chain],
+        lambda: (
+            lax.all_to_all(grad_t, "quad", 0, 0),
+            shuffle(at(vectors, 1 - low, 1), *Z),
+            layer_output,
+        ),
+    )
+    vectors = at(vectors, low, 1) + v
     input_grad = whole(
         turn_out, "turn_out", 8, sds((1024, 512)), [], got.reshape(16, 4, 16, 512)
     ).reshape(64, 16, 512)
-    early = lax.all_gather(jnp.concatenate([both_chain.keep, r_chain.keep]), "feat")
-    input_grad, vectors, early = together(
-        [s_chain], lambda: (input_grad, lax.all_to_all(vectors, SAMP, 0, 0), early)
-    )
-    vectors = whole(split, "split", 8, sds((24, 1088)), [], vectors)
-
-    rows = s_chain.keep
+
+    rows = jnp.concatenate([chain.keep for chain in late], axis=2)
     around_z = lambda value, mask: lax.ppermute(value, SAMP, [(j, j ^ mask) for j in range(8)])
     from_z = [around_z(rows[i // 2, i % 2], (0, 4, 2, 6)[i]) for i in (1, 2, 3)]
-    outs = [shuffle(out, "feat", d + 1) for d, out in enumerate((out1, out2, out3))]
-    from_z, vectors, outs = fence((from_z, vectors, outs))
-    layer_output = whole(
-        place, "place", 16, sds((4, 256, 512)), [], me, out0, *outs
-    ).reshape(64, 16, 512)
+    early = lax.all_gather(both_chain.keep, "feat")
+    v = shuffle(at(vectors, 1 - half), *W)
+    early, from_z, v, input_grad = fence((early, from_z, v, input_grad))
+    vectors = (at(vectors, half) + v).reshape(1, 1088)
+    vectors = whole(split, "split", 8, sds((24, 1088)), [], vectors)
     total = rows[0, 0].astype(F32)
     for value in from_z:
         total = total + value.astype(F32)
@@ -824,8 +832,10 @@
     mine = (mine[0] + mine[1]) + (mine[2] + mine[3])
 
     units_of = lambda rows: [rows[i].astype(F32) for i in (0, 2, 1, 3)]
-    expand, feature = units_of(early[:, :64]), units_of(early[:, 64:128])
-    reduce_grad = jnp.concatenate(units_of(early[:, 128:]))
+    feature, expand = units_of(early[:, :64]), units_of(early[:, 96:160])
+    reduce_grad = jnp.concatenate(
+        units_of(jnp.concatenate([early[:, 64:96], early[:, 160:]], axis=1))
+    )
     sample = units_of(last[:, :64])
 
     gain3, shift3, gain2, shift2, off2, bias_r = (mine[i * 64 : (i + 1) * 64] for i in range(6))

time: 257 us -> 242 us (0.942)
  blocking collectives: 14.4 us -> 35.1 us
  starting transfers between devices: 61.3 us -> 45.4 us
  Pallas kernels: 97.2 us -> 83.5 us
  waiting for transfers between devices: 48 us -> 43.5 us
    pallas_call x9 -> x4, Pallas kernels: 41.9 us -> 7.54 us  [whole(): pl.pallas_call(kernel, grid=(steps,), out_shape=outs, in_specs=specs, out...]
    all_to_all x0 -> x1, blocking collectives: none -> 20.7 us  [exchange(): return lax.all_to_all(value, ('quad', 'feat'), 0, 0).reshape(shape)]
    pallas_call x3 -> x5, Pallas kernels: 55.3 us -> 76 us  [the longest x1 41.5 us: local_small(): pl.pallas_call(middle, grid_spec=pltpu.PrefetchScalarGridSpec(num_scalar_...]
    all_to_all x4 -> x1, starting transfers between devices: 17.3 us -> 4.48 us  [exchange(): return lax.all_to_all(value, ('quad', 'feat'), 0, 0).reshape(shape)]
    all_to_all x1 -> x0, starting transfers between devices: 4.51 us -> none  [local_small(): lax.all_to_all(vectors, SAMP, 0, 0)]
    ppermute x3, waiting for transfers between devices: 3.88 us -> 0.01 us  [local_small(): lax.ppermute(value, SAMP, [(j, j ^ mask) for j in range(8)])]
    all_to_all x4 -> x1, waiting for transfers between devices: 10.3 us -> 8.09 us  [exchange(): return lax.all_to_all(value, ('quad', 'feat'), 0, 0).reshape(shape)]
    ppermute x24 -> x23, waiting for transfers between devices: 33.2 us -> 35.4 us  [shuffle(): return lax.ppermute(value, axis, [(i, i ^ mask) for i in range(size)])]
  transfers between devices with their start and end apart: 34 -> 29, of which waited for: 12 -> 8; matrix products, arithmetic and copies ran while one was open for 8% -> 7% of each run, Pallas kernels for 27% -> 12%
where the time goes in v2:
time: 242 us; the launch traced here: 241 us
  Pallas kernels  83.5 us (35%)
  starting transfers between devices  45.4 us (19%)
  waiting for transfers between devices  43.5 us (18%)
  blocking collectives  35.1 us (15%)
  other arithmetic  19.8 us (8%)
  local copies, waits for them, and re-layouts  8.43 us (3%)
  between operations  5.13 us (2%)
    pallas_call x1, Pallas kernels, local_small(): pl.pallas_call(middle, grid_spec=pltpu.PrefetchScalarGridSpec(num_scalar_...  41.5 us
    ppermute x23, waiting for transfers between devices, shuffle(): return lax.ppermute(value, axis, [(i, i ^ mask) for i in range(size)])  35.4 us
    pallas_call x4, Pallas kernels, by_feature(): pl.pallas_call(kernel, grid=(4,), out_shape=tuple((out for out, _ in outs...  34.5 us
    ppermute x23, starting transfers between devices, shuffle(): return lax.ppermute(value, axis, [(i, i ^ mask) for i in range(size)])  27.6 us
    all_to_all x1, blocking collectives, exchange(): return lax.all_to_all(value, ('quad', 'feat'), 0, 0).reshape(shape)  20.7 us
    convert_element_type x13, other arithmetic, plus(): return (a.astype(F32) + b.astype(F32)).astype(BF)  13.4 us
    all_gather x1, blocking collectives, local_small(): early = lax.all_gather(both_chain.keep, 'feat')  8.37 us
    all_to_all x1, waiting for transfers between devices, exchange(): return lax.all_to_all(value, ('quad', 'feat'), 0, 0).reshape(shape)  8.09 us
  transfers between devices with their start and end apart: 29, of which 8 were waited for; matrix products, arithmetic and copies ran while one was open for 7% of the time, Pallas kernels for 12%

profile of v2, /device:TPU:0, one launch (start us, length us, event | category | flops | bytes accessed | tf_op | source)
XLA Modules:
  0.0 241.0 jit_solution(7176939317655173191)
XLA Ops:
  0.7 2.6 %turn_in.1 = bf16[16,4,16,512]{3,2,1,0:T(8,128)(2,1)} custom-call(bf16[1024,512]{1,0:T(8,128)(2,1)} %bitcast.262), custom_call_target="tpu_custom_call" | custom-call | flops 3300000000 | bytes 6000000 | tf_op jit(solution)/shard_map/turn_in/pallas_call | solution.py:583
  3.3 5.4 %all-to-all-start = ((bf16[4,4,64,512]{3,2,1,0:T(8,128)(2,1)}), bf16[4,4,64,512]{3,2,1,0:T(8,128)(2,1)S(1)}, u32[]{:S(2)}, u32[]{:S(2)}) async-start(bf16[4,4,64,512]{3,2,1,0:T(8,128)(2,1)} %bitcast.246), calls=%async_computation | async-start | bytes 2097152 | tf_op jit(solution)/shard_map/all_to_all | solution.py:656
  9.4 1.4 collective-permute-done.refs_2_
  10.9 1.6 collective-permute-start.1
  17.6 7.3 %collective-permute-done.1.refs_3_.refs_4_ = bf16[2,256,512]{2,1,0:T(8,128)(2,1)S(1)} collective-permute-done((bf16[2,256,512]{2,1,0:T(8,128)(2,1)S(1)}, bf16[2,256,512]{2,1,0:T(8,128)(2,1)S(1)}, u32[]{:S(2)}, u32[]{:S(2)}) %collective-permute-start.1) | collective-permute-done | bytes 524320 | tf_op jit(solution)/shard_map/ppermute | solution.py:598
  25.0 2.7 %collective-permute-start.2 = (bf16[4,64,512]{2,1,0:T(8,128)(2,1)S(1)}, bf16[4,64,512]{2,1,0:T(8,128)(2,1)S(1)}, u32[]{:S(2)}, u32[]{:S(2)}) collective-permute-start(bf16[4,64,512]{2,1,0:T(8,128)(2,1)S(1)} %dynamic-slice_bitcast_fusion.own_ref), channel_id=1, source_target_pairs={{0,16},{16,0},{1,17},{17,1},{2,18},{18,2},{3,19},{19,3},{4,20},{20... | collective-permute-start | bytes 786440 | tf_op jit(solution)/shard_map/ppermute | solution.py:598
  27.7 4.9 %project_queries.1 = (bf16[4,256,512]{2,1,0:T(8,128)(2,1)}, bf16[4,256,512]{2,1,0:T(8,128)(2,1)}) custom-call(bf16[4,4,64,512]{3,2,1,0:T(8,128)(2,1)} %copy-done.7, f32[1,512]{1,0:T(1,128)S(1)} %bitcast.234, f32[1,512]{1,0:T(1,128)S(1)} %bitcast.231, bf16[512,1536]{1,0:T(8,128)(2,1)} %w_ref.5, f32[1,1024]{1,0:T(1,128)S(1)} %bitcast.229), custom_call_target="tpu_custom_call" | custom-call | flops 3300000000 | bytes 6000000 | tf_op jit(solution)/shard_map/project_queries/pallas_call | solution.py:553
  32.6 6.5 %collective-permute-done.2.got_ref = bf16[4,64,512]{2,1,0:T(8,128)(2,1)S(1)} collective-permute-done((bf16[4,64,512]{2,1,0:T(8,128)(2,1)S(1)}, bf16[4,64,512]{2,1,0:T(8,128)(2,1)S(1)}, u32[]{:S(2)}, u32[]{:S(2)}) %collective-permute-start.2) | collective-permute-done | bytes 262176 | tf_op jit(solution)/shard_map/ppermute | solution.py:598
  39.8 10.0 %forward_one.1 = (bf16[4,4,4,16,512]{4,3,2,1,0:T(8,128)(2,1)}, bf16[4,256,512]{2,1,0:T(8,128)(2,1)}, bf16[4,64,512]{2,1,0:T(8,128)(2,1)}, bf16[4,64,512]{2,1,0:T...) custom-call(s32[8]{0:T(128)S(1)} %stack.44.me_ref, ...), custom_call_target="tpu_custom_call" | custom-call | flops 7699999744 | bytes 14000000 | tf_op jit(solution)/shard_map/forward_one/pallas_call | solution.py:553
  49.8 20.7 %all_to_all.20 = bf16[16,4,16,512]{3,2,1,0:T(8,128)(2,1)} all-to-all(bf16[16,4,16,512]{3,2,1,0:T(8,128)(2,1)} %bitcast.250), channel_id=1, replica_groups=mesh['half'=2,'quad'=4,'feat'=4] {'quad','feat'}, dimensions={0} | all-to-all | bytes 2097152 | tf_op jit(solution)/shard_map/all_to_all | solution.py:691
  70.5 41.5 %middle.1 = (bf16[4,4,4,16,512]{4,3,2,1,0:T(8,128)(2,1)}, f32[8,512]{1,0:T(8,128)}, f32[1,2048]{1,0:T(1,128)}, bf16[256,512]{1,0:T(8,128)(2,1)}, bf16[256,512]{1...) custom-call(s32[8]{0:T(128)} %copy-done, ...), custom_call_target="tpu_custom_call" | custom-call | flops 49500000256 | bytes 90000000 | tf_op jit(solution)/shard_map/middle/pallas_call | solution.py:710
  112.1 4.5 %all-to-all-start.2 = ((bf16[16,4,16,512]{3,2,1,0:T(8,128)(2,1)}), bf16[16,4,16,512]{3,2,1,0:T(8,128)(2,1)}, u32[]{:S(2)}, u32[]{:S(2)}) async-start(bf16[16,4,16,512]{3,2,1,0:T(8,128)(2,1)} %bitcast.248), calls=%async_computation.2 | async-start | bytes 2097152 | tf_op jit(solution)/shard_map/all_to_all | solution.py:691
  116.9 1.6 fusion.48
  118.6 1.5 fusion.3
  120.1 1.6 collective-permute-start.4
  121.7 1.7 fusion.1
  123.3 1.5 collective-permute-start.7
  124.8 8.1 %all-to-all-done.2 = bf16[16,4,16,512]{3,2,1,0:T(8,128)(2,1)} async-done(((bf16[16,4,16,512]{3,2,1,0:T(8,128)(2,1)}), bf16[16,4,16,512]{3,2,1,0:T(8,128)(2,1)}, u32[]{:S(2)}, u32[]{:S(2)}) %all-to-all-start.2) | async-done | bytes 1048608 | tf_op jit(solution)/shard_map/all_to_all | solution.py:691
  132.9 14.6 %backward_one.1 = (bf16[4,256,512]{2,1,0:T(8,128)(2,1)}, f32[4,256,512]{2,1,0:T(8,128)}, bf16[4,64,512]{2,1,0:T(8,128)(2,1)}, f32[8,512]{1,0:T(8,128)S(1)}, bf16...) custom-call(s32[8]{0:T(128)S(1)} %copy-done.1, bf16[4,4,4,16,512]{4,3,2,1,0:T(8,128)(2,1)} %bitcast.30.g_ref, ...), custom_call_target="tpu_custom_call" | custom-call | flops 13200000000 | bytes 24000000 | tf_op jit(solution)/shard_map/backward_one/pallas_call | solution.py:553
  147.6 1.4 collective-permute-done.4
  149.0 1.8 fusion.6
  151.3 1.8 fusion.7
  153.9 3.4 %collective-permute-start.9 = (bf16[4,64,512]{2,1,0:T(8,128)(2,1)}, bf16[4,64,512]{2,1,0:T(8,128)(2,1)}, u32[]{:S(2)}, u32[]{:S(2)}) collective-permute-start(bf16[4,64,512]{2,1,0:T(8,128)(2,1)} %get-tuple-element.96.term_ref), channel_id=1, source_target_pairs={{0,16},{16,0},{1,17},{17,1},{2,18},{18,2},{3,19},{19,3},{4,20},{20... | collective-permute-start | bytes 786440 | tf_op jit(solution)/shard_map/ppermute | solution.py:598
  159.2 9.6 %collective-permute-done.9.got_ref = bf16[4,64,512]{2,1,0:T(8,128)(2,1)} collective-permute-done((bf16[4,64,512]{2,1,0:T(8,128)(2,1)}, bf16[4,64,512]{2,1,0:T(8,128)(2,1)}, u32[]{:S(2)}, u32[]{:S(2)}) %collective-permute-start.9) | collective-permute-done | bytes 262176 | tf_op jit(solution)/shard_map/ppermute | solution.py:598
  168.8 1.1 collective-permute-start.14
  169.9 1.4 fusion.4
  171.4 1.1 fusion.5
  173.4 1.6 add_convert_fusion.4
  174.9 1.3 collective-permute-start.11
  176.2 1.0 collective-permute-start.12
  177.2 4.9 %backward_input.1 = bf16[4,4,64,512]{3,2,1,0:T(8,128)(2,1)} custom-call(s32[8]{0:T(128)S(1)} %copy-done.1, bf16[4,256,512]{2,1,0:T(8,128)(2,1)} %get-tuple-element.101.gb1_ref, bf16[4,4,64,512]{3,2,1,0:T(8,128)(2,1)} %copy-done.7, f32[4,256,512]{2,1,0:T(8,128)} %get-tuple-element.102.a_ref, bf16[4,64,512]{2,1,0:T(8,128)(2,1)} %get-tuple-element.96.term_ref, ...), custom_call_target="tpu_custom_call" | custom-call | flops 3300000000 | bytes 6000000 | tf_op jit(solution)/shard_map/backward_input/pallas_call | solution.py:553
  183.3 3.5 %all-to-all-start.3 = ((bf16[4,4,64,512]{3,2,1,0:T(8,128)(2,1)}), bf16[4,4,64,512]{3,2,1,0:T(8,128)(2,1)S(1)}, u32[]{:S(2)}, u32[]{:S(2)}) async-start(bf16[4,4,64,512]{3,2,1,0:T(8,128)(2,1)} %backward_input.1), calls=%async_computation.3 | async-start | bytes 2097152 | tf_op jit(solution)/shard_map/all_to_all | solution.py:807
  186.8 2.0 collective-permute-start.15
  188.9 1.5 collective-permute-start.16
  190.6 3.2 %collective-permute-start.17 = (bf16[192,512]{1,0:T(8,128)(2,1)S(1)}, bf16[192,512]{1,0:T(8,128)(2,1)S(1)}, u32[]{:S(2)}, u32[]{:S(2)}) collective-permute-start(bf16[192,512]{1,0:T(8,128)(2,1)S(1)} %fusion.19), channel_id=1, source_target_pairs={{0,16},{16,0},{1,17},{17,1},{2,18},{18,2},{3,19},{19,3},{4,20},{20... | collective-permute-start | bytes 589832 | tf_op jit(solution)/shard_map/ppermute | solution.py:598
  193.7 1.5 collective-permute-start.18
  195.2 2.2 place.1
  197.4 8.8 %collective-permute-done.18 = f32[2,1088]{1,0:T(2,128)S(1)} collective-permute-done((f32[2,1088]{1,0:T(2,128)S(1)}, f32[2,1088]{1,0:T(2,128)S(1)}, u32[]{:S(2)}, u32[]{:S(2)}) %collective-permute-start.18) | collective-permute-done | bytes 8736 | tf_op jit(solution)/shard_map/ppermute | solution.py:598
  208.2 1.3 fusion.10
  209.5 1.0 fusion.15
  210.5 2.9 %collective-permute-start.22 = (bf16[64,512]{1,0:T(8,128)(2,1)S(1)}, bf16[64,512]{1,0:T(8,128)(2,1)S(1)}, u32[]{:S(2)}, u32[]{:S(2)}) collective-permute-start(bf16[64,512]{1,0:T(8,128)(2,1)S(1)} %get-tuple-element.168), channel_id=1, source_target_pairs={{0,16},{4,20},{8,24},{12,28},{16,0},{20,4},{24,8},{28,12},{1,17},{... | collective-permute-start | bytes 196616 | tf_op jit(solution)/shard_map/ppermute | solution.py:818
  213.5 1.5 collective-permute-start.24
  215.0 2.0 collective-permute-start.25
  217.0 2.6 %turn_out.1 = bf16[1024,512]{1,0:T(8,128)(2,1)} custom-call(bf16[16,4,16,512]{3,2,1,0:T(8,128)(2,1)} %bitcast.247), custom_call_target="tpu_custom_call" | custom-call | flops 3300000000 | bytes 6000000 | tf_op jit(solution)/shard_map/turn_out/pallas_call | solution.py:583
  219.7 8.4 %all-gather = bf16[768,512]{1,0:T(8,128)(2,1)S(1)} all-gather(bf16[192,512]{1,0:T(8,128)(2,1)S(1)} %fusion.10), channel_id=2, replica_groups=mesh['half'=2,'quad'=4,'feat'=4] {'feat'}, dimensions={0}, use_global_device_ids=true | all-gather | bytes 983040 | tf_op jit(solution)/shard_map/all_gather | solution.py:820
  228.3 6.0 %all-gather.1 = bf16[288,512]{1,0:T(8,128)(2,1)S(1)} all-gather(bf16[72,512]{1,0:T(8,128)(2,1)S(1)} %pad_maximum_fusion.4), channel_id=3, replica_groups=mesh['half'=2,'quad'=4,'feat'=4] {'feat'}, dimensions={0}, use_global_device_ids=true | all-gather | bytes 368640 | tf_op jit(solution)/shard_map/all_gather | solution.py:829
  239.3 0.8 maximum_convert_fusion
  240.1 0.9 maximum_convert_fusion.1
  (146 shorter events, 15.6 us)
Async XLA Ops:
  3.3 5.4 %copy-start.10 = (bf16[64,16,512]{2,1,0:T(8,128)(2,1)S(1)}, bf16[64,16,512]{2,1,0:T(8,128)(2,1)}, u32[]{:S(2)}) copy-start(bf16[64,16,512]{2,1,0:T(8,128)(2,1)} %param.43) | copy-start | bytes 3145732
  3.3 21.6 %all-to-all-start = ((bf16[4,4,64,512]{3,2,1,0:T(8,128)(2,1)}), bf16[4,4,64,512]{3,2,1,0:T(8,128)(2,1)S(1)}, u32[]{:S(2)}, u32[]{:S(2)}) async-start(bf16[4,4,64,512]{3,2,1,0:T(8,128)(2,1)} %bitcast.246), calls=%async_computation | async-start | bytes 2097152 | tf_op jit(solution)/shard_map/all_to_all | solution.py:656
  8.7 7.1 %copy-start.18 = (s32[512]{0:T(512)S(1)}, s32[512]{0:T(512)}, u32[]{:S(2)}) copy-start(s32[512]{0:T(512)} %param.23) | copy-start | bytes 6148
  8.7 18.9 %copy-start.2 = (f32[1024]{0:T(1024)S(1)}, f32[1024]{0:T(1024)}, u32[]{:S(2)}) copy-start(f32[1024]{0:T(1024)} %param.28) | copy-start | bytes 12292
  8.8 18.9 %copy-start.3 = (f32[512]{0:T(512)S(1)}, f32[512]{0:T(512)}, u32[]{:S(2)}) copy-start(f32[512]{0:T(512)} %param.26) | copy-start | bytes 6148
  8.8 18.9 %copy-start.5 = (f32[512]{0:T(512)S(1)}, f32[512]{0:T(512)}, u32[]{:S(2)}) copy-start(f32[512]{0:T(512)} %param.25) | copy-start | bytes 6148
  8.8 2.0 collective-permute-start
  10.8 21.8 %copy-start.13 = (bf16[2,256,512]{2,1,0:T(8,128)(2,1)}, bf16[2,256,512]{2,1,0:T(8,128)(2,1)S(1)}, u32[]{:S(2)}) copy-start(bf16[2,256,512]{2,1,0:T(8,128)(2,1)S(1)} %collective-permute-done.refs_2_) | copy-start | bytes 1572868
  10.9 14.0 %collective-permute-start.1 = (bf16[2,256,512]{2,1,0:T(8,128)(2,1)S(1)}, bf16[2,256,512]{2,1,0:T(8,128)(2,1)S(1)}, u32[]{:S(2)}, u32[]{:S(2)}) collective-permute-start(bf16[2,256,512]{2,1,0:T(8,128)(2,1)S(1)} %pad_maximum_fusion.1), channel_id=1, source_target_pairs={{0,2},{1,3},{2,0},{3,1},{4,6},{5,7},{6,4},{7,5},{8,10},{9,11},{10,... | collective-permute-start | bytes 1572872 | tf_op jit(solution)/shard_map/ppermute | solution.py:598
  17.5 21.6 %copy-start = (s32[8]{0:T(128)}, s32[8]{0:T(128)S(1)}, u32[]{:S(2)}) copy-start(s32[8]{0:T(128)S(1)} %stack.44.me_ref) | copy-start | bytes 100
  24.9 7.7 %copy-start.21 = (bf16[2,256,512]{2,1,0:T(8,128)(2,1)}, bf16[2,256,512]{2,1,0:T(8,128)(2,1)S(1)}, u32[]{:S(2)}) copy-start(bf16[2,256,512]{2,1,0:T(8,128)(2,1)S(1)} %collective-permute-done.1.refs_3_.refs_4_) | copy-start | bytes 1572868
  24.9 2.7 %copy-start.7 = (bf16[4,4,64,512]{3,2,1,0:T(8,128)(2,1)}, bf16[4,4,64,512]{3,2,1,0:T(8,128)(2,1)S(1)}, u32[]{:S(2)}) copy-start(bf16[4,4,64,512]{3,2,1,0:T(8,128)(2,1)S(1)} %all-to-all-done.x_ref) | copy-start | bytes 3145732
  25.0 7.6 %copy-start.11 = (bf16[4,64,512]{2,1,0:T(8,128)(2,1)}, bf16[4,64,512]{2,1,0:T(8,128)(2,1)S(1)}, u32[]{:S(2)}) copy-start(bf16[4,64,512]{2,1,0:T(8,128)(2,1)S(1)} %dynamic-slice_bitcast_fusion.own_ref) | copy-start | bytes 786436
  25.0 14.1 %collective-permute-start.2 = (bf16[4,64,512]{2,1,0:T(8,128)(2,1)S(1)}, bf16[4,64,512]{2,1,0:T(8,128)(2,1)S(1)}, u32[]{:S(2)}, u32[]{:S(2)}) collective-permute-start(bf16[4,64,512]{2,1,0:T(8,128)(2,1)S(1)} %dynamic-slice_bitcast_fusion.own_ref), channel_id=1, source_target_pairs={{0,16},{16,0},{1,17},{17,1},{2,18},{18,2},{3,19},{19,3},{4,20},{20... | collective-permute-start | bytes 786440 | tf_op jit(solution)/shard_map/ppermute | solution.py:598
  27.6 12.1 %copy-start.4 = (f32[512]{0:T(512)S(1)}, f32[512]{0:T(512)}, u32[]{:S(2)}) copy-start(f32[512]{0:T(512)} %param.30) | copy-start | bytes 6148
  39.1 0.7 copy-start.22
  112.0 4.9 %copy-start.8 = (bf16[16,96,512]{2,1,0:T(8,128)(2,1)S(1)}, bf16[16,96,512]{2,1,0:T(8,128)(2,1)}, u32[]{:S(2)}) copy-start(bf16[16,96,512]{2,1,0:T(8,128)(2,1)} %get-tuple-element.92) | copy-start | bytes 4718596
  112.0 6.5 %collective-permute-start.3 = (bf16[2,2,2,2,96,512]{5,4,3,2,1,0:T(8,128)(2,1)}, bf16[2,2,2,2,96,512]{5,4,3,2,1,0:T(8,128)(2,1)S(1)}, u32[]{:S(2)}, u32[]{:S(2)}) collective-permute-start(bf16[2,2,2,2,96,512]{5,4,3,2,1,0:T(8,128)(2,1)} %bitcast.261), channel_id=1, source_target_pairs={{0,1},{1,0},{2,3},{3,2},{4,5},{5,4},{6,7},{7,6},{8,9},{9,8},{10,11... | collective-permute-start | bytes 4718600 | tf_op jit(solution)/shard_map/ppermute | solution.py:598
  112.1 20.8 %all-to-all-start.2 = ((bf16[16,4,16,512]{3,2,1,0:T(8,128)(2,1)}), bf16[16,4,16,512]{3,2,1,0:T(8,128)(2,1)}, u32[]{:S(2)}, u32[]{:S(2)}) async-start(bf16[16,4,16,512]{3,2,1,0:T(8,128)(2,1)} %bitcast.248), calls=%async_computation.2 | async-start | bytes 2097152 | tf_op jit(solution)/shard_map/all_to_all | solution.py:691
  116.6 5.1 %collective-permute-start.6 = (bf16[2,2,2,2,96,512]{5,4,3,2,1,0:T(8,128)(2,1)}, bf16[2,2,2,2,96,512]{5,4,3,2,1,0:T(8,128)(2,1)S(1)}, u32[]{:S(2)}, u32[]{:S(2)}) collective-permute-start(bf16[2,2,2,2,96,512]{5,4,3,2,1,0:T(8,128)(2,1)} %bitcast.260), channel_id=1, source_target_pairs={{0,1},{1,0},{2,3},{3,2},{4,5},{5,4},{6,7},{7,6},{8,9},{9,8},{10,11... | collective-permute-start | bytes 4718600 | tf_op jit(solution)/shard_map/ppermute | solution.py:598
  120.1 29.0 %collective-permute-start.4 = (bf16[2,2,2,96,512]{4,3,2,1,0:T(8,128)(2,1)}, bf16[2,2,2,96,512]{4,3,2,1,0:T(8,128)(2,1)}, u32[]{:S(2)}, u32[]{:S(2)}) collective-permute-start(bf16[2,2,2,96,512]{4,3,2,1,0:T(8,128)(2,1)} %get-tuple-element.139), channel_id=1, source_target_pairs={{0,2},{1,3},{2,0},{3,1},{4,6},{5,7},{6,4},{7,5},{8,10},{9,11},{10,... | collective-permute-start | bytes 2359304 | tf_op jit(solution)/shard_map/ppermute | solution.py:598
  121.7 11.3 %copy-start.1 = (s32[8]{0:T(128)S(1)}, s32[8]{0:T(128)}, u32[]{:S(2)}) copy-start(s32[8]{0:T(128)} %copy-done) | copy-start | bytes 100
  123.3 27.9 %collective-permute-start.7 = (bf16[2,2,2,96,512]{4,3,2,1,0:T(8,128)(2,1)}, bf16[2,2,2,96,512]{4,3,2,1,0:T(8,128)(2,1)}, u32[]{:S(2)}, u32[]{:S(2)}) collective-permute-start(bf16[2,2,2,96,512]{4,3,2,1,0:T(8,128)(2,1)} %get-tuple-element.135), channel_id=1, source_target_pairs={{0,4},{4,0},{8,12},{12,8},{1,5},{5,1},{9,13},{13,9},{2,6},{6,2},{1... | collective-permute-start | bytes 2359304 | tf_op jit(solution)/shard_map/ppermute | solution.py:598
  132.9 18.4 %copy-start.6 = (bf16[2,2,2,96,512]{4,3,2,1,0:T(8,128)(2,1)S(1)}, bf16[2,2,2,96,512]{4,3,2,1,0:T(8,128)(2,1)}, u32[]{:S(2)}) copy-start(bf16[2,2,2,96,512]{4,3,2,1,0:T(8,128)(2,1)} %get-tuple-element.134) | copy-start | bytes 2359300
  147.5 9.8 %copy-start.17 = (f32[8,512]{1,0:T(8,128)S(1)}, f32[8,512]{1,0:T(8,128)}, u32[]{:S(2)}) copy-start(f32[8,512]{1,0:T(8,128)} %get-tuple-element.104) | copy-start | bytes 49156
  147.6 10.5 %copy-start.19 = (f32[1,2048]{1,0:T(1,128)S(1)}, f32[1,2048]{1,0:T(1,128)}, u32[]{:S(2)}) copy-start(f32[1,2048]{1,0:T(1,128)} %get-tuple-element.105) | copy-start | bytes 24580
  147.6 22.4 %collective-permute-start.10 = (bf16[2,16,32,512]{3,2,1,0:T(8,128)(2,1)S(1)}, bf16[2,16,32,512]{3,2,1,0:T(8,128)(2,1)}, u32[]{:S(2)}, u32[]{:S(2)}) collective-permute-start(bf16[2,16,32,512]{3,2,1,0:T(8,128)(2,1)S(1)} %get-tuple-element.97), channel_id=1, source_target_pairs={{0,1},{1,0},{2,3},{3,2},{4,5},{5,4},{6,7},{7,6},{8,9},{9,8},{10,11... | collective-permute-start | bytes 3145736 | tf_op jit(solution)/shard_map/ppermute | solution.py:598
  150.9 19.0 %collective-permute-start.5 = (bf16[2,2,96,512]{3,2,1,0:T(8,128)(2,1)}, bf16[2,2,96,512]{3,2,1,0:T(8,128)(2,1)S(1)}, u32[]{:S(2)}, u32[]{:S(2)}) collective-permute-start(bf16[2,2,96,512]{3,2,1,0:T(8,128)(2,1)} %fusion.6), channel_id=1, source_target_pairs={{0,4},{4,0},{8,12},{12,8},{1,5},{5,1},{9,13},{13,9},{2,6},{6,2},{1... | collective-permute-start | bytes 1179656 | tf_op jit(solution)/shard_map/ppermute | solution.py:598
  153.1 16.8 %collective-permute-start.8 = (bf16[2,2,96,512]{3,2,1,0:T(8,128)(2,1)}, bf16[2,2,96,512]{3,2,1,0:T(8,128)(2,1)}, u32[]{:S(2)}, u32[]{:S(2)}) collective-permute-start(bf16[2,2,96,512]{3,2,1,0:T(8,128)(2,1)} %fusion.7), channel_id=1, source_target_pairs={{0,2},{1,3},{2,0},{3,1},{4,6},{5,7},{6,4},{7,5},{8,10},{9,11},{10,... | collective-permute-start | bytes 1179656 | tf_op jit(solution)/shard_map/ppermute | solution.py:598
  153.9 14.9 %collective-permute-start.9 = (bf16[4,64,512]{2,1,0:T(8,128)(2,1)}, bf16[4,64,512]{2,1,0:T(8,128)(2,1)}, u32[]{:S(2)}, u32[]{:S(2)}) collective-permute-start(bf16[4,64,512]{2,1,0:T(8,128)(2,1)} %get-tuple-element.96.term_ref), channel_id=1, source_target_pairs={{0,16},{16,0},{1,17},{17,1},{2,18},{18,2},{3,19},{19,3},{4,20},{20... | collective-permute-start | bytes 786440 | tf_op jit(solution)/shard_map/ppermute | solution.py:598
  158.7 31.8 %collective-permute-start.19 = (bf16[256,512]{1,0:T(8,128)(2,1)}, bf16[256,512]{1,0:T(8,128)(2,1)}, u32[]{:S(2)}, u32[]{:S(2)}) collective-permute-start(bf16[256,512]{1,0:T(8,128)(2,1)} %get-tuple-element.113), channel_id=1, source_target_pairs={{0,1},{1,0},{2,3},{3,2},{4,5},{5,4},{6,7},{7,6},{8,9},{9,8},{10,11... | collective-permute-start | bytes 786440 | tf_op jit(solution)/shard_map/ppermute | solution.py:598
  168.8 13.4 %collective-permute-start.14 = (f32[2,2,1088]{2,1,0:T(2,128)S(1)}, f32[2,2,1088]{2,1,0:T(2,128)S(1)}, u32[]{:S(2)}, u32[]{:S(2)}) collective-permute-start(f32[2,2,1088]{2,1,0:T(2,128)S(1)} %bitcast.257), channel_id=1, source_target_pairs={{0,4},{4,0},{8,12},{12,8},{1,5},{5,1},{9,13},{13,9},{2,6},{6,2},{1... | collective-permute-start | bytes 52232 | tf_op jit(solution)/shard_map/ppermute | solution.py:598
  172.6 10.7 %collective-permute-start.13 = (bf16[2,192,512]{2,1,0:T(8,128)(2,1)S(1)}, bf16[2,192,512]{2,1,0:T(8,128)(2,1)S(1)}, u32[]{:S(2)}, u32[]{:S(2)}) collective-permute-start(bf16[2,192,512]{2,1,0:T(8,128)(2,1)S(1)} %pad_maximum_fusion.2), channel_id=1, source_target_pairs={{0,8},{4,12},{8,0},{12,4},{1,9},{5,13},{9,1},{13,5},{2,10},{6,14},... | collective-permute-start | bytes 1179656 | tf_op jit(solution)/shard_map/ppermute | solution.py:598
  174.9 7.9 %collective-permute-start.11 = (bf16[2,2,2,32,512]{4,3,2,1,0:T(8,128)(2,1)S(1)}, bf16[2,2,2,32,512]{4,3,2,1,0:T(8,128)(2,1)S(1)}, u32[]{:S(2)}, u32[]{:S(2)}) collective-permute-start(bf16[2,2,2,32,512]{4,3,2,1,0:T(8,128)(2,1)S(1)} %get-tuple-element.132), channel_id=1, source_target_pairs={{0,2},{1,3},{2,0},{3,1},{4,6},{5,7},{6,4},{7,5},{8,10},{9,11},{10,... | collective-permute-start | bytes 786440 | tf_op jit(solution)/shard_map/ppermute | solution.py:598
  176.2 7.1 %collective-permute-start.12 = (bf16[2,2,2,32,512]{4,3,2,1,0:T(8,128)(2,1)S(1)}, bf16[2,2,2,32,512]{4,3,2,1,0:T(8,128)(2,1)S(1)}, u32[]{:S(2)}, u32[]{:S(2)}) collective-permute-start(bf16[2,2,2,32,512]{4,3,2,1,0:T(8,128)(2,1)S(1)} %get-tuple-element.131), channel_id=1, source_target_pairs={{0,4},{4,0},{8,12},{12,8},{1,5},{5,1},{9,13},{13,9},{2,6},{6,2},{1... | collective-permute-start | bytes 786440 | tf_op jit(solution)/shard_map/ppermute | solution.py:598
  182.2 11.6 %collective-permute-start.20 = (bf16[256,512]{1,0:T(8,128)(2,1)}, bf16[256,512]{1,0:T(8,128)(2,1)}, u32[]{:S(2)}, u32[]{:S(2)}) collective-permute-start(bf16[256,512]{1,0:T(8,128)(2,1)} %get-tuple-element.114), channel_id=1, source_target_pairs={{0,2},{1,3},{2,0},{3,1},{4,6},{5,7},{6,4},{7,5},{8,10},{9,11},{10,... | collective-permute-start | bytes 786440 | tf_op jit(solution)/shard_map/ppermute | solution.py:598
  182.9 12.3 %collective-permute-start.21 = (bf16[256,512]{1,0:T(8,128)(2,1)}, bf16[256,512]{1,0:T(8,128)(2,1)}, u32[]{:S(2)}, u32[]{:S(2)}) collective-permute-start(bf16[256,512]{1,0:T(8,128)(2,1)} %get-tuple-element.115), channel_id=1, source_target_pairs={{0,3},{1,2},{2,1},{3,0},{4,7},{5,6},{6,5},{7,4},{8,11},{9,10},{10,... | collective-permute-start | bytes 786440 | tf_op jit(solution)/shard_map/ppermute | solution.py:598
  183.3 24.3 %all-to-all-start.3 = ((bf16[4,4,64,512]{3,2,1,0:T(8,128)(2,1)}), bf16[4,4,64,512]{3,2,1,0:T(8,128)(2,1)S(1)}, u32[]{:S(2)}, u32[]{:S(2)}) async-start(bf16[4,4,64,512]{3,2,1,0:T(8,128)(2,1)} %backward_input.1), calls=%async_computation.3 | async-start | bytes 2097152 | tf_op jit(solution)/shard_map/all_to_all | solution.py:807
  186.8 19.4 %collective-permute-start.15 = (bf16[2,2,32,512]{3,2,1,0:T(8,128)(2,1)S(1)}, bf16[2,2,32,512]{3,2,1,0:T(8,128)(2,1)S(1)}, u32[]{:S(2)}, u32[]{:S(2)}) collective-permute-start(bf16[2,2,32,512]{3,2,1,0:T(8,128)(2,1)S(1)} %fusion.22), channel_id=1, source_target_pairs={{0,4},{4,0},{8,12},{12,8},{1,5},{5,1},{9,13},{13,9},{2,6},{6,2},{1... | collective-permute-start | bytes 393224 | tf_op jit(solution)/shard_map/ppermute | solution.py:598
  188.9 17.3 %collective-permute-start.16 = (bf16[2,2,32,512]{3,2,1,0:T(8,128)(2,1)S(1)}, bf16[2,2,32,512]{3,2,1,0:T(8,128)(2,1)S(1)}, u32[]{:S(2)}, u32[]{:S(2)}) collective-permute-start(bf16[2,2,32,512]{3,2,1,0:T(8,128)(2,1)S(1)} %fusion.23), channel_id=1, source_target_pairs={{0,2},{1,3},{2,0},{3,1},{4,6},{5,7},{6,4},{7,5},{8,10},{9,11},{10,... | collective-permute-start | bytes 393224 | tf_op jit(solution)/shard_map/ppermute | solution.py:598
  190.6 17.0 %collective-permute-start.17 = (bf16[192,512]{1,0:T(8,128)(2,1)S(1)}, bf16[192,512]{1,0:T(8,128)(2,1)S(1)}, u32[]{:S(2)}, u32[]{:S(2)}) collective-permute-start(bf16[192,512]{1,0:T(8,128)(2,1)S(1)} %fusion.19), channel_id=1, source_target_pairs={{0,16},{16,0},{1,17},{17,1},{2,18},{18,2},{3,19},{19,3},{4,20},{20... | collective-permute-start | bytes 589832 | tf_op jit(solution)/shard_map/ppermute | solution.py:598
  193.7 12.5 %collective-permute-start.18 = (f32[2,1088]{1,0:T(2,128)S(1)}, f32[2,1088]{1,0:T(2,128)S(1)}, u32[]{:S(2)}, u32[]{:S(2)}) collective-permute-start(f32[2,1088]{1,0:T(2,128)S(1)} %bitcast.258), channel_id=1, source_target_pairs={{0,8},{4,12},{8,0},{12,4},{1,9},{5,13},{9,1},{13,5},{2,10},{6,14},... | collective-permute-start | bytes 26120 | tf_op jit(solution)/shard_map/ppermute | solution.py:598
  208.2 8.8 %copy-start.9 = (bf16[4,4,64,512]{3,2,1,0:T(8,128)(2,1)}, bf16[4,4,64,512]{3,2,1,0:T(8,128)(2,1)S(1)}, u32[]{:S(2)}) copy-start(bf16[4,4,64,512]{3,2,1,0:T(8,128)(2,1)S(1)} %all-to-all-done.3) | copy-start | bytes 3145732
  208.2 2.2 copy-start.16
  210.5 17.5 %collective-permute-start.22 = (bf16[64,512]{1,0:T(8,128)(2,1)S(1)}, bf16[64,512]{1,0:T(8,128)(2,1)S(1)}, u32[]{:S(2)}, u32[]{:S(2)}) collective-permute-start(bf16[64,512]{1,0:T(8,128)(2,1)S(1)} %get-tuple-element.168), channel_id=1, source_target_pairs={{0,16},{4,20},{8,24},{12,28},{16,0},{20,4},{24,8},{28,12},{1,17},{... | collective-permute-start | bytes 196616 | tf_op jit(solution)/shard_map/ppermute | solution.py:818
  213.4 14.6 %collective-permute-start.23 = (bf16[64,512]{1,0:T(8,128)(2,1)S(1)}, bf16[64,512]{1,0:T(8,128)(2,1)S(1)}, u32[]{:S(2)}, u32[]{:S(2)}) collective-permute-start(bf16[64,512]{1,0:T(8,128)(2,1)S(1)} %get-tuple-element.169), channel_id=1, source_target_pairs={{0,8},{4,12},{8,0},{12,4},{16,24},{20,28},{24,16},{28,20},{1,9},{5... | collective-permute-start | bytes 196616 | tf_op jit(solution)/shard_map/ppermute | solution.py:818
  213.5 14.5 %collective-permute-start.24 = (bf16[64,512]{1,0:T(8,128)(2,1)S(1)}, bf16[64,512]{1,0:T(8,128)(2,1)S(1)}, u32[]{:S(2)}, u32[]{:S(2)}) collective-permute-start(bf16[64,512]{1,0:T(8,128)(2,1)S(1)} %get-tuple-element.167), channel_id=1, source_target_pairs={{0,24},{4,28},{8,16},{12,20},{16,8},{20,12},{24,0},{28,4},{1,25},{... | collective-permute-start | bytes 196616 | tf_op jit(solution)/shard_map/ppermute | solution.py:818
  215.0 13.0 %collective-permute-start.25 = (f32[1088]{0:T(1024)S(1)}, f32[1088]{0:T(1024)S(1)}, u32[]{:S(2)}, u32[]{:S(2)}) collective-permute-start(f32[1088]{0:T(1024)S(1)} %get-tuple-element.129), channel_id=1, source_target_pairs={{0,16},{16,0},{1,17},{17,1},{2,18},{18,2},{3,19},{19,3},{4,20},{20... | collective-permute-start | bytes 13064 | tf_op jit(solution)/shard_map/ppermute | solution.py:598
  (4 other events, 2.7 us)

commit v3 on v2

--- a/solution.py
+++ b/solution.py
@@ -157,18 +157,20 @@
     def _():
         c_ref[...] = got_ref[...]
 
-    unit, _ = norm_parts(c_ref[0].astype(F32))
-    act = (unit * gain_ref[...] + shift_ref[...]).astype(BF)
-    cact_ref[0] = act
-    kv = mm(act, w_ref[:, 512:])
-    k = kv[:, :512].astype(BF)
-    v = (kv[:, 512:] + b_ref[:, 512:]).astype(BF)
-    k_ref[0], v_ref[0] = k, v
-    out, prob = attend(q_ref[0], k, v, masks, allow)
-    o_ref[0] = out.astype(BF)
-    p_ref[0] = prob
-    r1 = x_ref[:, 0].reshape(256, 512).astype(F32) + mm(o_ref[0], wm_ref[...]) + off_ref[...]
-    r_ref[:, :, 0] = r1.astype(BF).reshape(4, 4, 16, 512)
+    for e in range(c_ref.shape[0]):
+        unit, _ = norm_parts(c_ref[e].astype(F32))
+        act = (unit * gain_ref[...] + shift_ref[...]).astype(BF)
+        cact_ref[e] = act
+        kv = mm(act, w_ref[:, 512:])
+        k_ref[e] = kv[:, :512].astype(BF)
+        v_ref[e] = (kv[:, 512:] + b_ref[:, 512:]).astype(BF)
+    for e in range(c_ref.shape[0]):
+        out, prob = attend(q_ref[e], k_ref[e], v_ref[e], masks, allow)
+        o_ref[e] = out.astype(BF)
+        p_ref[e] = prob
+    for e in range(c_ref.shape[0]):
+        r1 = x_ref[:, e].reshape(256, 512).astype(F32) + mm(o_ref[e], wm_ref[...]) + off_ref[...]
+        r_ref[:, :, e] = r1.astype(BF).reshape(4, 4, 16, 512)
 
 
 HALF = 512
@@ -356,17 +358,33 @@
     def _():
         vec_ref[...] = jnp.zeros((8, 512), F32)
 
-    gb1 = g_ref[:, :, 0].reshape(256, 512)
-    gb1_ref[0] = gb1
-    go = mm(gb1, wm_ref[...], 1, 1).astype(BF)
-    dq, dk, dv = attend_back(q_ref[0], k_ref[0], v_ref[0], p_ref[0], go, masks, masks32)
-    dkv = jnp.concatenate([dk, dv], axis=1)
-    step = pl.program_id(0)
-    rows = pl.ds(pl.multiple_of(step * 256, 256), 256)
-    dq_scr[rows], g_scr[rows] = dq, gb1
-    dkv_scr[pl.ds(pl.multiple_of(step * 64, 64), 64)] = dkv
-
-    @pl.when(step == 3)
+    step, per = pl.program_id(0), q_ref.shape[0]
+    for e in range(per):
+        gb1 = g_ref[:, :, e].reshape(256, 512)
+        gb1_ref[e] = gb1
+        go = mm(gb1, wm_ref[...], 1, 1).astype(BF)
+        dq, dk, dv = attend_back(q_ref[e], k_ref[e], v_ref[e], p_ref[e], go, masks, masks32)
+        dkv = jnp.concatenate([dk, dv], axis=1)
+        at = step * per + e
+        rows = pl.ds(pl.multiple_of(at * 256, 256), 256)
+        dq_scr[rows], g_scr[rows] = dq, gb1
+        dkv_scr[pl.ds(pl.multiple_of(at * 64, 64), 64)] = dkv
+        back = mm(dq, w_ref[:, :512], 1, 1)
+        a_ref[e] = back
+        term = mm(dkv, w_ref[:, 512:], 1, 1)
+        term_ref[e] = term.astype(BF)
+        unit, _ = norm_parts(x_ref[:, e].reshape(256, 512).astype(F32))
+        unit_c, _ = norm_parts(c_ref[e].astype(F32))
+        zero = jnp.zeros((3, 512), F32)
+        vec_ref[...] += jnp.concatenate(
+            [
+                col_sum(back * unit) + col_sum(term * unit_c), col_sum(back) + col_sum(term),
+                col_sum(gb1), col_sum(dq), col_sum(dv), zero,
+            ],
+            axis=0,
+        )
+
+    @pl.when(step == pl.num_programs(0) - 1)
     def _():
         whole_rows = lambda ref: ref[...].reshape(-1, 512)
         act_c = whole_rows(cact_ref)
@@ -377,21 +395,6 @@
         for unit, (left, right) in enumerate(terms):
             place_sample(me_ref, mm(left, right, 0, 0).astype(BF), unit, keep_ref, send_ref)
 
-    back = mm(dq, w_ref[:, :512], 1, 1)
-    a_ref[0] = back
-    term = mm(dkv, w_ref[:, 512:], 1, 1)
-    term_ref[0] = term.astype(BF)
-    unit, _ = norm_parts(x_ref[:, 0].reshape(256, 512).astype(F32))
-    unit_c, _ = norm_parts(c_ref[0].astype(F32))
-    zero = jnp.zeros((3, 512), F32)
-    vec_ref[...] += jnp.concatenate(
-        [
-            col_sum(back * unit) + col_sum(term * unit_c), col_sum(back) + col_sum(term),
-            col_sum(gb1), col_sum(dq), col_sum(dv), zero,
-        ],
-        axis=0,
-    )
-
 
 def backward_input(me_ref, gb1_ref, x_ref, a_ref, term_ref, got_ref, gain_ref, grad_ref, a_scr):
     here, quad = me_ref[1] == me_ref[2], me_ref[3]
@@ -535,12 +538,12 @@
     return pl.BlockSpec(shape, lambda i: (0,) * len(shape))
 
 
-def moving_block(shape, axis):
-    block = tuple(1 if i == axis else n for i, n in enumerate(shape))
+def moving_block(shape, axis, per):
+    block = tuple(per if i == axis else n for i, n in enumerate(shape))
     return pl.BlockSpec(block, lambda i: tuple(i if j == axis else 0 for j in range(len(shape))))
 
 
-def by_feature(kernel, name, limit, outs, scratch, *inputs, time=3):
+def by_feature(kernel, name, limit, outs, scratch, *inputs, time=3, per=1):
     arrays, specs = [], []
     for entry in inputs:
         array, axis = entry if isinstance(entry, tuple) else (entry, None)
@@ -549,14 +552,16 @@
             specs.append(pl.BlockSpec(memory_space=pltpu.SMEM))
             continue
         arrays.append(outside(array))
-        specs.append(whole_block(array) if axis is None else moving_block(array.shape, axis))
+        specs.append(
+            whole_block(array) if axis is None else moving_block(array.shape, axis, per)
+        )
     return pl.pallas_call(
         kernel,
-        grid=(4,),
+        grid=(4 // per,),
         out_shape=tuple(out for out, _ in outs),
         in_specs=specs,
         out_specs=[
-            whole_block(out) if axis is None else moving_block(out.shape, axis)
+            whole_block(out) if axis is None else moving_block(out.shape, axis, per)
             for out, axis in outs
         ],
         scratch_shapes=scratch,
@@ -682,7 +687,7 @@
         me, (q1, 0), (own_context, 0), (got_context, 0), (x_t, 1),
         at(segment_ids.reshape(2, 256, 1), half), context_tasks,
         row(first_gain), row(first_shift), sample_weight, row(sample_bias), sample_mixer,
-        row(sample_offset), time=7,
+        row(sample_offset), time=7, per=2,
     )
 
     def exchange(value):
@@ -760,9 +765,13 @@
             [pltpu.VMEM((1024, 512), BF), pltpu.VMEM((256, 1024), BF), pltpu.VMEM((1024, 512), BF)],
             me, (gb_t, 2), o1, act1, cact, (x_t, 1),
             (context, 0), (q1, 0), (k1, 0), (v1, 0), (p1, 0), sample_weight, sample_mixer,
-            time=12,
+            time=12, per=2,
         )
     )()
+
+    gb1, back, term, vec1, keep_ab, send_ab, outs = fence(
+        (gb1, back, term, vec1, keep_ab, send_ab, outs)
+    )
 
     owned = lambda v, n: v.reshape(-1, 8, n).transpose(1, 0, 2).reshape(8, -1)
     vectors = jnp.concatenate(
@@ -773,7 +782,14 @@
         axis=1,
     )
     got_term = shuffle(term, *W)
-    got_term, got_ab = together(chains, lambda: (got_term, shuffle(send_ab, *CORE)))
+    vectors = vectors.reshape(2, 2, 2, 1088)
+    got_term, got_ab, v = together(
+        chains,
+        lambda: (
+            got_term, shuffle(send_ab, *CORE), shuffle(at(vectors, 1 - samp % 2, 2), *Y)
+        ),
+    )
+    vectors = at(vectors, samp % 2, 2) + v
     bits = lambda a: a.reshape(2, 2, 2, 2, 2, 32, 512)
     keep_ab, got_ab = bits(keep_ab), bits(got_ab)
     late = []
@@ -781,32 +797,43 @@
         pair = [plus(keep_ab[which, i], got_ab[which, i]) for i in range(2)]
         late.append(Chain(*pair, ()))
         late[-1].dims = dims
+    around_z = lambda value, mask: lax.ppermute(value, SAMP, [(j, j ^ mask) for j in range(8)])
+
+    def to_owner(rows):
+        return [around_z(rows[i // 2, i % 2], (0, 4, 2, 6)[i]) for i in (1, 2, 3)]
+
+    def add_up(rows, got):
+        total = rows[0, 0].astype(F32)
+        for value in got:
+            total = total + value.astype(F32)
+        return total.astype(BF)
+
     both = [jnp.concatenate([chain.keep[i] for chain in chains], axis=-2) for i in range(2)]
     both_chain = Chain(*both, ())
     both_chain.dims = (Z, W)
-    vectors = vectors.reshape(2, 2, 2, 1088)
-    (grad_t,), v = together(
+    (grad_t,) = together(
         late + [both_chain],
         lambda: (
             by_feature(
                 backward_input, "backward_input", 16, ((big((4, 4, 64, 512)), 1),),
                 [pltpu.VMEM((4, 64, 512), F32)],
                 me, (gb1, 0), (x_t, 1), (back, 0), (term, 0), (got_term, 0), row(first_gain),
-            ),
-            shuffle(at(vectors, 1 - samp % 2, 2), *Y),
+            )
         ),
     )
-    vectors = at(vectors, samp % 2, 2) + v
+    both_chain.take(both_chain.start())
     low = samp // 2 % 2
     layer_output = whole(
         place, "place", 16, sds((4, 256, 512)), [], me, out0, *outs
     ).reshape(64, 16, 512)
-    got, v, layer_output = together(
-        late + [both_chain],
+    early = lax.all_gather(both_chain.keep, "feat")
+    got, v, layer_output, early = together(
+        late,
         lambda: (
             lax.all_to_all(grad_t, "quad", 0, 0),
             shuffle(at(vectors, 1 - low, 1), *Z),
             layer_output,
+            early,
         ),
     )
     vectors = at(vectors, low, 1) + v
@@ -815,18 +842,14 @@
     ).reshape(64, 16, 512)
 
     rows = jnp.concatenate([chain.keep for chain in late], axis=2)
-    around_z = lambda value, mask: lax.ppermute(value, SAMP, [(j, j ^ mask) for j in range(8)])
-    from_z = [around_z(rows[i // 2, i % 2], (0, 4, 2, 6)[i]) for i in (1, 2, 3)]
-    early = lax.all_gather(both_chain.keep, "feat")
-    v = shuffle(at(vectors, 1 - half), *W)
-    early, from_z, v, input_grad = fence((early, from_z, v, input_grad))
+    from_z, v, input_grad = fence(
+        (to_owner(rows), shuffle(at(vectors, 1 - half), *W), input_grad)
+    )
     vectors = (at(vectors, half) + v).reshape(1, 1088)
     vectors = whole(split, "split", 8, sds((24, 1088)), [], vectors)
-    total = rows[0, 0].astype(F32)
-    for value in from_z:
-        total = total + value.astype(F32)
     vectors = jnp.pad(vectors[:3].reshape(-1), (0, 8 * 512 - 3 * 1088)).reshape(8, 512)
-    last = lax.all_gather(jnp.concatenate([total.astype(BF), vectors]), "feat")
+    total = add_up(rows, from_z)
+    last = lax.all_gather(jnp.concatenate([total, vectors]), "feat")
     mine = last[:, 64:].reshape(4, -1).astype(F32)
     mine = sum(mine[:, i * 1088 : (i + 1) * 1088] for i in range(3))
     mine = (mine[0] + mine[1]) + (mine[2] + mine[3])

time: 242 us -> 238 us (0.983)
  starting transfers between devices: 45.4 us -> 48.5 us
  other arithmetic: 19.8 us -> 16.8 us
    ppermute x3, starting transfers between devices: 4.45 us -> 8.01 us  [local_small(): lax.ppermute(value, SAMP, [(j, j ^ mask) for j in range(8)])]
    convert_element_type x13, other arithmetic: 13.4 us -> 10.4 us  [plus(): return (a.astype(F32) + b.astype(F32)).astype(BF)]
  transfers between devices with their start and end apart: 29 -> 29, of which waited for: 8 -> 9; matrix products, arithmetic and copies ran while one was open for 7% -> 6% of each run, Pallas kernels for 12% -> 12%
where the time goes in v3:
time: 238 us; the launch traced here: 237 us
  Pallas kernels  82.3 us (35%)
  starting transfers between devices  48.5 us (20%)
  waiting for transfers between devices  42.4 us (18%)
  blocking collectives  34.6 us (15%)
  other arithmetic  16.8 us (7%)
  local copies, waits for them, and re-layouts  7.51 us (3%)
  between operations  5.17 us (2%)
    pallas_call x1, Pallas kernels, local_small(): pl.pallas_call(middle, grid_spec=pltpu.PrefetchScalarGridSpec(num_scalar_...  41.9 us
    ppermute x23, waiting for transfers between devices, shuffle(): return lax.ppermute(value, axis, [(i, i ^ mask) for i in range(size)])  36.2 us
    pallas_call x4, Pallas kernels, by_feature(): pl.pallas_call(kernel, grid=(4 // per,), out_shape=tuple((out for out, _...  32.8 us
    ppermute x23, starting transfers between devices, shuffle(): return lax.ppermute(value, axis, [(i, i ^ mask) for i in range(size)])  27.1 us
    all_to_all x1, blocking collectives, exchange(): return lax.all_to_all(value, ('quad', 'feat'), 0, 0).reshape(shape)  20.7 us
    convert_element_type x13, other arithmetic, plus(): return (a.astype(F32) + b.astype(F32)).astype(BF)  10.4 us
    ppermute x3, starting transfers between devices, local_small(): lax.ppermute(value, SAMP, [(j, j ^ mask) for j in range(8)])  8.01 us
    all_gather x1, blocking collectives, local_small(): early = lax.all_gather(both_chain.keep, 'feat')  7.99 us
  transfers between devices with their start and end apart: 29, of which 9 were waited for; matrix products, arithmetic and copies ran while one was open for 6% of the time, Pallas kernels for 12%

profile of v3, /device:TPU:0, one launch (start us, length us, event | category | flops | bytes accessed | tf_op | source)
XLA Modules:
  0.0 237.3 jit_solution(5098800933180471942)
XLA Ops:
  0.7 2.6 %turn_in.1 = bf16[16,4,16,512]{3,2,1,0:T(8,128)(2,1)} custom-call(bf16[1024,512]{1,0:T(8,128)(2,1)} %bitcast.262), custom_call_target="tpu_custom_call" | custom-call | flops 3300000000 | bytes 6000000 | tf_op jit(solution)/shard_map/turn_in/pallas_call | solution.py:588
  3.3 5.4 %all-to-all-start = ((bf16[4,4,64,512]{3,2,1,0:T(8,128)(2,1)}), bf16[4,4,64,512]{3,2,1,0:T(8,128)(2,1)S(1)}, u32[]{:S(2)}, u32[]{:S(2)}) async-start(bf16[4,4,64,512]{3,2,1,0:T(8,128)(2,1)} %bitcast.246), calls=%async_computation | async-start | bytes 2097152 | tf_op jit(solution)/shard_map/all_to_all | solution.py:661
  9.4 1.4 collective-permute-done.refs_2_
  10.9 1.6 collective-permute-start.1
  17.6 7.3 %collective-permute-done.1.refs_3_.refs_4_ = bf16[2,256,512]{2,1,0:T(8,128)(2,1)S(1)} collective-permute-done((bf16[2,256,512]{2,1,0:T(8,128)(2,1)S(1)}, bf16[2,256,512]{2,1,0:T(8,128)(2,1)S(1)}, u32[]{:S(2)}, u32[]{:S(2)}) %collective-permute-start.1) | collective-permute-done | bytes 524320 | tf_op jit(solution)/shard_map/ppermute | solution.py:603
  25.0 2.7 %collective-permute-start.2 = (bf16[4,64,512]{2,1,0:T(8,128)(2,1)S(1)}, bf16[4,64,512]{2,1,0:T(8,128)(2,1)S(1)}, u32[]{:S(2)}, u32[]{:S(2)}) collective-permute-start(bf16[4,64,512]{2,1,0:T(8,128)(2,1)S(1)} %dynamic-slice_bitcast_fusion.own_ref), channel_id=1, source_target_pairs={{0,16},{16,0},{1,17},{17,1},{2,18},{18,2},{3,19},{19,3},{4,20},{20... | collective-permute-start | bytes 786440 | tf_op jit(solution)/shard_map/ppermute | solution.py:603
  27.7 4.9 %project_queries.1 = (bf16[4,256,512]{2,1,0:T(8,128)(2,1)}, bf16[4,256,512]{2,1,0:T(8,128)(2,1)}) custom-call(bf16[4,4,64,512]{3,2,1,0:T(8,128)(2,1)} %copy-done.7, f32[1,512]{1,0:T(1,128)S(1)} %bitcast.234, f32[1,512]{1,0:T(1,128)S(1)} %bitcast.231, bf16[512,1536]{1,0:T(8,128)(2,1)} %w_ref.5, f32[1,1024]{1,0:T(1,128)S(1)} %bitcast.229), custom_call_target="tpu_custom_call" | custom-call | flops 3300000000 | bytes 6000000 | tf_op jit(solution)/shard_map/project_queries/pallas_call | solution.py:558
  32.6 6.5 %collective-permute-done.2.got_ref = bf16[4,64,512]{2,1,0:T(8,128)(2,1)S(1)} collective-permute-done((bf16[4,64,512]{2,1,0:T(8,128)(2,1)S(1)}, bf16[4,64,512]{2,1,0:T(8,128)(2,1)S(1)}, u32[]{:S(2)}, u32[]{:S(2)}) %collective-permute-start.2) | collective-permute-done | bytes 262176 | tf_op jit(solution)/shard_map/ppermute | solution.py:603
  39.8 8.7 %forward_one.1 = (bf16[4,4,4,16,512]{4,3,2,1,0:T(8,128)(2,1)}, bf16[4,256,512]{2,1,0:T(8,128)(2,1)}, bf16[4,64,512]{2,1,0:T(8,128)(2,1)}, bf16[4,64,512]{2,1,0:T...) custom-call(s32[8]{0:T(128)S(1)} %stack.44.me_ref, ...), custom_call_target="tpu_custom_call" | custom-call | flops 7699999744 | bytes 14000000 | tf_op jit(solution)/shard_map/forward_one/pallas_call | solution.py:558
  48.5 20.7 %all_to_all.20 = bf16[16,4,16,512]{3,2,1,0:T(8,128)(2,1)} all-to-all(bf16[16,4,16,512]{3,2,1,0:T(8,128)(2,1)} %bitcast.250), channel_id=1, replica_groups=mesh['half'=2,'quad'=4,'feat'=4] {'quad','feat'}, dimensions={0} | all-to-all | bytes 2097152 | tf_op jit(solution)/shard_map/all_to_all | solution.py:696
  69.3 41.9 %middle.1 = (bf16[4,4,4,16,512]{4,3,2,1,0:T(8,128)(2,1)}, f32[8,512]{1,0:T(8,128)}, f32[1,2048]{1,0:T(1,128)}, bf16[256,512]{1,0:T(8,128)(2,1)}, bf16[256,512]{1...) custom-call(s32[8]{0:T(128)} %copy-done, ...), custom_call_target="tpu_custom_call" | custom-call | flops 49500000256 | bytes 90000000 | tf_op jit(solution)/shard_map/middle/pallas_call | solution.py:715
  111.2 4.5 %all-to-all-start.2 = ((bf16[16,4,16,512]{3,2,1,0:T(8,128)(2,1)}), bf16[16,4,16,512]{3,2,1,0:T(8,128)(2,1)}, u32[]{:S(2)}, u32[]{:S(2)}) async-start(bf16[16,4,16,512]{3,2,1,0:T(8,128)(2,1)} %bitcast.248), calls=%async_computation.2 | async-start | bytes 2097152 | tf_op jit(solution)/shard_map/all_to_all | solution.py:696
  116.3 1.7 collective-permute-start.4
  118.0 1.8 fusion.48
  119.7 1.4 fusion.3
  121.2 1.5 collective-permute-start.7
  122.7 1.6 fusion.1
  124.3 1.5 collective-permute-start.10
  125.8 6.2 %all-to-all-done.2 = bf16[16,4,16,512]{3,2,1,0:T(8,128)(2,1)} async-done(((bf16[16,4,16,512]{3,2,1,0:T(8,128)(2,1)}), bf16[16,4,16,512]{3,2,1,0:T(8,128)(2,1)}, u32[]{:S(2)}, u32[]{:S(2)}) %all-to-all-start.2) | async-done | bytes 1048608 | tf_op jit(solution)/shard_map/all_to_all | solution.py:696
  132.0 14.2 %backward_one.1 = (bf16[4,256,512]{2,1,0:T(8,128)(2,1)}, f32[4,256,512]{2,1,0:T(8,128)}, bf16[4,64,512]{2,1,0:T(8,128)(2,1)}, f32[8,512]{1,0:T(8,128)S(1)}, bf16...) custom-call(s32[8]{0:T(128)S(1)} %copy-done.1, bf16[4,4,4,16,512]{4,3,2,1,0:T(8,128)(2,1)} %bitcast.30.g_ref, ...), custom_call_target="tpu_custom_call" | custom-call | flops 13200000000 | bytes 24000000 | tf_op jit(solution)/shard_map/backward_one/pallas_call | solution.py:558
  147.9 3.4 %collective-permute-start.12 = (bf16[4,64,512]{2,1,0:T(8,128)(2,1)}, bf16[4,64,512]{2,1,0:T(8,128)(2,1)}, u32[]{:S(2)}, u32[]{:S(2)}) collective-permute-start(bf16[4,64,512]{2,1,0:T(8,128)(2,1)} %get-tuple-element.113.term_ref), channel_id=1, source_target_pairs={{0,16},{16,0},{1,17},{17,1},{2,18},{18,2},{3,19},{19,3},{4,20},{20... | collective-permute-start | bytes 786440 | tf_op jit(solution)/shard_map/ppermute | solution.py:603
  151.6 7.8 %collective-permute-done.7 = bf16[2,2,2,96,512]{4,3,2,1,0:T(8,128)(2,1)} collective-permute-done((bf16[2,2,2,96,512]{4,3,2,1,0:T(8,128)(2,1)}, bf16[2,2,2,96,512]{4,3,2,1,0:T(8,128)(2,1)}, u32[]{:S(2)}, u32[]{:S(2)}) %collective-permute-start.7) | collective-permute-done | bytes 786464 | tf_op jit(solution)/shard_map/ppermute | solution.py:603
  159.4 1.1 fusion.6
  160.9 1.2 fusion.7
  162.1 0.9 collective-permute-start.11
  163.1 0.9 collective-permute-start.14
  164.0 2.3 place.1
  166.3 5.3 %collective-permute-done.14 = f32[2,2,1088]{2,1,0:T(2,128)S(1)} collective-permute-done((f32[2,2,1088]{2,1,0:T(2,128)S(1)}, f32[2,2,1088]{2,1,0:T(2,128)S(1)}, u32[]{:S(2)}, u32[]{:S(2)}) %collective-permute-start.14) | collective-permute-done | bytes 17440 | tf_op jit(solution)/shard_map/ppermute | solution.py:603
  171.6 1.0 collective-permute-done.11
  172.6 1.2 fusion.4
  173.8 1.2 fusion.5
  175.0 1.6 collective-permute-start.17
  176.7 1.4 add_convert_fusion.4
  178.1 1.8 collective-permute-start.15
  180.3 4.9 %backward_input.1 = bf16[4,4,64,512]{3,2,1,0:T(8,128)(2,1)} custom-call(s32[8]{0:T(128)S(1)} %copy-done.1, bf16[4,256,512]{2,1,0:T(8,128)(2,1)} %get-tuple-element.121.gb1_ref, bf16[4,4,64,512]{3,2,1,0:T(8,128)(2,1)} %copy-done.7, f32[4,256,512]{2,1,0:T(8,128)} %get-tuple-element.122.a_ref, bf16[4,64,512]{2,1,0:T(8,128)(2,1)} %get-tuple-element.113.term_ref, ...), custom_call_target="tpu_custom_call" | custom-call | flops 3300000000 | bytes 6000000 | tf_op jit(solution)/shard_map/backward_input/pallas_call | solution.py:558
  185.2 1.2 collective-permute-done.16
  186.3 3.5 %all-to-all-start.3 = ((bf16[4,4,64,512]{3,2,1,0:T(8,128)(2,1)}), bf16[4,4,64,512]{3,2,1,0:T(8,128)(2,1)S(1)}, u32[]{:S(2)}, u32[]{:S(2)}) async-start(bf16[4,4,64,512]{3,2,1,0:T(8,128)(2,1)} %backward_input.1), calls=%async_computation.3 | async-start | bytes 2097152 | tf_op jit(solution)/shard_map/all_to_all | solution.py:833
  189.9 2.0 collective-permute-start.20
  192.0 1.5 collective-permute-start.18
  193.6 3.4 %collective-permute-start.21 = (bf16[192,512]{1,0:T(8,128)(2,1)S(1)}, bf16[192,512]{1,0:T(8,128)(2,1)S(1)}, u32[]{:S(2)}, u32[]{:S(2)}) collective-permute-start(bf16[192,512]{1,0:T(8,128)(2,1)S(1)} %fusion.20), channel_id=1, source_target_pairs={{0,16},{16,0},{1,17},{17,1},{2,18},{18,2},{3,19},{19,3},{4,20},{20... | collective-permute-start | bytes 589832 | tf_op jit(solution)/shard_map/ppermute | solution.py:603
  197.4 5.8 %collective-permute-done.21 = bf16[192,512]{1,0:T(8,128)(2,1)S(1)} collective-permute-done((bf16[192,512]{1,0:T(8,128)(2,1)S(1)}, bf16[192,512]{1,0:T(8,128)(2,1)S(1)}, u32[]{:S(2)}, u32[]{:S(2)}) %collective-permute-start.21) | collective-permute-done | bytes 196640 | tf_op jit(solution)/shard_map/ppermute | solution.py:603
  203.2 8.0 %all-gather = bf16[768,512]{1,0:T(8,128)(2,1)S(1)} all-gather(bf16[192,512]{1,0:T(8,128)(2,1)S(1)} %fusion.10), channel_id=2, replica_groups=mesh['half'=2,'quad'=4,'feat'=4] {'feat'}, dimensions={0}, use_global_device_ids=true | all-gather | bytes 983040 | tf_op jit(solution)/shard_map/all_gather | solution.py:829
  212.9 1.0 fusion.13
  213.9 3.4 %collective-permute-start.22 = (bf16[64,512]{1,0:T(8,128)(2,1)S(1)}, bf16[64,512]{1,0:T(8,128)(2,1)S(1)}, u32[]{:S(2)}, u32[]{:S(2)}) collective-permute-start(bf16[64,512]{1,0:T(8,128)(2,1)S(1)} %get-tuple-element.184), channel_id=1, source_target_pairs={{0,16},{4,20},{8,24},{12,28},{16,0},{20,4},{24,8},{28,12},{1,17},{... | collective-permute-start | bytes 196616 | tf_op jit(solution)/shard_map/ppermute | solution.py:800
  217.4 2.3 collective-permute-start.23
  219.7 2.3 collective-permute-start.24
  222.6 2.6 %turn_out.1 = bf16[1024,512]{1,0:T(8,128)(2,1)} custom-call(bf16[16,4,16,512]{3,2,1,0:T(8,128)(2,1)} %bitcast.247), custom_call_target="tpu_custom_call" | custom-call | flops 3300000000 | bytes 6000000 | tf_op jit(solution)/shard_map/turn_out/pallas_call | solution.py:588
  228.0 5.9 %all-gather.1 = bf16[288,512]{1,0:T(8,128)(2,1)S(1)} all-gather(bf16[72,512]{1,0:T(8,128)(2,1)S(1)} %pad_maximum_fusion.4), channel_id=3, replica_groups=mesh['half'=2,'quad'=4,'feat'=4] {'feat'}, dimensions={0}, use_global_device_ids=true | all-gather | bytes 368640 | tf_op jit(solution)/shard_map/all_gather | solution.py:852
  (144 shorter events, 15.0 us)
Async XLA Ops:
  3.3 5.4 %copy-start.10 = (bf16[64,16,512]{2,1,0:T(8,128)(2,1)S(1)}, bf16[64,16,512]{2,1,0:T(8,128)(2,1)}, u32[]{:S(2)}) copy-start(bf16[64,16,512]{2,1,0:T(8,128)(2,1)} %param.43) | copy-start | bytes 3145732
  3.3 21.7 %all-to-all-start = ((bf16[4,4,64,512]{3,2,1,0:T(8,128)(2,1)}), bf16[4,4,64,512]{3,2,1,0:T(8,128)(2,1)S(1)}, u32[]{:S(2)}, u32[]{:S(2)}) async-start(bf16[4,4,64,512]{3,2,1,0:T(8,128)(2,1)} %bitcast.246), calls=%async_computation | async-start | bytes 2097152 | tf_op jit(solution)/shard_map/all_to_all | solution.py:661
  8.7 7.1 %copy-start.16 = (s32[512]{0:T(512)S(1)}, s32[512]{0:T(512)}, u32[]{:S(2)}) copy-start(s32[512]{0:T(512)} %param.23) | copy-start | bytes 6148
  8.8 18.9 %copy-start.2 = (f32[1024]{0:T(1024)S(1)}, f32[1024]{0:T(1024)}, u32[]{:S(2)}) copy-start(f32[1024]{0:T(1024)} %param.28) | copy-start | bytes 12292
  8.8 18.9 %copy-start.3 = (f32[512]{0:T(512)S(1)}, f32[512]{0:T(512)}, u32[]{:S(2)}) copy-start(f32[512]{0:T(512)} %param.26) | copy-start | bytes 6148
  8.8 18.9 %copy-start.5 = (f32[512]{0:T(512)S(1)}, f32[512]{0:T(512)}, u32[]{:S(2)}) copy-start(f32[512]{0:T(512)} %param.25) | copy-start | bytes 6148
  8.9 2.0 collective-permute-start
  10.8 21.8 %copy-start.12 = (bf16[2,256,512]{2,1,0:T(8,128)(2,1)}, bf16[2,256,512]{2,1,0:T(8,128)(2,1)S(1)}, u32[]{:S(2)}) copy-start(bf16[2,256,512]{2,1,0:T(8,128)(2,1)S(1)} %collective-permute-done.refs_2_) | copy-start | bytes 1572868
  10.9 14.0 %collective-permute-start.1 = (bf16[2,256,512]{2,1,0:T(8,128)(2,1)S(1)}, bf16[2,256,512]{2,1,0:T(8,128)(2,1)S(1)}, u32[]{:S(2)}, u32[]{:S(2)}) collective-permute-start(bf16[2,256,512]{2,1,0:T(8,128)(2,1)S(1)} %pad_maximum_fusion.1), channel_id=1, source_target_pairs={{0,2},{1,3},{2,0},{3,1},{4,6},{5,7},{6,4},{7,5},{8,10},{9,11},{10,... | collective-permute-start | bytes 1572872 | tf_op jit(solution)/shard_map/ppermute | solution.py:603
  17.5 21.6 %copy-start = (s32[8]{0:T(128)}, s32[8]{0:T(128)S(1)}, u32[]{:S(2)}) copy-start(s32[8]{0:T(128)S(1)} %stack.44.me_ref) | copy-start | bytes 100
  24.9 7.7 %copy-start.19 = (bf16[2,256,512]{2,1,0:T(8,128)(2,1)}, bf16[2,256,512]{2,1,0:T(8,128)(2,1)S(1)}, u32[]{:S(2)}) copy-start(bf16[2,256,512]{2,1,0:T(8,128)(2,1)S(1)} %collective-permute-done.1.refs_3_.refs_4_) | copy-start | bytes 1572868
  24.9 2.7 %copy-start.7 = (bf16[4,4,64,512]{3,2,1,0:T(8,128)(2,1)}, bf16[4,4,64,512]{3,2,1,0:T(8,128)(2,1)S(1)}, u32[]{:S(2)}) copy-start(bf16[4,4,64,512]{3,2,1,0:T(8,128)(2,1)S(1)} %all-to-all-done.x_ref) | copy-start | bytes 3145732
  25.0 7.6 %copy-start.11 = (bf16[4,64,512]{2,1,0:T(8,128)(2,1)}, bf16[4,64,512]{2,1,0:T(8,128)(2,1)S(1)}, u32[]{:S(2)}) copy-start(bf16[4,64,512]{2,1,0:T(8,128)(2,1)S(1)} %dynamic-slice_bitcast_fusion.own_ref) | copy-start | bytes 786436
  25.0 14.1 %collective-permute-start.2 = (bf16[4,64,512]{2,1,0:T(8,128)(2,1)S(1)}, bf16[4,64,512]{2,1,0:T(8,128)(2,1)S(1)}, u32[]{:S(2)}, u32[]{:S(2)}) collective-permute-start(bf16[4,64,512]{2,1,0:T(8,128)(2,1)S(1)} %dynamic-slice_bitcast_fusion.own_ref), channel_id=1, source_target_pairs={{0,16},{16,0},{1,17},{17,1},{2,18},{18,2},{3,19},{19,3},{4,20},{20... | collective-permute-start | bytes 786440 | tf_op jit(solution)/shard_map/ppermute | solution.py:603
  27.7 12.1 %copy-start.4 = (f32[512]{0:T(512)S(1)}, f32[512]{0:T(512)}, u32[]{:S(2)}) copy-start(f32[512]{0:T(512)} %param.30) | copy-start | bytes 6148
  111.1 6.8 %copy-start.8 = (bf16[16,96,512]{2,1,0:T(8,128)(2,1)S(1)}, bf16[16,96,512]{2,1,0:T(8,128)(2,1)}, u32[]{:S(2)}) copy-start(bf16[16,96,512]{2,1,0:T(8,128)(2,1)} %get-tuple-element.109) | copy-start | bytes 4718596
  111.1 8.6 %collective-permute-start.6 = (bf16[2,2,2,2,96,512]{5,4,3,2,1,0:T(8,128)(2,1)}, bf16[2,2,2,2,96,512]{5,4,3,2,1,0:T(8,128)(2,1)S(1)}, u32[]{:S(2)}, u32[]{:S(2)}) collective-permute-start(bf16[2,2,2,2,96,512]{5,4,3,2,1,0:T(8,128)(2,1)} %bitcast.261), channel_id=1, source_target_pairs={{0,1},{1,0},{2,3},{3,2},{4,5},{5,4},{6,7},{7,6},{8,9},{9,8},{10,11... | collective-permute-start | bytes 4718600 | tf_op jit(solution)/shard_map/ppermute | solution.py:603
  111.2 20.8 %all-to-all-start.2 = ((bf16[16,4,16,512]{3,2,1,0:T(8,128)(2,1)}), bf16[16,4,16,512]{3,2,1,0:T(8,128)(2,1)}, u32[]{:S(2)}, u32[]{:S(2)}) async-start(bf16[16,4,16,512]{3,2,1,0:T(8,128)(2,1)} %bitcast.248), calls=%async_computation.2 | async-start | bytes 2097152 | tf_op jit(solution)/shard_map/all_to_all | solution.py:696
  115.7 7.0 %collective-permute-start.9 = (bf16[2,2,2,2,96,512]{5,4,3,2,1,0:T(8,128)(2,1)}, bf16[2,2,2,2,96,512]{5,4,3,2,1,0:T(8,128)(2,1)S(1)}, u32[]{:S(2)}, u32[]{:S(2)}) collective-permute-start(bf16[2,2,2,2,96,512]{5,4,3,2,1,0:T(8,128)(2,1)} %bitcast.260), channel_id=1, source_target_pairs={{0,1},{1,0},{2,3},{3,2},{4,5},{5,4},{6,7},{7,6},{8,9},{9,8},{10,11... | collective-permute-start | bytes 4718600 | tf_op jit(solution)/shard_map/ppermute | solution.py:603
  116.0 30.2 %collective-permute-start.3 = (bf16[256,512]{1,0:T(8,128)(2,1)}, bf16[256,512]{1,0:T(8,128)(2,1)S(1)}, u32[]{:S(2)}, u32[]{:S(2)}) collective-permute-start(bf16[256,512]{1,0:T(8,128)(2,1)} %get-tuple-element.105), channel_id=1, source_target_pairs={{0,1},{1,0},{2,3},{3,2},{4,5},{5,4},{6,7},{7,6},{8,9},{9,8},{10,11... | collective-permute-start | bytes 786440 | tf_op jit(solution)/shard_map/ppermute | solution.py:603
  116.3 30.0 %collective-permute-start.4 = (bf16[256,512]{1,0:T(8,128)(2,1)}, bf16[256,512]{1,0:T(8,128)(2,1)}, u32[]{:S(2)}, u32[]{:S(2)}) collective-permute-start(bf16[256,512]{1,0:T(8,128)(2,1)} %get-tuple-element.106), channel_id=1, source_target_pairs={{0,2},{1,3},{2,0},{3,1},{4,6},{5,7},{6,4},{7,5},{8,10},{9,11},{10,... | collective-permute-start | bytes 786440 | tf_op jit(solution)/shard_map/ppermute | solution.py:603
  118.0 28.3 %collective-permute-start.5 = (bf16[256,512]{1,0:T(8,128)(2,1)}, bf16[256,512]{1,0:T(8,128)(2,1)}, u32[]{:S(2)}, u32[]{:S(2)}) collective-permute-start(bf16[256,512]{1,0:T(8,128)(2,1)} %get-tuple-element.107), channel_id=1, source_target_pairs={{0,3},{1,2},{2,1},{3,0},{4,7},{5,6},{6,5},{7,4},{8,11},{9,10},{10,... | collective-permute-start | bytes 786440 | tf_op jit(solution)/shard_map/ppermute | solution.py:603
  121.2 38.2 %collective-permute-start.7 = (bf16[2,2,2,96,512]{4,3,2,1,0:T(8,128)(2,1)}, bf16[2,2,2,96,512]{4,3,2,1,0:T(8,128)(2,1)}, u32[]{:S(2)}, u32[]{:S(2)}) collective-permute-start(bf16[2,2,2,96,512]{4,3,2,1,0:T(8,128)(2,1)} %get-tuple-element.155), channel_id=1, source_target_pairs={{0,2},{1,3},{2,0},{3,1},{4,6},{5,7},{6,4},{7,5},{8,10},{9,11},{10,... | collective-permute-start | bytes 2359304 | tf_op jit(solution)/shard_map/ppermute | solution.py:603
  122.7 9.3 %copy-start.1 = (s32[8]{0:T(128)S(1)}, s32[8]{0:T(128)}, u32[]{:S(2)}) copy-start(s32[8]{0:T(128)} %copy-done) | copy-start | bytes 100
  124.3 36.6 %collective-permute-start.10 = (bf16[2,2,2,96,512]{4,3,2,1,0:T(8,128)(2,1)}, bf16[2,2,2,96,512]{4,3,2,1,0:T(8,128)(2,1)}, u32[]{:S(2)}, u32[]{:S(2)}) collective-permute-start(bf16[2,2,2,96,512]{4,3,2,1,0:T(8,128)(2,1)} %get-tuple-element.151), channel_id=1, source_target_pairs={{0,4},{4,0},{8,12},{12,8},{1,5},{5,1},{9,13},{13,9},{2,6},{6,2},{1... | collective-permute-start | bytes 2359304 | tf_op jit(solution)/shard_map/ppermute | solution.py:603
  132.0 14.4 %copy-start.15 = (f32[8,512]{1,0:T(8,128)S(1)}, f32[8,512]{1,0:T(8,128)}, u32[]{:S(2)}) copy-start(f32[8,512]{1,0:T(8,128)} %get-tuple-element.115) | copy-start | bytes 49156
  132.0 15.1 %copy-start.17 = (f32[1,2048]{1,0:T(1,128)S(1)}, f32[1,2048]{1,0:T(1,128)}, u32[]{:S(2)}) copy-start(f32[1,2048]{1,0:T(1,128)} %get-tuple-element.116) | copy-start | bytes 24580
  146.3 17.7 %copy-start.20 = (bf16[256,512]{1,0:T(8,128)(2,1)}, bf16[256,512]{1,0:T(8,128)(2,1)S(1)}, u32[]{:S(2)}) copy-start(bf16[256,512]{1,0:T(8,128)(2,1)S(1)} %collective-permute-done.3.b1) | copy-start | bytes 786436
  146.3 26.3 %collective-permute-start.13 = (bf16[2,16,32,512]{3,2,1,0:T(8,128)(2,1)S(1)}, bf16[2,16,32,512]{3,2,1,0:T(8,128)(2,1)}, u32[]{:S(2)}, u32[]{:S(2)}) collective-permute-start(bf16[2,16,32,512]{3,2,1,0:T(8,128)(2,1)S(1)} %get-tuple-element.114), channel_id=1, source_target_pairs={{0,1},{1,0},{2,3},{3,2},{4,5},{5,4},{6,7},{7,6},{8,9},{9,8},{10,11... | collective-permute-start | bytes 3145736 | tf_op jit(solution)/shard_map/ppermute | solution.py:603
  147.9 23.7 %collective-permute-start.12 = (bf16[4,64,512]{2,1,0:T(8,128)(2,1)}, bf16[4,64,512]{2,1,0:T(8,128)(2,1)}, u32[]{:S(2)}, u32[]{:S(2)}) collective-permute-start(bf16[4,64,512]{2,1,0:T(8,128)(2,1)} %get-tuple-element.113.term_ref), channel_id=1, source_target_pairs={{0,16},{16,0},{1,17},{17,1},{2,18},{18,2},{3,19},{19,3},{4,20},{20... | collective-permute-start | bytes 786440 | tf_op jit(solution)/shard_map/ppermute | solution.py:603
  160.5 11.1 %collective-permute-start.8 = (bf16[2,2,96,512]{3,2,1,0:T(8,128)(2,1)S(1)}, bf16[2,2,96,512]{3,2,1,0:T(8,128)(2,1)S(1)}, u32[]{:S(2)}, u32[]{:S(2)}) collective-permute-start(bf16[2,2,96,512]{3,2,1,0:T(8,128)(2,1)S(1)} %fusion.6), channel_id=1, source_target_pairs={{0,4},{4,0},{8,12},{12,8},{1,5},{5,1},{9,13},{13,9},{2,6},{6,2},{1... | collective-permute-start | bytes 1179656 | tf_op jit(solution)/shard_map/ppermute | solution.py:603
  162.1 10.4 %collective-permute-start.11 = (bf16[2,2,96,512]{3,2,1,0:T(8,128)(2,1)S(1)}, bf16[2,2,96,512]{3,2,1,0:T(8,128)(2,1)S(1)}, u32[]{:S(2)}, u32[]{:S(2)}) collective-permute-start(bf16[2,2,96,512]{3,2,1,0:T(8,128)(2,1)S(1)} %fusion.7), channel_id=1, source_target_pairs={{0,2},{1,3},{2,0},{3,1},{4,6},{5,7},{6,4},{7,5},{8,10},{9,11},{10,... | collective-permute-start | bytes 1179656 | tf_op jit(solution)/shard_map/ppermute | solution.py:603
  163.1 8.5 %collective-permute-start.14 = (f32[2,2,1088]{2,1,0:T(2,128)S(1)}, f32[2,2,1088]{2,1,0:T(2,128)S(1)}, u32[]{:S(2)}, u32[]{:S(2)}) collective-permute-start(f32[2,2,1088]{2,1,0:T(2,128)S(1)} %bitcast.257), channel_id=1, source_target_pairs={{0,4},{4,0},{8,12},{12,8},{1,5},{5,1},{9,13},{13,9},{2,6},{6,2},{1... | collective-permute-start | bytes 52232 | tf_op jit(solution)/shard_map/ppermute | solution.py:603
  164.0 8.6 %copy-start.6 = (bf16[2,2,2,96,512]{4,3,2,1,0:T(8,128)(2,1)S(1)}, bf16[2,2,2,96,512]{4,3,2,1,0:T(8,128)(2,1)}, u32[]{:S(2)}) copy-start(bf16[2,2,2,96,512]{4,3,2,1,0:T(8,128)(2,1)} %get-tuple-element.150) | copy-start | bytes 2359300
  175.0 11.3 %collective-permute-start.17 = (bf16[2,192,512]{2,1,0:T(8,128)(2,1)S(1)}, bf16[2,192,512]{2,1,0:T(8,128)(2,1)S(1)}, u32[]{:S(2)}, u32[]{:S(2)}) collective-permute-start(bf16[2,192,512]{2,1,0:T(8,128)(2,1)S(1)} %pad_maximum_fusion.2), channel_id=1, source_target_pairs={{0,8},{4,12},{8,0},{12,4},{1,9},{5,13},{9,1},{13,5},{2,10},{6,14},... | collective-permute-start | bytes 1179656 | tf_op jit(solution)/shard_map/ppermute | solution.py:603
  178.1 7.0 %collective-permute-start.15 = (bf16[2,2,2,32,512]{4,3,2,1,0:T(8,128)(2,1)S(1)}, bf16[2,2,2,32,512]{4,3,2,1,0:T(8,128)(2,1)S(1)}, u32[]{:S(2)}, u32[]{:S(2)}) collective-permute-start(bf16[2,2,2,32,512]{4,3,2,1,0:T(8,128)(2,1)S(1)} %get-tuple-element.148), channel_id=1, source_target_pairs={{0,2},{1,3},{2,0},{3,1},{4,6},{5,7},{6,4},{7,5},{8,10},{9,11},{10,... | collective-permute-start | bytes 786440 | tf_op jit(solution)/shard_map/ppermute | solution.py:603
  179.9 6.4 %collective-permute-start.16 = (bf16[2,2,2,32,512]{4,3,2,1,0:T(8,128)(2,1)S(1)}, bf16[2,2,2,32,512]{4,3,2,1,0:T(8,128)(2,1)S(1)}, u32[]{:S(2)}, u32[]{:S(2)}) collective-permute-start(bf16[2,2,2,32,512]{4,3,2,1,0:T(8,128)(2,1)S(1)} %get-tuple-element.147), channel_id=1, source_target_pairs={{0,4},{4,0},{8,12},{12,8},{1,5},{5,1},{9,13},{13,9},{2,6},{6,2},{1... | collective-permute-start | bytes 786440 | tf_op jit(solution)/shard_map/ppermute | solution.py:603
  186.3 25.6 %all-to-all-start.3 = ((bf16[4,4,64,512]{3,2,1,0:T(8,128)(2,1)}), bf16[4,4,64,512]{3,2,1,0:T(8,128)(2,1)S(1)}, u32[]{:S(2)}, u32[]{:S(2)}) async-start(bf16[4,4,64,512]{3,2,1,0:T(8,128)(2,1)} %backward_input.1), calls=%async_computation.3 | async-start | bytes 2097152 | tf_op jit(solution)/shard_map/all_to_all | solution.py:833
  189.9 21.3 %collective-permute-start.20 = (f32[2,1088]{1,0:T(2,128)S(1)}, f32[2,1088]{1,0:T(2,128)S(1)}, u32[]{:S(2)}, u32[]{:S(2)}) collective-permute-start(f32[2,1088]{1,0:T(2,128)S(1)} %bitcast.258), channel_id=1, source_target_pairs={{0,8},{4,12},{8,0},{12,4},{1,9},{5,13},{9,1},{13,5},{2,10},{6,14},... | collective-permute-start | bytes 26120 | tf_op jit(solution)/shard_map/ppermute | solution.py:603
  192.0 19.2 %collective-permute-start.18 = (bf16[2,2,32,512]{3,2,1,0:T(8,128)(2,1)S(1)}, bf16[2,2,32,512]{3,2,1,0:T(8,128)(2,1)S(1)}, u32[]{:S(2)}, u32[]{:S(2)}) collective-permute-start(bf16[2,2,32,512]{3,2,1,0:T(8,128)(2,1)S(1)} %fusion.22), channel_id=1, source_target_pairs={{0,4},{4,0},{8,12},{12,8},{1,5},{5,1},{9,13},{13,9},{2,6},{6,2},{1... | collective-permute-start | bytes 393224 | tf_op jit(solution)/shard_map/ppermute | solution.py:603
  193.6 9.6 %collective-permute-start.21 = (bf16[192,512]{1,0:T(8,128)(2,1)S(1)}, bf16[192,512]{1,0:T(8,128)(2,1)S(1)}, u32[]{:S(2)}, u32[]{:S(2)}) collective-permute-start(bf16[192,512]{1,0:T(8,128)(2,1)S(1)} %fusion.20), channel_id=1, source_target_pairs={{0,16},{16,0},{1,17},{17,1},{2,18},{18,2},{3,19},{19,3},{4,20},{20... | collective-permute-start | bytes 589832 | tf_op jit(solution)/shard_map/ppermute | solution.py:603
  197.0 14.8 %collective-permute-start.19 = (bf16[2,2,32,512]{3,2,1,0:T(8,128)(2,1)S(1)}, bf16[2,2,32,512]{3,2,1,0:T(8,128)(2,1)}, u32[]{:S(2)}, u32[]{:S(2)}) collective-permute-start(bf16[2,2,32,512]{3,2,1,0:T(8,128)(2,1)S(1)} %fusion.23), channel_id=1, source_target_pairs={{0,2},{1,3},{2,0},{3,1},{4,6},{5,7},{6,4},{7,5},{8,10},{9,11},{10,... | collective-permute-start | bytes 393224 | tf_op jit(solution)/shard_map/ppermute | solution.py:603
  211.9 1.0 copy-start.14
  211.9 2.0 copy-start.9
  213.9 13.8 %collective-permute-start.22 = (bf16[64,512]{1,0:T(8,128)(2,1)S(1)}, bf16[64,512]{1,0:T(8,128)(2,1)S(1)}, u32[]{:S(2)}, u32[]{:S(2)}) collective-permute-start(bf16[64,512]{1,0:T(8,128)(2,1)S(1)} %get-tuple-element.184), channel_id=1, source_target_pairs={{0,16},{4,20},{8,24},{12,28},{16,0},{20,4},{24,8},{28,12},{1,17},{... | collective-permute-start | bytes 196616 | tf_op jit(solution)/shard_map/ppermute | solution.py:800
  217.4 10.4 %collective-permute-start.23 = (bf16[64,512]{1,0:T(8,128)(2,1)S(1)}, bf16[64,512]{1,0:T(8,128)(2,1)S(1)}, u32[]{:S(2)}, u32[]{:S(2)}) collective-permute-start(bf16[64,512]{1,0:T(8,128)(2,1)S(1)} %get-tuple-element.185), channel_id=1, source_target_pairs={{0,8},{4,12},{8,0},{12,4},{16,24},{20,28},{24,16},{28,20},{1,9},{5... | collective-permute-start | bytes 196616 | tf_op jit(solution)/shard_map/ppermute | solution.py:800
  219.7 8.1 %collective-permute-start.24 = (bf16[64,512]{1,0:T(8,128)(2,1)S(1)}, bf16[64,512]{1,0:T(8,128)(2,1)S(1)}, u32[]{:S(2)}, u32[]{:S(2)}) collective-permute-start(bf16[64,512]{1,0:T(8,128)(2,1)S(1)} %get-tuple-element.183), channel_id=1, source_target_pairs={{0,24},{4,28},{8,16},{12,20},{16,8},{20,12},{24,0},{28,4},{1,25},{... | collective-permute-start | bytes 196616 | tf_op jit(solution)/shard_map/ppermute | solution.py:800
  222.0 5.8 %collective-permute-start.25 = (f32[1088]{0:T(1024)S(1)}, f32[1088]{0:T(1024)S(1)}, u32[]{:S(2)}, u32[]{:S(2)}) collective-permute-start(f32[1088]{0:T(1024)S(1)} %get-tuple-element.145), channel_id=1, source_target_pairs={{0,16},{16,0},{1,17},{17,1},{2,18},{18,2},{3,19},{19,3},{4,20},{20... | collective-permute-start | bytes 13064 | tf_op jit(solution)/shard_map/ppermute | solution.py:603
  (3 other events, 2.0 us)

commit v4 on v3

--- a/solution.py
+++ b/solution.py
@@ -410,12 +410,35 @@
     grad_ref[:, 0] = grad.astype(BF).reshape(4, 64, 512)
 
 
+VECTORS = (64,) * 6 + (128, 256, 128) + (64,) * 3
+
+
+def finale(early_ref, last_ref, fw_ref, fm_ref, ew_ref, rw_ref, sw_ref, sm_ref, *vector_refs):
+    for unit, feat in enumerate((0, 2, 1, 3)):
+        cols = slice(unit * 512, (unit + 1) * 512)
+        feature, sample = early_ref[feat, 0:64].astype(F32), last_ref[feat, 0:64].astype(F32)
+        if unit < 3:
+            fw_ref[:, cols], sw_ref[:, cols] = feature, sample
+        else:
+            fm_ref[...], sm_ref[...] = feature, sample
+        ew_ref[:, cols] = early_ref[feat, 96:160].astype(F32)
+        rw_ref[unit * 64 : unit * 64 + 32] = early_ref[feat, 64:96].astype(F32)
+        rw_ref[unit * 64 + 32 : unit * 64 + 64] = early_ref[feat, 160:192].astype(F32)
+    planes = last_ref[:, 64:88].astype(F32)
+    total = (planes[0] + planes[1]) + (planes[2] + planes[3])
+    total = total[0:8] + total[8:16] + total[16:24]
+    start = 0
+    for size, ref in zip(VECTORS, vector_refs):
+        row, at = start // 512, start % 512
+        ref[...] = total[row : row + 1, at : at + size]
+        start += size
+
+
 def split(got_ref, out_ref):
     rest = got_ref[...]
-    out_ref[...] = jnp.zeros_like(out_ref)
     for i in range(3):
         term = rest.astype(BF)
-        out_ref[i : i + 1] = term
+        out_ref[i * 8 : (i + 1) * 8] = term
         rest = rest - term.astype(F32)
 
 
@@ -687,7 +710,7 @@
         me, (q1, 0), (own_context, 0), (got_context, 0), (x_t, 1),
         at(segment_ids.reshape(2, 256, 1), half), context_tasks,
         row(first_gain), row(first_shift), sample_weight, row(sample_bias), sample_mixer,
-        row(sample_offset), time=7, per=2,
+        row(sample_offset), time=7, per=4,
     )
 
     def exchange(value):
@@ -777,7 +800,7 @@
     vectors = jnp.concatenate(
         [
             owned(vec2[:6], 64), vec2[6:].reshape(8, 128), bias2.reshape(8, 256),
-            owned(vec1[:3], 64), vec1[3:5].reshape(8, 128),
+            vec1[3:5].reshape(8, 128), owned(vec1[:3], 64),
         ],
         axis=1,
     )
@@ -845,34 +868,24 @@
     from_z, v, input_grad = fence(
         (to_owner(rows), shuffle(at(vectors, 1 - half), *W), input_grad)
     )
-    vectors = (at(vectors, half) + v).reshape(1, 1088)
-    vectors = whole(split, "split", 8, sds((24, 1088)), [], vectors)
-    vectors = jnp.pad(vectors[:3].reshape(-1), (0, 8 * 512 - 3 * 1088)).reshape(8, 512)
+    vectors = jnp.pad((at(vectors, half) + v).reshape(-1), (0, 8 * 512 - 1088)).reshape(8, 512)
+    vectors = whole(split, "split", 8, sds((24, 512)), [], vectors)
     total = add_up(rows, from_z)
     last = lax.all_gather(jnp.concatenate([total, vectors]), "feat")
-    mine = last[:, 64:].reshape(4, -1).astype(F32)
-    mine = sum(mine[:, i * 1088 : (i + 1) * 1088] for i in range(3))
-    mine = (mine[0] + mine[1]) + (mine[2] + mine[3])
-
-    units_of = lambda rows: [rows[i].astype(F32) for i in (0, 2, 1, 3)]
-    feature, expand = units_of(early[:, :64]), units_of(early[:, 96:160])
-    reduce_grad = jnp.concatenate(
-        units_of(jnp.concatenate([early[:, 64:96], early[:, 160:]], axis=1))
-    )
-    sample = units_of(last[:, :64])
-
-    gain3, shift3, gain2, shift2, off2, bias_r = (mine[i * 64 : (i + 1) * 64] for i in range(6))
-    feature_b, expand_b = mine[384:512], mine[512:768]
-    gain1, shift1, off1 = (mine[768 + i * 64 : 832 + i * 64] for i in range(3))
-    sample_b = mine[960:1088]
-    columns = lambda blocks: jnp.concatenate(blocks, axis=1)
-
+    matrices = ((64, 1536), (64, 512), (64, 2048), (256, 512), (64, 1536), (64, 512))
+    feature_w, feature_m, expand_w, reduce_w, sample_w, sample_m, *mine = whole(
+        finale, "finale", 12,
+        tuple(sds(shape, F32) for shape in matrices + tuple((1, n) for n in VECTORS)), [],
+        early, last,
+    )
+    mine = [v.reshape(-1) for v in mine]
+    gain3, shift3, gain2, shift2, off2, bias_r, feature_b, expand_b = mine[:8]
+    sample_b, gain1, shift1, off1 = mine[8:]
     return (
         layer_output, input_grad,
-        gain1, shift1, columns(sample[:3]), sample_b, sample[3], off1,
-        gain2, shift2, columns(feature[:3]), feature_b, feature[3], off2,
-        gain3, shift3, columns(expand), expand_b,
-        reduce_grad, bias_r,
+        gain1, shift1, sample_w, sample_b, sample_m, off1,
+        gain2, shift2, feature_w, feature_b, feature_m, off2,
+        gain3, shift3, expand_w, expand_b, reduce_w, bias_r,
     )
 
 

time: 238 us -> 235 us (0.987)
  other arithmetic: 16.8 us -> 12.4 us
  local copies, waits for them, and re-layouts: 7.51 us -> 4.66 us
    ppermute x23, waiting for transfers between devices: 36.2 us -> 40 us  [shuffle(): return lax.ppermute(value, axis, [(i, i ^ mask) for i in range(size)])]
    concatenate x4 -> x0, other arithmetic: 3.23 us -> none  [the longest x3 2.38 us: local_small(): columns = lambda blocks: jnp.concatenate(blocks, axis=1)]
    all_to_all x1, waiting for transfers between devices: 6.2 us -> 3.44 us  [exchange(): return lax.all_to_all(value, ('quad', 'feat'), 0, 0).reshape(shape)]
    pallas_call x4 -> x5, Pallas kernels: 7.62 us -> 10.2 us  [whole(): pl.pallas_call(kernel, grid=(steps,), out_shape=outs, in_specs=specs, out...]
  transfers between devices with their start and end apart: 29 -> 29, of which waited for: 9 -> 10; matrix products, arithmetic and copies ran while one was open for 6% -> 6% of each run, Pallas kernels for 12% -> 12%
where the time goes in v4:
time: 235 us; the launch traced here: 234 us
  Pallas kernels  84.2 us (36%)
  starting transfers between devices  48.5 us (21%)
  waiting for transfers between devices  43.4 us (18%)
  blocking collectives  35.6 us (15%)
  other arithmetic  12.4 us (5%)
  between operations  5.31 us (2%)
  local copies, waits for them, and re-layouts  4.66 us (2%)
    pallas_call x1, Pallas kernels, local_small(): pl.pallas_call(middle, grid_spec=pltpu.PrefetchScalarGridSpec(num_scalar_...  41.8 us
    ppermute x23, waiting for transfers between devices, shuffle(): return lax.ppermute(value, axis, [(i, i ^ mask) for i in range(size)])  40 us
    pallas_call x4, Pallas kernels, by_feature(): pl.pallas_call(kernel, grid=(4 // per,), out_shape=tuple((out for out, _...  32.2 us
    ppermute x23, starting transfers between devices, shuffle(): return lax.ppermute(value, axis, [(i, i ^ mask) for i in range(size)])  27.1 us
    all_to_all x1, blocking collectives, exchange(): return lax.all_to_all(value, ('quad', 'feat'), 0, 0).reshape(shape)  20.7 us
    convert_element_type x13, other arithmetic, plus(): return (a.astype(F32) + b.astype(F32)).astype(BF)  10.7 us
    pallas_call x5, Pallas kernels, whole(): pl.pallas_call(kernel, grid=(steps,), out_shape=outs, in_specs=specs, out...  10.2 us
    all_gather x1, blocking collectives, local_small(): early = lax.all_gather(both_chain.keep, 'feat')  8.42 us
  transfers between devices with their start and end apart: 29, of which 10 were waited for; matrix products, arithmetic and copies ran while one was open for 6% of the time, Pallas kernels for 12%

profile of v4, /device:TPU:0, one launch (start us, length us, event | category | flops | bytes accessed | tf_op | source)
XLA Modules:
  0.0 234.1 jit_solution(14291520856537949400)
XLA Ops:
  0.7 2.6 %turn_in.1 = bf16[16,4,16,512]{3,2,1,0:T(8,128)(2,1)} custom-call(bf16[1024,512]{1,0:T(8,128)(2,1)} %bitcast.208), custom_call_target="tpu_custom_call" | custom-call | flops 3300000000 | bytes 6000000 | tf_op jit(solution)/shard_map/turn_in/pallas_call | solution.py:611
  3.3 5.4 %all-to-all-start = ((bf16[4,4,64,512]{3,2,1,0:T(8,128)(2,1)}), bf16[4,4,64,512]{3,2,1,0:T(8,128)(2,1)S(1)}, u32[]{:S(2)}, u32[]{:S(2)}) async-start(bf16[4,4,64,512]{3,2,1,0:T(8,128)(2,1)} %bitcast.192), calls=%async_computation | async-start | bytes 2097152 | tf_op jit(solution)/shard_map/all_to_all | solution.py:684
  9.4 1.4 collective-permute-done.refs_2_
  10.9 1.6 collective-permute-start.1
  17.6 7.3 %collective-permute-done.1.refs_3_.refs_4_ = bf16[2,256,512]{2,1,0:T(8,128)(2,1)S(1)} collective-permute-done((bf16[2,256,512]{2,1,0:T(8,128)(2,1)S(1)}, bf16[2,256,512]{2,1,0:T(8,128)(2,1)S(1)}, u32[]{:S(2)}, u32[]{:S(2)}) %collective-permute-start.1) | collective-permute-done | bytes 524320 | tf_op jit(solution)/shard_map/ppermute | solution.py:626
  25.0 2.7 %collective-permute-start.2 = (bf16[4,64,512]{2,1,0:T(8,128)(2,1)S(1)}, bf16[4,64,512]{2,1,0:T(8,128)(2,1)S(1)}, u32[]{:S(2)}, u32[]{:S(2)}) collective-permute-start(bf16[4,64,512]{2,1,0:T(8,128)(2,1)S(1)} %dynamic-slice_bitcast_fusion.own_ref), channel_id=1, source_target_pairs={{0,16},{16,0},{1,17},{17,1},{2,18},{18,2},{3,19},{19,3},{4,20},{20... | collective-permute-start | bytes 786440 | tf_op jit(solution)/shard_map/ppermute | solution.py:626
  27.7 4.9 %project_queries.1 = (bf16[4,256,512]{2,1,0:T(8,128)(2,1)}, bf16[4,256,512]{2,1,0:T(8,128)(2,1)}) custom-call(bf16[4,4,64,512]{3,2,1,0:T(8,128)(2,1)} %copy-done.7, f32[1,512]{1,0:T(1,128)S(1)} %bitcast.184, f32[1,512]{1,0:T(1,128)S(1)} %bitcast.181, bf16[512,1536]{1,0:T(8,128)(2,1)} %w_ref.5, f32[1,1024]{1,0:T(1,128)S(1)} %bitcast.179), custom_call_target="tpu_custom_call" | custom-call | flops 3300000000 | bytes 6000000 | tf_op jit(solution)/shard_map/project_queries/pallas_call | solution.py:581
  32.6 6.5 %collective-permute-done.2.got_ref = bf16[4,64,512]{2,1,0:T(8,128)(2,1)S(1)} collective-permute-done((bf16[4,64,512]{2,1,0:T(8,128)(2,1)S(1)}, bf16[4,64,512]{2,1,0:T(8,128)(2,1)S(1)}, u32[]{:S(2)}, u32[]{:S(2)}) %collective-permute-start.2) | collective-permute-done | bytes 262176 | tf_op jit(solution)/shard_map/ppermute | solution.py:626
  39.8 8.1 %forward_one.1 = (bf16[4,4,4,16,512]{4,3,2,1,0:T(8,128)(2,1)}, bf16[4,256,512]{2,1,0:T(8,128)(2,1)}, bf16[4,64,512]{2,1,0:T(8,128)(2,1)}, bf16[4,64,512]{2,1,0:T...) custom-call(s32[8]{0:T(128)S(1)} %stack.44.me_ref, ...), custom_call_target="tpu_custom_call" | custom-call | flops 7699999744 | bytes 14000000 | tf_op jit(solution)/shard_map/forward_one/pallas_call | solution.py:581
  47.9 20.7 %all_to_all.20 = bf16[16,4,16,512]{3,2,1,0:T(8,128)(2,1)} all-to-all(bf16[16,4,16,512]{3,2,1,0:T(8,128)(2,1)} %bitcast.196), channel_id=1, replica_groups=mesh['half'=2,'quad'=4,'feat'=4] {'quad','feat'}, dimensions={0} | all-to-all | bytes 2097152 | tf_op jit(solution)/shard_map/all_to_all | solution.py:719
  68.7 41.8 %middle.1 = (bf16[4,4,4,16,512]{4,3,2,1,0:T(8,128)(2,1)}, f32[8,512]{1,0:T(8,128)}, f32[1,2048]{1,0:T(1,128)}, bf16[256,512]{1,0:T(8,128)(2,1)}, bf16[256,512]{1...) custom-call(s32[8]{0:T(128)} %copy-done, ...), custom_call_target="tpu_custom_call" | custom-call | flops 49500000256 | bytes 90000000 | tf_op jit(solution)/shard_map/middle/pallas_call | solution.py:738
  110.6 4.5 %all-to-all-start.2 = ((bf16[16,4,16,512]{3,2,1,0:T(8,128)(2,1)}), bf16[16,4,16,512]{3,2,1,0:T(8,128)(2,1)}, u32[]{:S(2)}, u32[]{:S(2)}) async-start(bf16[16,4,16,512]{3,2,1,0:T(8,128)(2,1)} %bitcast.193), calls=%async_computation.2 | async-start | bytes 2097152 | tf_op jit(solution)/shard_map/all_to_all | solution.py:719
  115.7 1.7 collective-permute-start.4
  118.8 1.8 fusion.39
  120.7 2.7 %fusion.3 = (bf16[2,2,2,96,512]{4,3,2,1,0:T(8,128)(2,1)S(1)}, bf16[2,2,2,96,512]{4,3,2,1,0:T(8,128)(2,1)}) fusion(bf16[2,2,2,96,512]{4,3,2,1,0:T(8,128)(2,1)S(1)} %bitcast.191, bf16[2,2,2,2,96,512]{5,4,3,2,1,0:T(8,128)(2,1)} %collective-permute-done.6, bf16[2,2,2,96,512]{4,3,2,1,0:T(8,128)(2,1)S(1)} %bitcast.190), kind=kLoop, calls=%fused_computation.7 | loop fusion | flops 3145728 | bytes 4718592 | tf_op jit(solution)/shard_map/convert_element_type | solution.py:642
  123.3 1.5 collective-permute-start.7
  124.8 1.7 fusion.1
  126.5 1.5 collective-permute-start.10
  128.0 3.4 %all-to-all-done.2 = bf16[16,4,16,512]{3,2,1,0:T(8,128)(2,1)} async-done(((bf16[16,4,16,512]{3,2,1,0:T(8,128)(2,1)}), bf16[16,4,16,512]{3,2,1,0:T(8,128)(2,1)}, u32[]{:S(2)}, u32[]{:S(2)}) %all-to-all-start.2) | async-done | bytes 1048608 | tf_op jit(solution)/shard_map/all_to_all | solution.py:719
  131.4 14.3 %backward_one.1 = (bf16[4,256,512]{2,1,0:T(8,128)(2,1)}, f32[4,256,512]{2,1,0:T(8,128)}, bf16[4,64,512]{2,1,0:T(8,128)(2,1)}, f32[8,512]{1,0:T(8,128)S(1)}, bf16...) custom-call(s32[8]{0:T(128)S(1)} %copy-done.1, bf16[4,4,4,16,512]{4,3,2,1,0:T(8,128)(2,1)} %bitcast.30.g_ref, ...), custom_call_target="tpu_custom_call" | custom-call | flops 13200000000 | bytes 24000000 | tf_op jit(solution)/shard_map/backward_one/pallas_call | solution.py:581
  145.7 3.4 %collective-permute-start.12 = (bf16[4,64,512]{2,1,0:T(8,128)(2,1)}, bf16[4,64,512]{2,1,0:T(8,128)(2,1)}, u32[]{:S(2)}, u32[]{:S(2)}) collective-permute-start(bf16[4,64,512]{2,1,0:T(8,128)(2,1)} %get-tuple-element.131.term_ref), channel_id=1, source_target_pairs={{0,16},{16,0},{1,17},{17,1},{2,18},{18,2},{3,19},{19,3},{4,20},{20... | collective-permute-start | bytes 786440 | tf_op jit(solution)/shard_map/ppermute | solution.py:626
  149.4 9.3 %collective-permute-done.7 = bf16[2,2,2,96,512]{4,3,2,1,0:T(8,128)(2,1)} collective-permute-done((bf16[2,2,2,96,512]{4,3,2,1,0:T(8,128)(2,1)}, bf16[2,2,2,96,512]{4,3,2,1,0:T(8,128)(2,1)}, u32[]{:S(2)}, u32[]{:S(2)}) %collective-permute-start.7) | collective-permute-done | bytes 786464 | tf_op jit(solution)/shard_map/ppermute | solution.py:626
  158.7 1.1 fusion.6
  160.3 1.2 fusion.7
  161.5 0.9 collective-permute-start.11
  163.3 2.3 place.1
  165.6 5.3 %collective-permute-done.14 = f32[2,2,1088]{2,1,0:T(2,128)S(1)} collective-permute-done((f32[2,2,1088]{2,1,0:T(2,128)S(1)}, f32[2,2,1088]{2,1,0:T(2,128)S(1)}, u32[]{:S(2)}, u32[]{:S(2)}) %collective-permute-start.14) | collective-permute-done | bytes 17440 | tf_op jit(solution)/shard_map/ppermute | solution.py:626
  170.9 1.1 collective-permute-done.11
  172.0 1.2 fusion.4
  173.2 1.2 fusion.5
  174.4 1.6 collective-permute-start.17
  176.1 1.4 add_convert_fusion.4
  177.5 1.8 collective-permute-start.15
  179.6 4.9 %backward_input.1 = bf16[4,4,64,512]{3,2,1,0:T(8,128)(2,1)} custom-call(s32[8]{0:T(128)S(1)} %copy-done.1, bf16[4,256,512]{2,1,0:T(8,128)(2,1)} %get-tuple-element.139.gb1_ref, bf16[4,4,64,512]{3,2,1,0:T(8,128)(2,1)} %copy-done.7, f32[4,256,512]{2,1,0:T(8,128)} %get-tuple-element.140.a_ref, bf16[4,64,512]{2,1,0:T(8,128)(2,1)} %get-tuple-element.131.term_ref, ...), custom_call_target="tpu_custom_call" | custom-call | flops 3300000000 | bytes 6000000 | tf_op jit(solution)/shard_map/backward_input/pallas_call | solution.py:581
  184.5 1.2 collective-permute-done.16
  185.7 3.5 %all-to-all-start.3 = ((bf16[4,4,64,512]{3,2,1,0:T(8,128)(2,1)}), bf16[4,4,64,512]{3,2,1,0:T(8,128)(2,1)S(1)}, u32[]{:S(2)}, u32[]{:S(2)}) async-start(bf16[4,4,64,512]{3,2,1,0:T(8,128)(2,1)} %backward_input.1), calls=%async_computation.3 | async-start | bytes 2097152 | tf_op jit(solution)/shard_map/all_to_all | solution.py:856
  189.3 2.0 collective-permute-start.20
  191.4 1.5 collective-permute-start.18
  192.9 3.4 %collective-permute-start.21 = (bf16[192,512]{1,0:T(8,128)(2,1)S(1)}, bf16[192,512]{1,0:T(8,128)(2,1)S(1)}, u32[]{:S(2)}, u32[]{:S(2)}) collective-permute-start(bf16[192,512]{1,0:T(8,128)(2,1)S(1)} %fusion.20), channel_id=1, source_target_pairs={{0,16},{16,0},{1,17},{17,1},{2,18},{18,2},{3,19},{19,3},{4,20},{20... | collective-permute-start | bytes 589832 | tf_op jit(solution)/shard_map/ppermute | solution.py:626
  196.8 5.7 %collective-permute-done.21 = bf16[192,512]{1,0:T(8,128)(2,1)S(1)} collective-permute-done((bf16[192,512]{1,0:T(8,128)(2,1)S(1)}, bf16[192,512]{1,0:T(8,128)(2,1)S(1)}, u32[]{:S(2)}, u32[]{:S(2)}) %collective-permute-start.21) | collective-permute-done | bytes 196640 | tf_op jit(solution)/shard_map/ppermute | solution.py:626
  202.6 8.4 %all-gather = bf16[768,512]{1,0:T(8,128)(2,1)} all-gather(bf16[192,512]{1,0:T(8,128)(2,1)S(1)} %fusion.10), channel_id=2, replica_groups=mesh['half'=2,'quad'=4,'feat'=4] {'feat'}, dimensions={0}, use_global_device_ids=true | all-gather | bytes 983040 | tf_op jit(solution)/shard_map/all_gather | solution.py:852
  211.2 3.4 %collective-permute-start.22 = (bf16[64,512]{1,0:T(8,128)(2,1)S(1)}, bf16[64,512]{1,0:T(8,128)(2,1)S(1)}, u32[]{:S(2)}, u32[]{:S(2)}) collective-permute-start(bf16[64,512]{1,0:T(8,128)(2,1)S(1)} %get-tuple-element.202), channel_id=1, source_target_pairs={{0,16},{4,20},{8,24},{12,28},{16,0},{20,4},{24,8},{28,12},{1,17},{... | collective-permute-start | bytes 196616 | tf_op jit(solution)/shard_map/ppermute | solution.py:823
  214.6 2.3 collective-permute-start.23
  216.9 2.3 collective-permute-start.24
  219.9 2.6 %turn_out.1 = bf16[1024,512]{1,0:T(8,128)(2,1)} custom-call(bf16[16,4,16,512]{3,2,1,0:T(8,128)(2,1)} %bitcast.194), custom_call_target="tpu_custom_call" | custom-call | flops 3300000000 | bytes 6000000 | tf_op jit(solution)/shard_map/turn_out/pallas_call | solution.py:611
  222.5 2.1 collective-permute-done.25
  224.8 6.5 %all-gather.1 = bf16[352,512]{1,0:T(8,128)(2,1)} all-gather(bf16[88,512]{1,0:T(8,128)(2,1)S(1)} %pad_maximum_fusion.4), channel_id=3, replica_groups=mesh['half'=2,'quad'=4,'feat'=4] {'feat'}, dimensions={0}, use_global_device_ids=true | all-gather | bytes 450560 | tf_op jit(solution)/shard_map/all_gather | solution.py:874
  231.3 2.6 %finale.1 = (f32[64,1536]{1,0:T(8,128)}, f32[64,512]{1,0:T(8,128)}, f32[64,2048]{1,0:T(8,128)}, f32[256,512]{1,0:T(8,128)}, f32[64,1536]{1,0:T(8,128)}, /*index=...) custom-call(bf16[4,192,512]{2,1,0:T(8,128)(2,1)} %bitcast.197, ...), custom_call_target="tpu_custom_call" | custom-call | flops 3300000000 | bytes 6000000 | tf_op jit(solution)/shard_map/finale/pallas_call | solution.py:611
  (125 shorter events, 8.3 us)
Async XLA Ops:
  3.3 5.4 %copy-start.10 = (bf16[64,16,512]{2,1,0:T(8,128)(2,1)S(1)}, bf16[64,16,512]{2,1,0:T(8,128)(2,1)}, u32[]{:S(2)}) copy-start(bf16[64,16,512]{2,1,0:T(8,128)(2,1)} %param.43) | copy-start | bytes 3145732
  3.3 21.7 %all-to-all-start = ((bf16[4,4,64,512]{3,2,1,0:T(8,128)(2,1)}), bf16[4,4,64,512]{3,2,1,0:T(8,128)(2,1)S(1)}, u32[]{:S(2)}, u32[]{:S(2)}) async-start(bf16[4,4,64,512]{3,2,1,0:T(8,128)(2,1)} %bitcast.192), calls=%async_computation | async-start | bytes 2097152 | tf_op jit(solution)/shard_map/all_to_all | solution.py:684
  8.7 0.7 copy-start.16
  8.7 7.1 %copy-start.14 = (s32[512]{0:T(512)S(1)}, s32[512]{0:T(512)}, u32[]{:S(2)}) copy-start(s32[512]{0:T(512)} %param.23) | copy-start | bytes 6148
  8.8 18.9 %copy-start.2 = (f32[1024]{0:T(1024)S(1)}, f32[1024]{0:T(1024)}, u32[]{:S(2)}) copy-start(f32[1024]{0:T(1024)} %param.28) | copy-start | bytes 12292
  8.8 18.9 %copy-start.3 = (f32[512]{0:T(512)S(1)}, f32[512]{0:T(512)}, u32[]{:S(2)}) copy-start(f32[512]{0:T(512)} %param.26) | copy-start | bytes 6148
  8.8 18.9 %copy-start.5 = (f32[512]{0:T(512)S(1)}, f32[512]{0:T(512)}, u32[]{:S(2)}) copy-start(f32[512]{0:T(512)} %param.25) | copy-start | bytes 6148
  8.9 2.0 collective-permute-start
  10.8 21.8 %copy-start.12 = (bf16[2,256,512]{2,1,0:T(8,128)(2,1)}, bf16[2,256,512]{2,1,0:T(8,128)(2,1)S(1)}, u32[]{:S(2)}) copy-start(bf16[2,256,512]{2,1,0:T(8,128)(2,1)S(1)} %collective-permute-done.refs_2_) | copy-start | bytes 1572868
  10.9 14.0 %collective-permute-start.1 = (bf16[2,256,512]{2,1,0:T(8,128)(2,1)S(1)}, bf16[2,256,512]{2,1,0:T(8,128)(2,1)S(1)}, u32[]{:S(2)}, u32[]{:S(2)}) collective-permute-start(bf16[2,256,512]{2,1,0:T(8,128)(2,1)S(1)} %pad_maximum_fusion.1), channel_id=1, source_target_pairs={{0,2},{1,3},{2,0},{3,1},{4,6},{5,7},{6,4},{7,5},{8,10},{9,11},{10,... | collective-permute-start | bytes 1572872 | tf_op jit(solution)/shard_map/ppermute | solution.py:626
  17.5 21.6 %copy-start = (s32[8]{0:T(128)}, s32[8]{0:T(128)S(1)}, u32[]{:S(2)}) copy-start(s32[8]{0:T(128)S(1)} %stack.44.me_ref) | copy-start | bytes 100
  24.9 7.7 %copy-start.17 = (bf16[2,256,512]{2,1,0:T(8,128)(2,1)}, bf16[2,256,512]{2,1,0:T(8,128)(2,1)S(1)}, u32[]{:S(2)}) copy-start(bf16[2,256,512]{2,1,0:T(8,128)(2,1)S(1)} %collective-permute-done.1.refs_3_.refs_4_) | copy-start | bytes 1572868
  24.9 2.7 %copy-start.7 = (bf16[4,4,64,512]{3,2,1,0:T(8,128)(2,1)}, bf16[4,4,64,512]{3,2,1,0:T(8,128)(2,1)S(1)}, u32[]{:S(2)}) copy-start(bf16[4,4,64,512]{3,2,1,0:T(8,128)(2,1)S(1)} %all-to-all-done.x_ref) | copy-start | bytes 3145732
  25.0 7.6 %copy-start.11 = (bf16[4,64,512]{2,1,0:T(8,128)(2,1)}, bf16[4,64,512]{2,1,0:T(8,128)(2,1)S(1)}, u32[]{:S(2)}) copy-start(bf16[4,64,512]{2,1,0:T(8,128)(2,1)S(1)} %dynamic-slice_bitcast_fusion.own_ref) | copy-start | bytes 786436
  25.0 14.1 %collective-permute-start.2 = (bf16[4,64,512]{2,1,0:T(8,128)(2,1)S(1)}, bf16[4,64,512]{2,1,0:T(8,128)(2,1)S(1)}, u32[]{:S(2)}, u32[]{:S(2)}) collective-permute-start(bf16[4,64,512]{2,1,0:T(8,128)(2,1)S(1)} %dynamic-slice_bitcast_fusion.own_ref), channel_id=1, source_target_pairs={{0,16},{16,0},{1,17},{17,1},{2,18},{18,2},{3,19},{19,3},{4,20},{20... | collective-permute-start | bytes 786440 | tf_op jit(solution)/shard_map/ppermute | solution.py:626
  27.7 12.1 %copy-start.4 = (f32[512]{0:T(512)S(1)}, f32[512]{0:T(512)}, u32[]{:S(2)}) copy-start(f32[512]{0:T(512)} %param.30) | copy-start | bytes 6148
  39.1 0.7 copy-start.18
  110.5 6.9 %copy-start.13 = (f32[8,512]{1,0:T(8,128)S(1)}, f32[8,512]{1,0:T(8,128)}, u32[]{:S(2)}) copy-start(f32[8,512]{1,0:T(8,128)} %get-tuple-element.133) | copy-start | bytes 49156
  110.5 7.6 %copy-start.15 = (f32[1,2048]{1,0:T(1,128)S(1)}, f32[1,2048]{1,0:T(1,128)}, u32[]{:S(2)}) copy-start(f32[1,2048]{1,0:T(1,128)} %get-tuple-element.134) | copy-start | bytes 24580
  110.5 8.3 %copy-start.8 = (bf16[16,96,512]{2,1,0:T(8,128)(2,1)S(1)}, bf16[16,96,512]{2,1,0:T(8,128)(2,1)}, u32[]{:S(2)}) copy-start(bf16[16,96,512]{2,1,0:T(8,128)(2,1)} %get-tuple-element.127) | copy-start | bytes 4718596
  110.5 10.1 %collective-permute-start.6 = (bf16[2,2,2,2,96,512]{5,4,3,2,1,0:T(8,128)(2,1)}, bf16[2,2,2,2,96,512]{5,4,3,2,1,0:T(8,128)(2,1)}, u32[]{:S(2)}, u32[]{:S(2)}) collective-permute-start(bf16[2,2,2,2,96,512]{5,4,3,2,1,0:T(8,128)(2,1)} %bitcast.207), channel_id=1, source_target_pairs={{0,1},{1,0},{2,3},{3,2},{4,5},{5,4},{6,7},{7,6},{8,9},{9,8},{10,11... | collective-permute-start | bytes 4718600 | tf_op jit(solution)/shard_map/ppermute | solution.py:626
  110.6 20.8 %all-to-all-start.2 = ((bf16[16,4,16,512]{3,2,1,0:T(8,128)(2,1)}), bf16[16,4,16,512]{3,2,1,0:T(8,128)(2,1)}, u32[]{:S(2)}, u32[]{:S(2)}) async-start(bf16[16,4,16,512]{3,2,1,0:T(8,128)(2,1)} %bitcast.193), calls=%async_computation.2 | async-start | bytes 2097152 | tf_op jit(solution)/shard_map/all_to_all | solution.py:719
  115.1 9.7 %collective-permute-start.9 = (bf16[2,2,2,2,96,512]{5,4,3,2,1,0:T(8,128)(2,1)}, bf16[2,2,2,2,96,512]{5,4,3,2,1,0:T(8,128)(2,1)S(1)}, u32[]{:S(2)}, u32[]{:S(2)}) collective-permute-start(bf16[2,2,2,2,96,512]{5,4,3,2,1,0:T(8,128)(2,1)} %bitcast.206), channel_id=1, source_target_pairs={{0,1},{1,0},{2,3},{3,2},{4,5},{5,4},{6,7},{7,6},{8,9},{9,8},{10,11... | collective-permute-start | bytes 4718600 | tf_op jit(solution)/shard_map/ppermute | solution.py:626
  115.4 30.3 %collective-permute-start.3 = (bf16[256,512]{1,0:T(8,128)(2,1)}, bf16[256,512]{1,0:T(8,128)(2,1)}, u32[]{:S(2)}, u32[]{:S(2)}) collective-permute-start(bf16[256,512]{1,0:T(8,128)(2,1)} %get-tuple-element.123), channel_id=1, source_target_pairs={{0,1},{1,0},{2,3},{3,2},{4,5},{5,4},{6,7},{7,6},{8,9},{9,8},{10,11... | collective-permute-start | bytes 786440 | tf_op jit(solution)/shard_map/ppermute | solution.py:626
  115.7 30.0 %collective-permute-start.4 = (bf16[256,512]{1,0:T(8,128)(2,1)}, bf16[256,512]{1,0:T(8,128)(2,1)}, u32[]{:S(2)}, u32[]{:S(2)}) collective-permute-start(bf16[256,512]{1,0:T(8,128)(2,1)} %get-tuple-element.124), channel_id=1, source_target_pairs={{0,2},{1,3},{2,0},{3,1},{4,6},{5,7},{6,4},{7,5},{8,10},{9,11},{10,... | collective-permute-start | bytes 786440 | tf_op jit(solution)/shard_map/ppermute | solution.py:626
  117.3 28.4 %collective-permute-start.5 = (bf16[256,512]{1,0:T(8,128)(2,1)}, bf16[256,512]{1,0:T(8,128)(2,1)}, u32[]{:S(2)}, u32[]{:S(2)}) collective-permute-start(bf16[256,512]{1,0:T(8,128)(2,1)} %get-tuple-element.125), channel_id=1, source_target_pairs={{0,3},{1,2},{2,1},{3,0},{4,7},{5,6},{6,5},{7,4},{8,11},{9,10},{10,... | collective-permute-start | bytes 786440 | tf_op jit(solution)/shard_map/ppermute | solution.py:626
  123.3 35.4 %collective-permute-start.7 = (bf16[2,2,2,96,512]{4,3,2,1,0:T(8,128)(2,1)}, bf16[2,2,2,96,512]{4,3,2,1,0:T(8,128)(2,1)}, u32[]{:S(2)}, u32[]{:S(2)}) collective-permute-start(bf16[2,2,2,96,512]{4,3,2,1,0:T(8,128)(2,1)} %get-tuple-element.191), channel_id=1, source_target_pairs={{0,2},{1,3},{2,0},{3,1},{4,6},{5,7},{6,4},{7,5},{8,10},{9,11},{10,... | collective-permute-start | bytes 2359304 | tf_op jit(solution)/shard_map/ppermute | solution.py:626
  124.8 6.6 %copy-start.1 = (s32[8]{0:T(128)S(1)}, s32[8]{0:T(128)}, u32[]{:S(2)}) copy-start(s32[8]{0:T(128)} %copy-done) | copy-start | bytes 100
  126.5 33.8 %collective-permute-start.10 = (bf16[2,2,2,96,512]{4,3,2,1,0:T(8,128)(2,1)}, bf16[2,2,2,96,512]{4,3,2,1,0:T(8,128)(2,1)}, u32[]{:S(2)}, u32[]{:S(2)}) collective-permute-start(bf16[2,2,2,96,512]{4,3,2,1,0:T(8,128)(2,1)} %get-tuple-element.187), channel_id=1, source_target_pairs={{0,4},{4,0},{8,12},{12,8},{1,5},{5,1},{9,13},{13,9},{2,6},{6,2},{1... | collective-permute-start | bytes 2359304 | tf_op jit(solution)/shard_map/ppermute | solution.py:626
  145.7 25.2 %collective-permute-start.12 = (bf16[4,64,512]{2,1,0:T(8,128)(2,1)}, bf16[4,64,512]{2,1,0:T(8,128)(2,1)}, u32[]{:S(2)}, u32[]{:S(2)}) collective-permute-start(bf16[4,64,512]{2,1,0:T(8,128)(2,1)} %get-tuple-element.131.term_ref), channel_id=1, source_target_pairs={{0,16},{16,0},{1,17},{17,1},{2,18},{18,2},{3,19},{19,3},{4,20},{20... | collective-permute-start | bytes 786440 | tf_op jit(solution)/shard_map/ppermute | solution.py:626
  149.2 22.8 %collective-permute-start.13 = (bf16[2,16,32,512]{3,2,1,0:T(8,128)(2,1)S(1)}, bf16[2,16,32,512]{3,2,1,0:T(8,128)(2,1)}, u32[]{:S(2)}, u32[]{:S(2)}) collective-permute-start(bf16[2,16,32,512]{3,2,1,0:T(8,128)(2,1)S(1)} %get-tuple-element.132), channel_id=1, source_target_pairs={{0,1},{1,0},{2,3},{3,2},{4,5},{5,4},{6,7},{7,6},{8,9},{9,8},{10,11... | collective-permute-start | bytes 3145736 | tf_op jit(solution)/shard_map/ppermute | solution.py:626
  159.8 11.1 %collective-permute-start.8 = (bf16[2,2,96,512]{3,2,1,0:T(8,128)(2,1)S(1)}, bf16[2,2,96,512]{3,2,1,0:T(8,128)(2,1)S(1)}, u32[]{:S(2)}, u32[]{:S(2)}) collective-permute-start(bf16[2,2,96,512]{3,2,1,0:T(8,128)(2,1)S(1)} %fusion.6), channel_id=1, source_target_pairs={{0,4},{4,0},{8,12},{12,8},{1,5},{5,1},{9,13},{13,9},{2,6},{6,2},{1... | collective-permute-start | bytes 1179656 | tf_op jit(solution)/shard_map/ppermute | solution.py:626
  161.5 10.4 %collective-permute-start.11 = (bf16[2,2,96,512]{3,2,1,0:T(8,128)(2,1)S(1)}, bf16[2,2,96,512]{3,2,1,0:T(8,128)(2,1)S(1)}, u32[]{:S(2)}, u32[]{:S(2)}) collective-permute-start(bf16[2,2,96,512]{3,2,1,0:T(8,128)(2,1)S(1)} %fusion.7), channel_id=1, source_target_pairs={{0,2},{1,3},{2,0},{3,1},{4,6},{5,7},{6,4},{7,5},{8,10},{9,11},{10,... | collective-permute-start | bytes 1179656 | tf_op jit(solution)/shard_map/ppermute | solution.py:626
  162.4 8.4 %collective-permute-start.14 = (f32[2,2,1088]{2,1,0:T(2,128)S(1)}, f32[2,2,1088]{2,1,0:T(2,128)S(1)}, u32[]{:S(2)}, u32[]{:S(2)}) collective-permute-start(f32[2,2,1088]{2,1,0:T(2,128)S(1)} %bitcast.204), channel_id=1, source_target_pairs={{0,4},{4,0},{8,12},{12,8},{1,5},{5,1},{9,13},{13,9},{2,6},{6,2},{1... | collective-permute-start | bytes 52232 | tf_op jit(solution)/shard_map/ppermute | solution.py:626
  163.3 8.7 %copy-start.6 = (bf16[2,2,2,96,512]{4,3,2,1,0:T(8,128)(2,1)S(1)}, bf16[2,2,2,96,512]{4,3,2,1,0:T(8,128)(2,1)}, u32[]{:S(2)}) copy-start(bf16[2,2,2,96,512]{4,3,2,1,0:T(8,128)(2,1)} %get-tuple-element.186) | copy-start | bytes 2359300
  174.4 11.3 %collective-permute-start.17 = (bf16[2,192,512]{2,1,0:T(8,128)(2,1)S(1)}, bf16[2,192,512]{2,1,0:T(8,128)(2,1)S(1)}, u32[]{:S(2)}, u32[]{:S(2)}) collective-permute-start(bf16[2,192,512]{2,1,0:T(8,128)(2,1)S(1)} %pad_maximum_fusion.2), channel_id=1, source_target_pairs={{0,8},{4,12},{8,0},{12,4},{1,9},{5,13},{9,1},{13,5},{2,10},{6,14},... | collective-permute-start | bytes 1179656 | tf_op jit(solution)/shard_map/ppermute | solution.py:626
  177.5 7.0 %collective-permute-start.15 = (bf16[2,2,2,32,512]{4,3,2,1,0:T(8,128)(2,1)S(1)}, bf16[2,2,2,32,512]{4,3,2,1,0:T(8,128)(2,1)S(1)}, u32[]{:S(2)}, u32[]{:S(2)}) collective-permute-start(bf16[2,2,2,32,512]{4,3,2,1,0:T(8,128)(2,1)S(1)} %get-tuple-element.184), channel_id=1, source_target_pairs={{0,2},{1,3},{2,0},{3,1},{4,6},{5,7},{6,4},{7,5},{8,10},{9,11},{10,... | collective-permute-start | bytes 786440 | tf_op jit(solution)/shard_map/ppermute | solution.py:626
  179.3 6.4 %collective-permute-start.16 = (bf16[2,2,2,32,512]{4,3,2,1,0:T(8,128)(2,1)S(1)}, bf16[2,2,2,32,512]{4,3,2,1,0:T(8,128)(2,1)S(1)}, u32[]{:S(2)}, u32[]{:S(2)}) collective-permute-start(bf16[2,2,2,32,512]{4,3,2,1,0:T(8,128)(2,1)S(1)} %get-tuple-element.183), channel_id=1, source_target_pairs={{0,4},{4,0},{8,12},{12,8},{1,5},{5,1},{9,13},{13,9},{2,6},{6,2},{1... | collective-permute-start | bytes 786440 | tf_op jit(solution)/shard_map/ppermute | solution.py:626
  185.7 25.3 %all-to-all-start.3 = ((bf16[4,4,64,512]{3,2,1,0:T(8,128)(2,1)}), bf16[4,4,64,512]{3,2,1,0:T(8,128)(2,1)S(1)}, u32[]{:S(2)}, u32[]{:S(2)}) async-start(bf16[4,4,64,512]{3,2,1,0:T(8,128)(2,1)} %backward_input.1), calls=%async_computation.3 | async-start | bytes 2097152 | tf_op jit(solution)/shard_map/all_to_all | solution.py:856
  189.3 21.7 %collective-permute-start.20 = (f32[2,1088]{1,0:T(2,128)S(1)}, f32[2,1088]{1,0:T(2,128)S(1)}, u32[]{:S(2)}, u32[]{:S(2)}) collective-permute-start(f32[2,1088]{1,0:T(2,128)S(1)} %bitcast.205), channel_id=1, source_target_pairs={{0,8},{4,12},{8,0},{12,4},{1,9},{5,13},{9,1},{13,5},{2,10},{6,14},... | collective-permute-start | bytes 26120 | tf_op jit(solution)/shard_map/ppermute | solution.py:626
  191.4 19.6 %collective-permute-start.18 = (bf16[2,2,32,512]{3,2,1,0:T(8,128)(2,1)S(1)}, bf16[2,2,32,512]{3,2,1,0:T(8,128)(2,1)S(1)}, u32[]{:S(2)}, u32[]{:S(2)}) collective-permute-start(bf16[2,2,32,512]{3,2,1,0:T(8,128)(2,1)S(1)} %fusion.22), channel_id=1, source_target_pairs={{0,4},{4,0},{8,12},{12,8},{1,5},{5,1},{9,13},{13,9},{2,6},{6,2},{1... | collective-permute-start | bytes 393224 | tf_op jit(solution)/shard_map/ppermute | solution.py:626
  192.9 9.6 %collective-permute-start.21 = (bf16[192,512]{1,0:T(8,128)(2,1)S(1)}, bf16[192,512]{1,0:T(8,128)(2,1)S(1)}, u32[]{:S(2)}, u32[]{:S(2)}) collective-permute-start(bf16[192,512]{1,0:T(8,128)(2,1)S(1)} %fusion.20), channel_id=1, source_target_pairs={{0,16},{16,0},{1,17},{17,1},{2,18},{18,2},{3,19},{19,3},{4,20},{20... | collective-permute-start | bytes 589832 | tf_op jit(solution)/shard_map/ppermute | solution.py:626
  196.4 14.6 %collective-permute-start.19 = (bf16[2,2,32,512]{3,2,1,0:T(8,128)(2,1)S(1)}, bf16[2,2,32,512]{3,2,1,0:T(8,128)(2,1)S(1)}, u32[]{:S(2)}, u32[]{:S(2)}) collective-permute-start(bf16[2,2,32,512]{3,2,1,0:T(8,128)(2,1)S(1)} %fusion.23), channel_id=1, source_target_pairs={{0,2},{1,3},{2,0},{3,1},{4,6},{5,7},{6,4},{7,5},{8,10},{9,11},{10,... | collective-permute-start | bytes 393224 | tf_op jit(solution)/shard_map/ppermute | solution.py:626
  211.0 8.9 %copy-start.9 = (bf16[4,4,64,512]{3,2,1,0:T(8,128)(2,1)}, bf16[4,4,64,512]{3,2,1,0:T(8,128)(2,1)S(1)}, u32[]{:S(2)}) copy-start(bf16[4,4,64,512]{3,2,1,0:T(8,128)(2,1)S(1)} %all-to-all-done.3) | copy-start | bytes 3145732
  211.2 13.5 %collective-permute-start.22 = (bf16[64,512]{1,0:T(8,128)(2,1)S(1)}, bf16[64,512]{1,0:T(8,128)(2,1)S(1)}, u32[]{:S(2)}, u32[]{:S(2)}) collective-permute-start(bf16[64,512]{1,0:T(8,128)(2,1)S(1)} %get-tuple-element.202), channel_id=1, source_target_pairs={{0,16},{4,20},{8,24},{12,28},{16,0},{20,4},{24,8},{28,12},{1,17},{... | collective-permute-start | bytes 196616 | tf_op jit(solution)/shard_map/ppermute | solution.py:823
  214.6 10.1 %collective-permute-start.23 = (bf16[64,512]{1,0:T(8,128)(2,1)S(1)}, bf16[64,512]{1,0:T(8,128)(2,1)S(1)}, u32[]{:S(2)}, u32[]{:S(2)}) collective-permute-start(bf16[64,512]{1,0:T(8,128)(2,1)S(1)} %get-tuple-element.203), channel_id=1, source_target_pairs={{0,8},{4,12},{8,0},{12,4},{16,24},{20,28},{24,16},{28,20},{1,9},{5... | collective-permute-start | bytes 196616 | tf_op jit(solution)/shard_map/ppermute | solution.py:823
  216.9 7.8 %collective-permute-start.24 = (bf16[64,512]{1,0:T(8,128)(2,1)S(1)}, bf16[64,512]{1,0:T(8,128)(2,1)S(1)}, u32[]{:S(2)}, u32[]{:S(2)}) collective-permute-start(bf16[64,512]{1,0:T(8,128)(2,1)S(1)} %get-tuple-element.201), channel_id=1, source_target_pairs={{0,24},{4,28},{8,16},{12,20},{16,8},{20,12},{24,0},{28,4},{1,25},{... | collective-permute-start | bytes 196616 | tf_op jit(solution)/shard_map/ppermute | solution.py:823
  219.3 5.4 %collective-permute-start.25 = (f32[1088]{0:T(1024)S(1)}, f32[1088]{0:T(1024)S(1)}, u32[]{:S(2)}, u32[]{:S(2)}) collective-permute-start(f32[1088]{0:T(1024)S(1)} %get-tuple-element.181), channel_id=1, source_target_pairs={{0,16},{16,0},{1,17},{17,1},{2,18},{18,2},{3,19},{19,3},{4,20},{20... | collective-permute-start | bytes 13064 | tf_op jit(solution)/shard_map/ppermute | solution.py:626

commit v5 on v4

--- a/solution.py
+++ b/solution.py
@@ -421,9 +421,8 @@
             fw_ref[:, cols], sw_ref[:, cols] = feature, sample
         else:
             fm_ref[...], sm_ref[...] = feature, sample
-        ew_ref[:, cols] = early_ref[feat, 96:160].astype(F32)
-        rw_ref[unit * 64 : unit * 64 + 32] = early_ref[feat, 64:96].astype(F32)
-        rw_ref[unit * 64 + 32 : unit * 64 + 64] = early_ref[feat, 160:192].astype(F32)
+        ew_ref[:, cols] = early_ref[feat, 64:128].astype(F32)
+        rw_ref[unit * 64 : unit * 64 + 64] = early_ref[feat, 128:192].astype(F32)
     planes = last_ref[:, 64:88].astype(F32)
     total = (planes[0] + planes[1]) + (planes[2] + planes[3])
     total = total[0:8] + total[8:16] + total[16:24]
@@ -484,10 +483,8 @@
     def from_hidden(n):
         piece = mm(hid[:, block(n)], gb3[...], 0, 0).astype(BF)
         for i in range(8):
-            for part in range(2):
-                at = i * 64 + part * 32
-                rows = piece[at : at + 32]
-                place_piece(part, rows, i % 4, 2 * n + i // 4, slice(64, 96))
+            rows = piece[i * 64 : (i + 1) * 64]
+            place_piece(1, rows, i % 4, 2 * n + i // 4, slice(64, 128))
 
     loop(4, from_hidden)
     turn[...] = act3[...].T
@@ -751,11 +748,11 @@
             + [vmem((1024, n)) for n in (512, 1536, 512, 512, 512, 2048, 2048, 512)]
             + [
                 vmem((4, 256, 512)), vmem((4, 256, 512)), rows, rows, rows, rows32, rows32, rows,
-                rows, rows32, rows32, vmem((32, 96, 512)), vmem((32, 96, 512)), vmem((512, 1024)),
+                rows, rows32, rows32, vmem((32, 64, 512)), vmem((32, 128, 512)), vmem((512, 1024)),
                 pltpu.SemaphoreType.DMA((4,)), pltpu.SemaphoreType.DMA((4,)),
             ],
         ),
-        out_shape=outs + (big((256, 512)),) * 4 + (sds((16, 96, 512)),) * 4,
+        out_shape=outs + (big((256, 512)),) * 4 + (sds((16, 64, 512)),) * 2 + (sds((16, 128, 512)),) * 2,
         compiler_params=params(58),
         cost_estimate=cost(45),
         name="middle",
@@ -769,7 +766,7 @@
 
     gb_t = exchange(gb1_f)
     outs = [shuffle(out, "feat", d + 1) for d, out in enumerate((out1, out2, out3))]
-    pk, ps, qk, qs = (g.reshape(2, 2, 2, 2, 96, 512) for g in grads)
+    pk, ps, qk, qs = (g.reshape(2, 2, 2, 2, -1, 512) for g in grads)
     p_chain, q_chain = Chain(pk, ps, (X, Y)), Chain(qk, qs, (Y, X))
     chains = [p_chain, q_chain]
     for chain in chains:

time: 235 us -> 234 us (level)
  starting transfers between devices: 48.5 us -> 45 us
    convert_element_type x13 -> x12, other arithmetic: 10.7 us -> 10.8 us  [plus(): return (a.astype(F32) + b.astype(F32)).astype(BF)]
  transfers between devices with their start and end apart: 29 -> 29, of which waited for: 10 -> 11; matrix products, arithmetic and copies ran while one was open for 6% -> 6% of each run, Pallas kernels for 12% -> 12%
where the time goes in v5:
time: 234 us; the launch traced here: 233 us
  Pallas kernels  83.9 us (36%)
  waiting for transfers between devices  45.1 us (19%)
  starting transfers between devices  45 us (19%)
  blocking collectives  35.7 us (15%)
  other arithmetic  13.2 us (6%)
  between operations  5.28 us (2%)
  local copies, waits for them, and re-layouts  5.02 us (2%)
    pallas_call x1, Pallas kernels, local_small(): pl.pallas_call(middle, grid_spec=pltpu.PrefetchScalarGridSpec(num_scalar_...  41.5 us
    ppermute x23, waiting for transfers between devices, shuffle(): return lax.ppermute(value, axis, [(i, i ^ mask) for i in range(size)])  41.3 us
    pallas_call x4, Pallas kernels, by_feature(): pl.pallas_call(kernel, grid=(4 // per,), out_shape=tuple((out for out, _...  32.3 us
    ppermute x23, starting transfers between devices, shuffle(): return lax.ppermute(value, axis, [(i, i ^ mask) for i in range(size)])  24.9 us
    all_to_all x1, blocking collectives, exchange(): return lax.all_to_all(value, ('quad', 'feat'), 0, 0).reshape(shape)  20.7 us
    convert_element_type x12, other arithmetic, plus(): return (a.astype(F32) + b.astype(F32)).astype(BF)  10.8 us
    pallas_call x5, Pallas kernels, whole(): pl.pallas_call(kernel, grid=(steps,), out_shape=outs, in_specs=specs, out...  10.1 us
    all_gather x1, blocking collectives, local_small(): early = lax.all_gather(both_chain.keep, 'feat')  8.43 us
  transfers between devices with their start and end apart: 29, of which 11 were waited for; matrix products, arithmetic and copies ran while one was open for 6% of the time, Pallas kernels for 12%

profile of v5, /device:TPU:0, one launch (start us, length us, event | category | flops | bytes accessed | tf_op | source)
XLA Modules:
  0.0 233.2 jit_solution(2432048404324645813)
XLA Ops:
  0.7 2.6 %turn_in.1 = bf16[16,4,16,512]{3,2,1,0:T(8,128)(2,1)} custom-call(bf16[1024,512]{1,0:T(8,128)(2,1)} %bitcast.207), custom_call_target="tpu_custom_call" | custom-call | flops 3300000000 | bytes 6000000 | tf_op jit(solution)/shard_map/turn_in/pallas_call | solution.py:608
  3.3 5.4 %all-to-all-start = ((bf16[4,4,64,512]{3,2,1,0:T(8,128)(2,1)}), bf16[4,4,64,512]{3,2,1,0:T(8,128)(2,1)S(1)}, u32[]{:S(2)}, u32[]{:S(2)}) async-start(bf16[4,4,64,512]{3,2,1,0:T(8,128)(2,1)} %bitcast.192), calls=%async_computation | async-start | bytes 2097152 | tf_op jit(solution)/shard_map/all_to_all | solution.py:681
  9.0 1.8 collective-permute-done.refs_2_
  10.9 1.6 collective-permute-start.1
  17.6 7.3 %collective-permute-done.1.refs_3_.refs_4_ = bf16[2,256,512]{2,1,0:T(8,128)(2,1)S(1)} collective-permute-done((bf16[2,256,512]{2,1,0:T(8,128)(2,1)S(1)}, bf16[2,256,512]{2,1,0:T(8,128)(2,1)S(1)}, u32[]{:S(2)}, u32[]{:S(2)}) %collective-permute-start.1) | collective-permute-done | bytes 524320 | tf_op jit(solution)/shard_map/ppermute | solution.py:623
  25.0 2.7 %collective-permute-start.2 = (bf16[4,64,512]{2,1,0:T(8,128)(2,1)S(1)}, bf16[4,64,512]{2,1,0:T(8,128)(2,1)S(1)}, u32[]{:S(2)}, u32[]{:S(2)}) collective-permute-start(bf16[4,64,512]{2,1,0:T(8,128)(2,1)S(1)} %dynamic-slice_bitcast_fusion.own_ref), channel_id=1, source_target_pairs={{0,16},{16,0},{1,17},{17,1},{2,18},{18,2},{3,19},{19,3},{4,20},{20... | collective-permute-start | bytes 786440 | tf_op jit(solution)/shard_map/ppermute | solution.py:623
  27.7 4.9 %project_queries.1 = (bf16[4,256,512]{2,1,0:T(8,128)(2,1)}, bf16[4,256,512]{2,1,0:T(8,128)(2,1)}) custom-call(bf16[4,4,64,512]{3,2,1,0:T(8,128)(2,1)} %copy-done.9, f32[1,512]{1,0:T(1,128)S(1)} %bitcast.184, f32[1,512]{1,0:T(1,128)S(1)} %bitcast.181, bf16[512,1536]{1,0:T(8,128)(2,1)} %w_ref.5, f32[1,1024]{1,0:T(1,128)S(1)} %bitcast.179), custom_call_target="tpu_custom_call" | custom-call | flops 3300000000 | bytes 6000000 | tf_op jit(solution)/shard_map/project_queries/pallas_call | solution.py:578
  32.6 6.5 %collective-permute-done.2.got_ref = bf16[4,64,512]{2,1,0:T(8,128)(2,1)S(1)} collective-permute-done((bf16[4,64,512]{2,1,0:T(8,128)(2,1)S(1)}, bf16[4,64,512]{2,1,0:T(8,128)(2,1)S(1)}, u32[]{:S(2)}, u32[]{:S(2)}) %collective-permute-start.2) | collective-permute-done | bytes 262176 | tf_op jit(solution)/shard_map/ppermute | solution.py:623
  39.8 8.2 %forward_one.1 = (bf16[4,4,4,16,512]{4,3,2,1,0:T(8,128)(2,1)}, bf16[4,256,512]{2,1,0:T(8,128)(2,1)}, bf16[4,64,512]{2,1,0:T(8,128)(2,1)}, bf16[4,64,512]{2,1,0:T...) custom-call(s32[8]{0:T(128)S(1)} %stack.44.me_ref, ...), custom_call_target="tpu_custom_call" | custom-call | flops 7699999744 | bytes 14000000 | tf_op jit(solution)/shard_map/forward_one/pallas_call | solution.py:578
  47.9 20.7 %all_to_all.20 = bf16[16,4,16,512]{3,2,1,0:T(8,128)(2,1)} all-to-all(bf16[16,4,16,512]{3,2,1,0:T(8,128)(2,1)} %bitcast.196), channel_id=1, replica_groups=mesh['half'=2,'quad'=4,'feat'=4] {'quad','feat'}, dimensions={0} | all-to-all | bytes 2097152 | tf_op jit(solution)/shard_map/all_to_all | solution.py:716
  68.7 41.5 %middle.1 = (bf16[4,4,4,16,512]{4,3,2,1,0:T(8,128)(2,1)}, f32[8,512]{1,0:T(8,128)}, f32[1,2048]{1,0:T(1,128)}, bf16[256,512]{1,0:T(8,128)(2,1)}, bf16[256,512]{1...) custom-call(s32[8]{0:T(128)} %copy-done, ...), custom_call_target="tpu_custom_call" | custom-call | flops 49500000256 | bytes 90000000 | tf_op jit(solution)/shard_map/middle/pallas_call | solution.py:735
  110.2 4.5 %all-to-all-start.2 = ((bf16[16,4,16,512]{3,2,1,0:T(8,128)(2,1)}), bf16[16,4,16,512]{3,2,1,0:T(8,128)(2,1)}, u32[]{:S(2)}, u32[]{:S(2)}) async-start(bf16[16,4,16,512]{3,2,1,0:T(8,128)(2,1)} %bitcast.193), calls=%async_computation.2 | async-start | bytes 2097152 | tf_op jit(solution)/shard_map/all_to_all | solution.py:716
  115.3 1.7 collective-permute-start.4
  118.5 1.3 fusion.40
  119.9 1.3 fusion.4
  121.3 1.5 collective-permute-start.7
  122.7 3.1 %fusion.1 = (bf16[2,2,2,128,512]{4,3,2,1,0:T(8,128)(2,1)S(1)}, bf16[2,2,2,128,512]{4,3,2,1,0:T(8,128)(2,1)}) fusion(bf16[2,2,2,128,512]{4,3,2,1,0:T(8,128)(2,1)S(1)} %bitcast.188, bf16[2,2,2,2,128,512]{5,4,3,2,1,0:T(8,128)(2,1)} %collective-permute-done.9, bf16[2,2,2,128,512]{4,3,2,1,0:T(8,128)(2,1)S(1)} %bitcast.189), kind=kLoop, calls=%fused_computation.3 | loop fusion | flops 4194304 | bytes 6291456 | tf_op jit(solution)/shard_map/convert_element_type | solution.py:639
  125.8 1.5 collective-permute-start.10
  127.3 3.8 %all-to-all-done.2 = bf16[16,4,16,512]{3,2,1,0:T(8,128)(2,1)} async-done(((bf16[16,4,16,512]{3,2,1,0:T(8,128)(2,1)}), bf16[16,4,16,512]{3,2,1,0:T(8,128)(2,1)}, u32[]{:S(2)}, u32[]{:S(2)}) %all-to-all-start.2) | async-done | bytes 1048608 | tf_op jit(solution)/shard_map/all_to_all | solution.py:716
  131.1 14.3 %backward_one.1 = (bf16[4,256,512]{2,1,0:T(8,128)(2,1)}, f32[4,256,512]{2,1,0:T(8,128)}, bf16[4,64,512]{2,1,0:T(8,128)(2,1)}, f32[8,512]{1,0:T(8,128)S(1)}, bf16...) custom-call(s32[8]{0:T(128)S(1)} %copy-done.1, bf16[4,4,4,16,512]{4,3,2,1,0:T(8,128)(2,1)} %bitcast.30.g_ref, ...), custom_call_target="tpu_custom_call" | custom-call | flops 13200000000 | bytes 24000000 | tf_op jit(solution)/shard_map/backward_one/pallas_call | solution.py:578
  145.5 7.2 %collective-permute-done.7 = bf16[2,2,2,64,512]{4,3,2,1,0:T(8,128)(2,1)} collective-permute-done((bf16[2,2,2,64,512]{4,3,2,1,0:T(8,128)(2,1)}, bf16[2,2,2,64,512]{4,3,2,1,0:T(8,128)(2,1)}, u32[]{:S(2)}, u32[]{:S(2)}) %collective-permute-start.7) | collective-permute-done | bytes 524320 | tf_op jit(solution)/shard_map/ppermute | solution.py:623
  152.7 1.0 fusion.9
  154.3 3.4 %collective-permute-start.12 = (bf16[4,64,512]{2,1,0:T(8,128)(2,1)}, bf16[4,64,512]{2,1,0:T(8,128)(2,1)}, u32[]{:S(2)}, u32[]{:S(2)}) collective-permute-start(bf16[4,64,512]{2,1,0:T(8,128)(2,1)} %get-tuple-element.131.term_ref), channel_id=1, source_target_pairs={{0,16},{16,0},{1,17},{17,1},{2,18},{18,2},{3,19},{19,3},{4,20},{20... | collective-permute-start | bytes 786440 | tf_op jit(solution)/shard_map/ppermute | solution.py:623
  157.9 1.2 fusion.5
  159.1 0.9 collective-permute-start.11
  160.8 2.2 place.1
  163.8 5.6 %collective-permute-done.12.got_ref = bf16[4,64,512]{2,1,0:T(8,128)(2,1)} collective-permute-done((bf16[4,64,512]{2,1,0:T(8,128)(2,1)}, bf16[4,64,512]{2,1,0:T(8,128)(2,1)}, u32[]{:S(2)}, u32[]{:S(2)}) %collective-permute-start.12) | collective-permute-done | bytes 262176 | tf_op jit(solution)/shard_map/ppermute | solution.py:623
  169.5 2.6 %collective-permute-done.11 = bf16[2,2,128,512]{3,2,1,0:T(8,128)(2,1)S(1)} collective-permute-done((bf16[2,2,128,512]{3,2,1,0:T(8,128)(2,1)S(1)}, bf16[2,2,128,512]{3,2,1,0:T(8,128)(2,1)S(1)}, u32[]{:S(2)}, u32[]{:S(2)}) %collective-permute-start.11) | collective-permute-done | bytes 524320 | tf_op jit(solution)/shard_map/ppermute | solution.py:623
  172.0 1.3 fusion.2
  173.4 1.2 fusion.7
  174.6 1.6 collective-permute-start.17
  176.2 1.5 add_convert_fusion.2
  177.7 1.8 collective-permute-start.15
  179.9 4.9 %backward_input.1 = bf16[4,4,64,512]{3,2,1,0:T(8,128)(2,1)} custom-call(s32[8]{0:T(128)S(1)} %copy-done.1, bf16[4,256,512]{2,1,0:T(8,128)(2,1)} %get-tuple-element.139.gb1_ref, bf16[4,4,64,512]{3,2,1,0:T(8,128)(2,1)} %copy-done.9, f32[4,256,512]{2,1,0:T(8,128)} %get-tuple-element.140.a_ref, bf16[4,64,512]{2,1,0:T(8,128)(2,1)} %get-tuple-element.131.term_ref, ...), custom_call_target="tpu_custom_call" | custom-call | flops 3300000000 | bytes 6000000 | tf_op jit(solution)/shard_map/backward_input/pallas_call | solution.py:578
  184.8 1.1 collective-permute-done.16
  185.9 3.5 %all-to-all-start.3 = ((bf16[4,4,64,512]{3,2,1,0:T(8,128)(2,1)}), bf16[4,4,64,512]{3,2,1,0:T(8,128)(2,1)S(1)}, u32[]{:S(2)}, u32[]{:S(2)}) async-start(bf16[4,4,64,512]{3,2,1,0:T(8,128)(2,1)} %backward_input.1), calls=%async_computation.3 | async-start | bytes 2097152 | tf_op jit(solution)/shard_map/all_to_all | solution.py:853
  190.1 2.0 collective-permute-start.20
  192.1 1.5 collective-permute-start.18
  194.1 1.3 collective-permute-start.19
  195.4 7.1 %collective-permute-done.21 = bf16[192,512]{1,0:T(8,128)(2,1)S(1)} collective-permute-done((bf16[192,512]{1,0:T(8,128)(2,1)S(1)}, bf16[192,512]{1,0:T(8,128)(2,1)S(1)}, u32[]{:S(2)}, u32[]{:S(2)}) %collective-permute-start.21) | collective-permute-done | bytes 196640 | tf_op jit(solution)/shard_map/ppermute | solution.py:623
  202.5 8.4 %all-gather = bf16[768,512]{1,0:T(8,128)(2,1)} all-gather(bf16[192,512]{1,0:T(8,128)(2,1)S(1)} %fusion.8), channel_id=2, replica_groups=mesh['half'=2,'quad'=4,'feat'=4] {'feat'}, dimensions={0}, use_global_device_ids=true | all-gather | bytes 983040 | tf_op jit(solution)/shard_map/all_gather | solution.py:849
  211.7 3.4 %collective-permute-start.22 = (bf16[64,512]{1,0:T(8,128)(2,1)S(1)}, bf16[64,512]{1,0:T(8,128)(2,1)S(1)}, u32[]{:S(2)}, u32[]{:S(2)}) collective-permute-start(bf16[64,512]{1,0:T(8,128)(2,1)S(1)} %get-tuple-element.200), channel_id=1, source_target_pairs={{0,16},{4,20},{8,24},{12,28},{16,0},{20,4},{24,8},{28,12},{1,17},{... | collective-permute-start | bytes 196616 | tf_op jit(solution)/shard_map/ppermute | solution.py:820
  215.1 1.0 collective-permute-start.23
  216.1 2.3 collective-permute-start.24
  219.8 2.6 %turn_out.1 = bf16[1024,512]{1,0:T(8,128)(2,1)} custom-call(bf16[16,4,16,512]{3,2,1,0:T(8,128)(2,1)} %bitcast.194), custom_call_target="tpu_custom_call" | custom-call | flops 3300000000 | bytes 6000000 | tf_op jit(solution)/shard_map/turn_out/pallas_call | solution.py:608
  222.4 1.4 collective-permute-done.25
  223.9 6.5 %all-gather.1 = bf16[352,512]{1,0:T(8,128)(2,1)} all-gather(bf16[88,512]{1,0:T(8,128)(2,1)S(1)} %pad_maximum_fusion.4), channel_id=3, replica_groups=mesh['half'=2,'quad'=4,'feat'=4] {'feat'}, dimensions={0}, use_global_device_ids=true | all-gather | bytes 450560 | tf_op jit(solution)/shard_map/all_gather | solution.py:871
  230.5 2.6 %finale.1 = (f32[64,1536]{1,0:T(8,128)}, f32[64,512]{1,0:T(8,128)}, f32[64,2048]{1,0:T(8,128)}, f32[256,512]{1,0:T(8,128)}, f32[64,1536]{1,0:T(8,128)}, /*index=...) custom-call(bf16[4,192,512]{2,1,0:T(8,128)(2,1)} %bitcast.197, ...), custom_call_target="tpu_custom_call" | custom-call | flops 3300000000 | bytes 6000000 | tf_op jit(solution)/shard_map/finale/pallas_call | solution.py:608
  (129 shorter events, 10.9 us)
Async XLA Ops:
  3.3 5.4 %copy-start.11 = (bf16[64,16,512]{2,1,0:T(8,128)(2,1)S(1)}, bf16[64,16,512]{2,1,0:T(8,128)(2,1)}, u32[]{:S(2)}) copy-start(bf16[64,16,512]{2,1,0:T(8,128)(2,1)} %param.43) | copy-start | bytes 3145732
  3.3 5.6 %copy-start.18 = (s32[512]{0:T(512)S(1)}, s32[512]{0:T(512)}, u32[]{:S(2)}) copy-start(s32[512]{0:T(512)} %param.24) | copy-start | bytes 6148
  3.3 21.6 %all-to-all-start = ((bf16[4,4,64,512]{3,2,1,0:T(8,128)(2,1)}), bf16[4,4,64,512]{3,2,1,0:T(8,128)(2,1)S(1)}, u32[]{:S(2)}, u32[]{:S(2)}) async-start(bf16[4,4,64,512]{3,2,1,0:T(8,128)(2,1)} %bitcast.192), calls=%async_computation | async-start | bytes 2097152 | tf_op jit(solution)/shard_map/all_to_all | solution.py:681
  8.7 7.2 %copy-start.16 = (s32[512]{0:T(512)S(1)}, s32[512]{0:T(512)}, u32[]{:S(2)}) copy-start(s32[512]{0:T(512)} %param.23) | copy-start | bytes 6148
  8.7 18.9 %copy-start.2 = (f32[1024]{0:T(1024)S(1)}, f32[1024]{0:T(1024)}, u32[]{:S(2)}) copy-start(f32[1024]{0:T(1024)} %param.28) | copy-start | bytes 12292
  8.8 18.9 %copy-start.3 = (f32[512]{0:T(512)S(1)}, f32[512]{0:T(512)}, u32[]{:S(2)}) copy-start(f32[512]{0:T(512)} %param.26) | copy-start | bytes 6148
  8.8 18.9 %copy-start.5 = (f32[512]{0:T(512)S(1)}, f32[512]{0:T(512)}, u32[]{:S(2)}) copy-start(f32[512]{0:T(512)} %param.25) | copy-start | bytes 6148
  8.8 2.0 collective-permute-start
  10.8 21.8 %copy-start.13 = (bf16[2,256,512]{2,1,0:T(8,128)(2,1)}, bf16[2,256,512]{2,1,0:T(8,128)(2,1)S(1)}, u32[]{:S(2)}) copy-start(bf16[2,256,512]{2,1,0:T(8,128)(2,1)S(1)} %collective-permute-done.refs_2_) | copy-start | bytes 1572868
  10.9 14.0 %collective-permute-start.1 = (bf16[2,256,512]{2,1,0:T(8,128)(2,1)S(1)}, bf16[2,256,512]{2,1,0:T(8,128)(2,1)S(1)}, u32[]{:S(2)}, u32[]{:S(2)}) collective-permute-start(bf16[2,256,512]{2,1,0:T(8,128)(2,1)S(1)} %pad_maximum_fusion.1), channel_id=1, source_target_pairs={{0,2},{1,3},{2,0},{3,1},{4,6},{5,7},{6,4},{7,5},{8,10},{9,11},{10,... | collective-permute-start | bytes 1572872 | tf_op jit(solution)/shard_map/ppermute | solution.py:623
  17.5 21.6 %copy-start = (s32[8]{0:T(128)}, s32[8]{0:T(128)S(1)}, u32[]{:S(2)}) copy-start(s32[8]{0:T(128)S(1)} %stack.44.me_ref) | copy-start | bytes 100
  24.9 7.7 %copy-start.19 = (bf16[2,256,512]{2,1,0:T(8,128)(2,1)}, bf16[2,256,512]{2,1,0:T(8,128)(2,1)S(1)}, u32[]{:S(2)}) copy-start(bf16[2,256,512]{2,1,0:T(8,128)(2,1)S(1)} %collective-permute-done.1.refs_3_.refs_4_) | copy-start | bytes 1572868
  24.9 2.7 %copy-start.9 = (bf16[4,4,64,512]{3,2,1,0:T(8,128)(2,1)}, bf16[4,4,64,512]{3,2,1,0:T(8,128)(2,1)S(1)}, u32[]{:S(2)}) copy-start(bf16[4,4,64,512]{3,2,1,0:T(8,128)(2,1)S(1)} %all-to-all-done.x_ref) | copy-start | bytes 3145732
  25.0 7.6 %copy-start.12 = (bf16[4,64,512]{2,1,0:T(8,128)(2,1)}, bf16[4,64,512]{2,1,0:T(8,128)(2,1)S(1)}, u32[]{:S(2)}) copy-start(bf16[4,64,512]{2,1,0:T(8,128)(2,1)S(1)} %dynamic-slice_bitcast_fusion.own_ref) | copy-start | bytes 786436
  25.0 14.1 %collective-permute-start.2 = (bf16[4,64,512]{2,1,0:T(8,128)(2,1)S(1)}, bf16[4,64,512]{2,1,0:T(8,128)(2,1)S(1)}, u32[]{:S(2)}, u32[]{:S(2)}) collective-permute-start(bf16[4,64,512]{2,1,0:T(8,128)(2,1)S(1)} %dynamic-slice_bitcast_fusion.own_ref), channel_id=1, source_target_pairs={{0,16},{16,0},{1,17},{17,1},{2,18},{18,2},{3,19},{19,3},{4,20},{20... | collective-permute-start | bytes 786440 | tf_op jit(solution)/shard_map/ppermute | solution.py:623
  27.6 12.1 %copy-start.4 = (f32[512]{0:T(512)S(1)}, f32[512]{0:T(512)}, u32[]{:S(2)}) copy-start(f32[512]{0:T(512)} %param.30) | copy-start | bytes 6148
  110.1 6.9 %copy-start.14 = (f32[8,512]{1,0:T(8,128)S(1)}, f32[8,512]{1,0:T(8,128)}, u32[]{:S(2)}) copy-start(f32[8,512]{1,0:T(8,128)} %get-tuple-element.133) | copy-start | bytes 49156
  110.1 7.6 %copy-start.17 = (f32[1,2048]{1,0:T(1,128)S(1)}, f32[1,2048]{1,0:T(1,128)}, u32[]{:S(2)}) copy-start(f32[1,2048]{1,0:T(1,128)} %get-tuple-element.134) | copy-start | bytes 24580
  110.1 12.6 %collective-permute-start.9 = (bf16[2,2,2,2,128,512]{5,4,3,2,1,0:T(8,128)(2,1)}, bf16[2,2,2,2,128,512]{5,4,3,2,1,0:T(8,128)(2,1)}, u32[]{:S(2)}, u32[]{:S(2)}) collective-permute-start(bf16[2,2,2,2,128,512]{5,4,3,2,1,0:T(8,128)(2,1)} %bitcast.206), channel_id=1, source_target_pairs={{0,1},{1,0},{2,3},{3,2},{4,5},{5,4},{6,7},{7,6},{8,9},{9,8},{10,11... | collective-permute-start | bytes 6291464 | tf_op jit(solution)/shard_map/ppermute | solution.py:623
  110.2 9.6 %copy-start.6 = (bf16[16,128,512]{2,1,0:T(8,128)(2,1)S(1)}, bf16[16,128,512]{2,1,0:T(8,128)(2,1)}, u32[]{:S(2)}) copy-start(bf16[16,128,512]{2,1,0:T(8,128)(2,1)} %get-tuple-element.129) | copy-start | bytes 6291460
  110.2 20.8 %all-to-all-start.2 = ((bf16[16,4,16,512]{3,2,1,0:T(8,128)(2,1)}), bf16[16,4,16,512]{3,2,1,0:T(8,128)(2,1)}, u32[]{:S(2)}, u32[]{:S(2)}) async-start(bf16[16,4,16,512]{3,2,1,0:T(8,128)(2,1)} %bitcast.193), calls=%async_computation.2 | async-start | bytes 2097152 | tf_op jit(solution)/shard_map/all_to_all | solution.py:716
  114.7 5.2 %collective-permute-start.6 = (bf16[2,2,2,2,64,512]{5,4,3,2,1,0:T(8,128)(2,1)}, bf16[2,2,2,2,64,512]{5,4,3,2,1,0:T(8,128)(2,1)S(1)}, u32[]{:S(2)}, u32[]{:S(2)}) collective-permute-start(bf16[2,2,2,2,64,512]{5,4,3,2,1,0:T(8,128)(2,1)} %bitcast.208), channel_id=1, source_target_pairs={{0,1},{1,0},{2,3},{3,2},{4,5},{5,4},{6,7},{7,6},{8,9},{9,8},{10,11... | collective-permute-start | bytes 3145736 | tf_op jit(solution)/shard_map/ppermute | solution.py:623
  115.2 30.2 %collective-permute-start.3 = (bf16[256,512]{1,0:T(8,128)(2,1)}, bf16[256,512]{1,0:T(8,128)(2,1)}, u32[]{:S(2)}, u32[]{:S(2)}) collective-permute-start(bf16[256,512]{1,0:T(8,128)(2,1)} %get-tuple-element.123), channel_id=1, source_target_pairs={{0,1},{1,0},{2,3},{3,2},{4,5},{5,4},{6,7},{7,6},{8,9},{9,8},{10,11... | collective-permute-start | bytes 786440 | tf_op jit(solution)/shard_map/ppermute | solution.py:623
  115.3 30.1 %collective-permute-start.4 = (bf16[256,512]{1,0:T(8,128)(2,1)}, bf16[256,512]{1,0:T(8,128)(2,1)}, u32[]{:S(2)}, u32[]{:S(2)}) collective-permute-start(bf16[256,512]{1,0:T(8,128)(2,1)} %get-tuple-element.124), channel_id=1, source_target_pairs={{0,2},{1,3},{2,0},{3,1},{4,6},{5,7},{6,4},{7,5},{8,10},{9,11},{10,... | collective-permute-start | bytes 786440 | tf_op jit(solution)/shard_map/ppermute | solution.py:623
  117.0 28.4 %collective-permute-start.5 = (bf16[256,512]{1,0:T(8,128)(2,1)}, bf16[256,512]{1,0:T(8,128)(2,1)}, u32[]{:S(2)}, u32[]{:S(2)}) collective-permute-start(bf16[256,512]{1,0:T(8,128)(2,1)} %get-tuple-element.125), channel_id=1, source_target_pairs={{0,3},{1,2},{2,1},{3,0},{4,7},{5,6},{6,5},{7,4},{8,11},{9,10},{10,... | collective-permute-start | bytes 786440 | tf_op jit(solution)/shard_map/ppermute | solution.py:623
  121.3 31.4 %collective-permute-start.7 = (bf16[2,2,2,64,512]{4,3,2,1,0:T(8,128)(2,1)}, bf16[2,2,2,64,512]{4,3,2,1,0:T(8,128)(2,1)}, u32[]{:S(2)}, u32[]{:S(2)}) collective-permute-start(bf16[2,2,2,64,512]{4,3,2,1,0:T(8,128)(2,1)} %get-tuple-element.191), channel_id=1, source_target_pairs={{0,2},{1,3},{2,0},{3,1},{4,6},{5,7},{6,4},{7,5},{8,10},{9,11},{10,... | collective-permute-start | bytes 1572872 | tf_op jit(solution)/shard_map/ppermute | solution.py:623
  122.7 8.3 %copy-start.1 = (s32[8]{0:T(128)S(1)}, s32[8]{0:T(128)}, u32[]{:S(2)}) copy-start(s32[8]{0:T(128)} %copy-done) | copy-start | bytes 100
  125.8 32.1 %collective-permute-start.10 = (bf16[2,2,2,128,512]{4,3,2,1,0:T(8,128)(2,1)}, bf16[2,2,2,128,512]{4,3,2,1,0:T(8,128)(2,1)}, u32[]{:S(2)}, u32[]{:S(2)}) collective-permute-start(bf16[2,2,2,128,512]{4,3,2,1,0:T(8,128)(2,1)} %get-tuple-element.187), channel_id=1, source_target_pairs={{0,4},{4,0},{8,12},{12,8},{1,5},{5,1},{9,13},{13,9},{2,6},{6,2},{1... | collective-permute-start | bytes 3145736 | tf_op jit(solution)/shard_map/ppermute | solution.py:623
  131.1 21.6 %copy-start.7 = (bf16[2,2,2,64,512]{4,3,2,1,0:T(8,128)(2,1)S(1)}, bf16[2,2,2,64,512]{4,3,2,1,0:T(8,128)(2,1)}, u32[]{:S(2)}) copy-start(bf16[2,2,2,64,512]{4,3,2,1,0:T(8,128)(2,1)} %get-tuple-element.190) | copy-start | bytes 1572868
  145.4 24.0 %collective-permute-start.13 = (bf16[2,16,32,512]{3,2,1,0:T(8,128)(2,1)S(1)}, bf16[2,16,32,512]{3,2,1,0:T(8,128)(2,1)}, u32[]{:S(2)}, u32[]{:S(2)}) collective-permute-start(bf16[2,16,32,512]{3,2,1,0:T(8,128)(2,1)S(1)} %get-tuple-element.132), channel_id=1, source_target_pairs={{0,1},{1,0},{2,3},{3,2},{4,5},{5,4},{6,7},{7,6},{8,9},{9,8},{10,11... | collective-permute-start | bytes 3145736 | tf_op jit(solution)/shard_map/ppermute | solution.py:623
  153.7 9.3 %collective-permute-start.8 = (bf16[2,2,64,512]{3,2,1,0:T(8,128)(2,1)S(1)}, bf16[2,2,64,512]{3,2,1,0:T(8,128)(2,1)}, u32[]{:S(2)}, u32[]{:S(2)}) collective-permute-start(bf16[2,2,64,512]{3,2,1,0:T(8,128)(2,1)S(1)} %fusion.9), channel_id=1, source_target_pairs={{0,4},{4,0},{8,12},{12,8},{1,5},{5,1},{9,13},{13,9},{2,6},{6,2},{1... | collective-permute-start | bytes 786440 | tf_op jit(solution)/shard_map/ppermute | solution.py:623
  154.3 15.2 %collective-permute-start.12 = (bf16[4,64,512]{2,1,0:T(8,128)(2,1)}, bf16[4,64,512]{2,1,0:T(8,128)(2,1)}, u32[]{:S(2)}, u32[]{:S(2)}) collective-permute-start(bf16[4,64,512]{2,1,0:T(8,128)(2,1)} %get-tuple-element.131.term_ref), channel_id=1, source_target_pairs={{0,16},{16,0},{1,17},{17,1},{2,18},{18,2},{3,19},{19,3},{4,20},{20... | collective-permute-start | bytes 786440 | tf_op jit(solution)/shard_map/ppermute | solution.py:623
  159.1 13.0 %collective-permute-start.11 = (bf16[2,2,128,512]{3,2,1,0:T(8,128)(2,1)S(1)}, bf16[2,2,128,512]{3,2,1,0:T(8,128)(2,1)S(1)}, u32[]{:S(2)}, u32[]{:S(2)}) collective-permute-start(bf16[2,2,128,512]{3,2,1,0:T(8,128)(2,1)S(1)} %fusion.5), channel_id=1, source_target_pairs={{0,2},{1,3},{2,0},{3,1},{4,6},{5,7},{6,4},{7,5},{8,10},{9,11},{10,... | collective-permute-start | bytes 1572872 | tf_op jit(solution)/shard_map/ppermute | solution.py:623
  160.0 3.8 %collective-permute-start.14 = (f32[2,2,1088]{2,1,0:T(2,128)S(1)}, f32[2,2,1088]{2,1,0:T(2,128)S(1)}, u32[]{:S(2)}, u32[]{:S(2)}) collective-permute-start(f32[2,2,1088]{2,1,0:T(2,128)S(1)} %bitcast.204), channel_id=1, source_target_pairs={{0,4},{4,0},{8,12},{12,8},{1,5},{5,1},{9,13},{13,9},{2,6},{6,2},{1... | collective-permute-start | bytes 52232 | tf_op jit(solution)/shard_map/ppermute | solution.py:623
  163.1 10.3 %copy-start.8 = (bf16[2,2,2,64,512]{4,3,2,1,0:T(8,128)(2,1)S(1)}, bf16[2,2,2,64,512]{4,3,2,1,0:T(8,128)(2,1)}, u32[]{:S(2)}) copy-start(bf16[2,2,2,64,512]{4,3,2,1,0:T(8,128)(2,1)} %get-tuple-element.190) | copy-start | bytes 1572868
  174.6 11.3 %collective-permute-start.17 = (bf16[2,192,512]{2,1,0:T(8,128)(2,1)S(1)}, bf16[2,192,512]{2,1,0:T(8,128)(2,1)S(1)}, u32[]{:S(2)}, u32[]{:S(2)}) collective-permute-start(bf16[2,192,512]{2,1,0:T(8,128)(2,1)S(1)} %pad_maximum_fusion.2), channel_id=1, source_target_pairs={{0,8},{4,12},{8,0},{12,4},{1,9},{5,13},{9,1},{13,5},{2,10},{6,14},... | collective-permute-start | bytes 1179656 | tf_op jit(solution)/shard_map/ppermute | solution.py:623
  177.7 7.1 %collective-permute-start.15 = (bf16[2,2,2,32,512]{4,3,2,1,0:T(8,128)(2,1)S(1)}, bf16[2,2,2,32,512]{4,3,2,1,0:T(8,128)(2,1)S(1)}, u32[]{:S(2)}, u32[]{:S(2)}) collective-permute-start(bf16[2,2,2,32,512]{4,3,2,1,0:T(8,128)(2,1)S(1)} %get-tuple-element.184), channel_id=1, source_target_pairs={{0,2},{1,3},{2,0},{3,1},{4,6},{5,7},{6,4},{7,5},{8,10},{9,11},{10,... | collective-permute-start | bytes 786440 | tf_op jit(solution)/shard_map/ppermute | solution.py:623
  179.5 6.4 %collective-permute-start.16 = (bf16[2,2,2,32,512]{4,3,2,1,0:T(8,128)(2,1)S(1)}, bf16[2,2,2,32,512]{4,3,2,1,0:T(8,128)(2,1)S(1)}, u32[]{:S(2)}, u32[]{:S(2)}) collective-permute-start(bf16[2,2,2,32,512]{4,3,2,1,0:T(8,128)(2,1)S(1)} %get-tuple-element.183), channel_id=1, source_target_pairs={{0,4},{4,0},{8,12},{12,8},{1,5},{5,1},{9,13},{13,9},{2,6},{6,2},{1... | collective-permute-start | bytes 786440 | tf_op jit(solution)/shard_map/ppermute | solution.py:623
  185.9 25.7 %all-to-all-start.3 = ((bf16[4,4,64,512]{3,2,1,0:T(8,128)(2,1)}), bf16[4,4,64,512]{3,2,1,0:T(8,128)(2,1)S(1)}, u32[]{:S(2)}, u32[]{:S(2)}) async-start(bf16[4,4,64,512]{3,2,1,0:T(8,128)(2,1)} %backward_input.1), calls=%async_computation.3 | async-start | bytes 2097152 | tf_op jit(solution)/shard_map/all_to_all | solution.py:853
  190.1 20.9 %collective-permute-start.20 = (f32[2,1088]{1,0:T(2,128)S(1)}, f32[2,1088]{1,0:T(2,128)S(1)}, u32[]{:S(2)}, u32[]{:S(2)}) collective-permute-start(f32[2,1088]{1,0:T(2,128)S(1)} %bitcast.205), channel_id=1, source_target_pairs={{0,8},{4,12},{8,0},{12,4},{1,9},{5,13},{9,1},{13,5},{2,10},{6,14},... | collective-permute-start | bytes 26120 | tf_op jit(solution)/shard_map/ppermute | solution.py:623
  192.1 18.9 %collective-permute-start.18 = (bf16[2,2,32,512]{3,2,1,0:T(8,128)(2,1)S(1)}, bf16[2,2,32,512]{3,2,1,0:T(8,128)(2,1)S(1)}, u32[]{:S(2)}, u32[]{:S(2)}) collective-permute-start(bf16[2,2,32,512]{3,2,1,0:T(8,128)(2,1)S(1)} %fusion.22), channel_id=1, source_target_pairs={{0,4},{4,0},{8,12},{12,8},{1,5},{5,1},{9,13},{13,9},{2,6},{6,2},{1... | collective-permute-start | bytes 393224 | tf_op jit(solution)/shard_map/ppermute | solution.py:623
  193.7 8.8 %collective-permute-start.21 = (bf16[192,512]{1,0:T(8,128)(2,1)S(1)}, bf16[192,512]{1,0:T(8,128)(2,1)S(1)}, u32[]{:S(2)}, u32[]{:S(2)}) collective-permute-start(bf16[192,512]{1,0:T(8,128)(2,1)S(1)} %fusion.20), channel_id=1, source_target_pairs={{0,16},{16,0},{1,17},{17,1},{2,18},{18,2},{3,19},{19,3},{4,20},{20... | collective-permute-start | bytes 589832 | tf_op jit(solution)/shard_map/ppermute | solution.py:623
  194.1 17.5 %collective-permute-start.19 = (bf16[2,2,32,512]{3,2,1,0:T(8,128)(2,1)S(1)}, bf16[2,2,32,512]{3,2,1,0:T(8,128)(2,1)S(1)}, u32[]{:S(2)}, u32[]{:S(2)}) collective-permute-start(bf16[2,2,32,512]{3,2,1,0:T(8,128)(2,1)S(1)} %fusion.23), channel_id=1, source_target_pairs={{0,2},{1,3},{2,0},{3,1},{4,6},{5,7},{6,4},{7,5},{8,10},{9,11},{10,... | collective-permute-start | bytes 393224 | tf_op jit(solution)/shard_map/ppermute | solution.py:623
  211.5 8.3 %copy-start.10 = (bf16[4,4,64,512]{3,2,1,0:T(8,128)(2,1)}, bf16[4,4,64,512]{3,2,1,0:T(8,128)(2,1)S(1)}, u32[]{:S(2)}) copy-start(bf16[4,4,64,512]{3,2,1,0:T(8,128)(2,1)S(1)} %all-to-all-done.3) | copy-start | bytes 3145732
  211.7 12.1 %collective-permute-start.22 = (bf16[64,512]{1,0:T(8,128)(2,1)S(1)}, bf16[64,512]{1,0:T(8,128)(2,1)S(1)}, u32[]{:S(2)}, u32[]{:S(2)}) collective-permute-start(bf16[64,512]{1,0:T(8,128)(2,1)S(1)} %get-tuple-element.200), channel_id=1, source_target_pairs={{0,16},{4,20},{8,24},{12,28},{16,0},{20,4},{24,8},{28,12},{1,17},{... | collective-permute-start | bytes 196616 | tf_op jit(solution)/shard_map/ppermute | solution.py:820
  215.1 8.7 %collective-permute-start.23 = (bf16[64,512]{1,0:T(8,128)(2,1)S(1)}, bf16[64,512]{1,0:T(8,128)(2,1)S(1)}, u32[]{:S(2)}, u32[]{:S(2)}) collective-permute-start(bf16[64,512]{1,0:T(8,128)(2,1)S(1)} %get-tuple-element.201), channel_id=1, source_target_pairs={{0,8},{4,12},{8,0},{12,4},{16,24},{20,28},{24,16},{28,20},{1,9},{5... | collective-permute-start | bytes 196616 | tf_op jit(solution)/shard_map/ppermute | solution.py:820
  216.1 7.7 %collective-permute-start.24 = (bf16[64,512]{1,0:T(8,128)(2,1)S(1)}, bf16[64,512]{1,0:T(8,128)(2,1)S(1)}, u32[]{:S(2)}, u32[]{:S(2)}) collective-permute-start(bf16[64,512]{1,0:T(8,128)(2,1)S(1)} %get-tuple-element.199), channel_id=1, source_target_pairs={{0,24},{4,28},{8,16},{12,20},{16,8},{20,12},{24,0},{28,4},{1,25},{... | collective-permute-start | bytes 196616 | tf_op jit(solution)/shard_map/ppermute | solution.py:820
  219.2 4.6 %collective-permute-start.25 = (f32[1088]{0:T(1024)S(1)}, f32[1088]{0:T(1024)S(1)}, u32[]{:S(2)}, u32[]{:S(2)}) collective-permute-start(f32[1088]{0:T(1024)S(1)} %get-tuple-element.181), channel_id=1, source_target_pairs={{0,16},{16,0},{1,17},{17,1},{2,18},{18,2},{3,19},{19,3},{4,20},{20... | collective-permute-start | bytes 13064 | tf_op jit(solution)/shard_map/ppermute | solution.py:623
  (2 other events, 1.3 us)
